TPU v7x, 32 devices: a whole 2x2x4 slice. The times are simulated.
32 devices in a mesh: grp: 2 (over y), ctx: 4 (over z), kvh: 2 (over x), sub: 2 (over core).
Axes of the slice: x: 2, y: 2, z: 4, core: 2. Of those that a mesh axis runs over, the one named last changes fastest.
Arguments:
- queries: bfloat16 [1024, 8, 8, 128], P(('grp', 'ctx'), 'kvh', 'sub'), parts along dimension 0
- new_keys: bfloat16 [1024, 8, 128], P(('grp', 'ctx'), 'kvh'), parts along dimension 0
- new_values: bfloat16 [1024, 8, 128], P(('grp', 'ctx'), 'kvh'), parts along dimension 0, may hold values from -6 to 6
- cache_keys: bfloat16 [16384, 8, 128], P(('grp', 'ctx'), 'kvh'), parts along dimension 0, may hold values from -16 to 16
- cache_values: bfloat16 [16384, 8, 128], P(('grp', 'ctx'), 'kvh'), parts along dimension 0, may hold values from -6 to 6
- vertical_pool: int32 [16], P(('grp', 'ctx')), parts along dimension 0, may hold values from 0 to 15, as said below
- vertical_lists: int32 [8, 6], P(('grp', 'ctx')), parts along dimension 0, may hold values from 0 to 7, as said below
- slash_lists: int32 [8, 2], P(('grp', 'ctx')), parts along dimension 0, may hold values from 0 to 1, as said below
- list_counts: int32 [8, 2], P(('grp', 'ctx')), parts along dimension 0, may hold values from 1 to 6, as said below
Outputs:
- attention: bfloat16 [1024, 8, 8, 128], P(('grp', 'ctx'), 'kvh', 'sub'), parts along dimension 0
There are 2 independent parts, one for each index of `grp`. A program takes and returns all parts, laid end to end along the dimension named above; each array names one. Nothing has to cross between parts.
Inputs may be any that keep to these rules, and one draw needn't show every extreme that they name: `vertical_pool`: the 2 entries of one index of ctx are distinct. `vertical_lists`: in row b the first list_counts[b, 0] entries are distinct; later entries are never read. `slash_lists`: row b begins with 0; its first list_counts[b, 1] entries are distinct and none exceeds b or 1 plus b modulo 1; later entries are never read. `list_counts`: column 0 lies between 1 and 6, column 1 between 1 and 2, each reached in every draw.
All inputs are finite; a program needn't handle non-finite values.
Results may differ from a plain program's by a relative error of at most 0.014.
Values may be sent and summed in bfloat16 or wider, within the bound.
A program may use at most 64 MiB of HBM per device.

v0:
```python
import functools
import math

import jax
import jax.numpy as jnp
from jax import lax
from jax.experimental import pallas as pl
from jax.experimental.pallas import tpu as pltpu
from jax.sharding import PartitionSpec as P

BLK = 128
MESH = pl.DeviceIdType.MESH


def attend(n, q_hbm, nk_hbm, nv_hbm, ck_hbm, cv_hbm, vp_ref, vl_ref, sl_ref, cnt_ref, o_ref,
           q_raw, nk_raw, nv_raw, ck_raw, cv_raw, q_ref, own_ref, new_ref, sort_kv, sort_q,
           pool, slash_raw, slash, acc, peak, total, rounded, fade,
           hop_send, hop_recv, sib_send, sib_recv, sl_sem, in_sem):
    z = lax.axis_index("ctx")
    s = lax.axis_index("sub")
    heads, rows, head_dim = q_ref.shape
    groups = rows // BLK
    wide = heads * BLK
    loads = [pltpu.make_async_copy(src, dst, in_sem.at[i]) for i, (src, dst) in enumerate(
        [(ck_hbm, ck_raw), (cv_hbm, cv_raw), (nk_hbm, nk_raw), (nv_hbm, nv_raw), (q_hbm, q_raw)])]
    loads[0].start()
    c = math.log2(math.e) / math.sqrt(head_dim)
    has_left = z > 0
    has_right = z < n - 1
    sib_id = {"sub": 1 - s}

    barrier = pltpu.get_barrier_semaphore()
    pl.semaphore_signal(barrier, inc=1, device_id=sib_id, device_id_type=MESH)

    @pl.when(has_left)
    def _():
        pl.semaphore_signal(barrier, inc=1, device_id={"ctx": z - 1}, device_id_type=MESH)

    @pl.when(has_right)
    def _():
        pl.semaphore_signal(barrier, inc=1, device_id={"ctx": z + 1}, device_id_type=MESH)

    ids = lax.broadcasted_iota(jnp.int32, (wide, wide), 0)
    at = lax.broadcasted_iota(jnp.int32, (wide, wide), 1)
    sort_kv[...] = jnp.where(at == (ids % BLK) * heads + ids // BLK, 1.0, 0.0).astype(jnp.bfloat16)
    token = (ids % BLK) // groups
    sort_q[...] = jnp.where(at == (token * heads + ids // BLK) * groups + ids % groups,
                            1.0, 0.0).astype(jnp.bfloat16)

    def by_head(raw):
        return jnp.dot(sort_kv[...], raw, preferred_element_type=jnp.float32).astype(jnp.bfloat16)

    def put_keys(dst, raw):
        ordered = by_head(raw)
        for h in range(heads):
            dst[h] = ordered[h * BLK:(h + 1) * BLK]

    def put_values(dst, raw):
        ordered = lax.dot_general(raw, sort_kv[...], (((0,), (1,)), ((), ())),
                                  preferred_element_type=jnp.float32).astype(jnp.bfloat16)
        for h in range(heads):
            dst[h] = ordered[:, h * BLK:(h + 1) * BLK]

    def chosen(cache, b):
        return cache[vp_ref[b]]

    pl.semaphore_wait(barrier, 1 + has_left.astype(jnp.int32) + has_right.astype(jnp.int32))

    def hop(src_ref, src, kv, right):
        return pltpu.make_async_remote_copy(
            src_ref=src_ref, dst_ref=pool.at[src, s, kv],
            send_sem=hop_send.at[src, int(right), kv], recv_sem=hop_recv.at[src, kv],
            device_id={"ctx": z + 1 if right else z - 1}, device_id_type=MESH)

    def sib(src, kv):
        return pltpu.make_async_remote_copy(
            src_ref=pool.at[src, s, kv], dst_ref=pool.at[src, s, kv],
            send_sem=sib_send.at[src, kv], recv_sem=sib_recv.at[src, kv],
            device_id=sib_id, device_id_type=MESH)

    def sib_in(src, kv):
        return pltpu.make_async_remote_copy(
            src_ref=pool.at[src, 1 - s, kv], dst_ref=pool.at[src, 1 - s, kv],
            send_sem=sib_send.at[src, kv], recv_sem=sib_recv.at[src, kv],
            device_id=sib_id, device_id_type=MESH)

    def slash_hop(src_ref=nk_hbm):
        return pltpu.make_async_remote_copy(
            src_ref=src_ref, dst_ref=slash_raw.at[s],
            send_sem=sl_sem.at[0], recv_sem=sl_sem.at[1],
            device_id={"ctx": z + 1}, device_id_type=MESH)

    def slash_sib(part):
        return pltpu.make_async_remote_copy(
            src_ref=slash_raw.at[part], dst_ref=slash_raw.at[part],
            send_sem=sl_sem.at[2], recv_sem=sl_sem.at[3],
            device_id=sib_id, device_id_type=MESH)

    for part, src_ref in enumerate((nk_hbm, nv_hbm)):
        @pl.when(has_right & (s == part))
        def _():
            slash_hop(src_ref).start()

    def send_own(kv):
        @pl.when(has_right)
        def _():
            hop(own_ref.at[s, kv], z, kv, True).start()

        @pl.when(has_left)
        def _():
            hop(own_ref.at[s, kv], z, kv, False).start()

    loads[0].wait()
    loads[1].start()
    put_keys(own_ref.at[s, 0], chosen(ck_raw, s))
    for load in loads[2:]:
        load.start()
    send_own(0)
    loads[1].wait()
    put_values(own_ref.at[s, 1], chosen(cv_raw, s))
    send_own(1)
    loads[2].wait()
    loads[3].wait()
    put_keys(new_ref.at[0], nk_raw[...])
    put_values(new_ref.at[1], nv_raw[...])
    put_keys(own_ref.at[1 - s, 0], chosen(ck_raw, 1 - s))
    put_values(own_ref.at[1 - s, 1], chosen(cv_raw, 1 - s))
    loads[4].wait()
    for part in range(rows // BLK):
        ordered = jnp.dot(sort_q[...], q_raw[part * wide:(part + 1) * wide],
                          preferred_element_type=jnp.float32).astype(jnp.bfloat16)
        for h in range(heads):
            q_ref[h, part * BLK:(part + 1) * BLK] = ordered[h * BLK:(h + 1) * BLK]

    def listed(slot):
        count = cnt_ref[0, 0]
        width = vl_ref.shape[1]
        if width <= 8:
            hit = jnp.int32(0)
            for i in range(width):
                hit = hit | jnp.where((vl_ref[0, i] == slot) & (i < count), 1, 0)
            return hit

        def one(i, hit):
            return hit | jnp.where((vl_ref[0, i] == slot) & (i < count), 1, 0)

        return lax.fori_loop(0, width, one, jnp.int32(0))

    def score(keys, q):
        return lax.dot_general(keys, q, (((1,), (1,)), ((), ())),
                               preferred_element_type=jnp.float32)

    def take_keys(side, blocks, first=False):
        for h in range(heads):
            q = q_ref[h]
            raw = []
            tops = []
            for keys, seen in blocks:
                scores = score(keys[h], q)
                if seen is None:
                    key_id = lax.broadcasted_iota(jnp.int32, scores.shape, 0)
                    row_id = lax.broadcasted_iota(jnp.int32, scores.shape, 1) // groups
                    scores = jnp.where(key_id <= row_id, scores, -jnp.inf)
                top = jnp.max(scores, axis=0, keepdims=True)
                if seen is not None:
                    top = jnp.where(seen > 0, top, -jnp.inf)
                raw.append(scores)
                tops.append(top)
            high = functools.reduce(jnp.maximum, tops)
            if not first:
                old = peak[h]
                high = jnp.maximum(old, high)
                factor = jnp.exp2((old - high) * c)
                fade[side, h] = factor
            peak[h] = high
            sums = []
            for i, ((_, seen), scores) in enumerate(zip(blocks, raw)):
                base = high if seen is None else jnp.where(seen > 0, high, jnp.inf)
                weights = jnp.exp2((scores - base) * c)
                sums.append(jnp.sum(weights, axis=0, keepdims=True))
                rounded[side, h, i * BLK:(i + 1) * BLK] = weights.astype(jnp.bfloat16)
            add = sum(sums[1:], sums[0])
            total[h] = add if first else total[h] * fade[side, h] + add

    def take_values(side, blocks, first=False):
        depth = len(blocks) * BLK
        for h in range(heads):
            values = jnp.concatenate([values[h] for values in blocks], 1)
            add = jnp.dot(values, rounded[side, h, :depth], preferred_element_type=jnp.float32)
            acc[h] = add if first else acc[h] * fade[side, h] + add

    take_keys(0, [(new_ref.at[0], None)]
              + [(own_ref.at[b, 0], listed(2 * z + b)) for b in range(2)], first=True)
    take_values(0, [new_ref.at[1]] + [own_ref.at[b, 1] for b in range(2)], first=True)

    @pl.when(has_left)
    def _():
        slash_hop().wait_recv()
        slash_sib(s).start()

    def arrive(src, kv, right):
        hop(own_ref.at[s, kv], src, kv, right).wait_recv()

        @pl.when(has_right if right else has_left)
        def _():
            hop(pool.at[src, s, kv], src, kv, right).start()

        sib(src, kv).start()

    def step(d, carry):
        sides = ((z + d, z + d < n, False), (z - d, z - d >= 0, True))
        for kv in range(2):
            for src, there, right in sides:
                @pl.when(there)
                def _():
                    arrive(src, kv, right)

            for side, (src, there, right) in enumerate(sides):
                @pl.when(there)
                def _():
                    sib_in(src, kv).wait_recv()
                    if kv == 0:
                        take_keys(side, [(pool.at[src, b, 0], listed(2 * src + b))
                                         for b in range(2)])
                    else:
                        take_values(side, [pool.at[src, b, 1] for b in range(2)])

        @pl.when((d == 1) & has_left)
        def _():
            slash_sib(1 - s).wait_recv()
            put_keys(slash.at[0], slash_raw[0])
            put_values(slash.at[1], slash_raw[1])
            back = jnp.int32(0)
            for i in range(sl_ref.shape[1]):
                back = back | jnp.where((sl_ref[0, i] == 1) & (i < cnt_ref[0, 1]), 1, 0)
            take_keys(0, [(slash.at[0], back)])
            take_values(0, [slash.at[1]])

        return carry

    lax.fori_loop(1, n, step, 0)

    for part in range(rows // BLK):
        lanes = slice(part * BLK, (part + 1) * BLK)
        done = jnp.concatenate(
            [(acc[h, :, lanes] / total[h, :, lanes]).astype(jnp.bfloat16) for h in range(heads)], 1)
        o_ref[part * wide:(part + 1) * wide] = lax.dot_general(
            sort_q[...], done, (((0,), (1,)), ((), ())),
            preferred_element_type=jnp.float32).astype(o_ref.dtype)

    def drain(src, carry):
        for kv in range(2):
            @pl.when(has_right & (src <= z))
            def _():
                hop(own_ref.at[s, kv], src, kv, True).wait_send()

            @pl.when(has_left & (src >= z))
            def _():
                hop(own_ref.at[s, kv], src, kv, False).wait_send()

            @pl.when(src != z)
            def _():
                sib(src, kv).wait_send()
        return carry

    lax.fori_loop(0, n, drain, 0)

    @pl.when(has_right)
    def _():
        slash_hop().wait_send()

    @pl.when(has_left)
    def _():
        slash_sib(s).wait_send()


def shards(n, queries, new_keys, new_values, cache_keys, cache_values,
           vertical_pool, vertical_lists, slash_lists, list_counts):
    tokens, heads, groups, head_dim = queries.shape
    rows = tokens * groups
    picked = vertical_pool.shape[0]

    def flat(x):
        return x.reshape(-1, head_dim)

    def vmem(*shape):
        return pltpu.VMEM(shape, jnp.bfloat16)

    hbm = pl.BlockSpec(memory_space=pltpu.HBM)
    smem = pl.BlockSpec(memory_space=pltpu.SMEM)
    dma = pltpu.SemaphoreType.DMA
    wide = heads * BLK
    cached = cache_keys.shape[0] // BLK
    out = pl.pallas_call(
        functools.partial(attend, n),
        out_shape=jax.ShapeDtypeStruct((tokens * heads * groups, head_dim), jnp.bfloat16),
        in_specs=[hbm] * 5 + [smem] * 4,
        out_specs=pl.BlockSpec(memory_space=pltpu.VMEM),
        scratch_shapes=[
            vmem(heads * rows, head_dim), vmem(wide, head_dim), vmem(wide, head_dim),
            vmem(cached, wide, head_dim), vmem(cached, wide, head_dim),
            vmem(heads, rows, head_dim), vmem(picked, 2, heads, BLK, head_dim),
            vmem(2, heads, BLK, head_dim), vmem(wide, wide), vmem(wide, wide),
            vmem(n, picked, 2, heads, BLK, head_dim),
            vmem(2, wide, head_dim), vmem(2, heads, BLK, head_dim),
            pltpu.VMEM((heads, head_dim, rows), jnp.float32),
            pltpu.VMEM((heads, 1, rows), jnp.float32),
            pltpu.VMEM((heads, 1, rows), jnp.float32),
            vmem(2, heads, 3 * BLK, rows), pltpu.VMEM((2, heads, 1, rows), jnp.float32),
            dma((n, 2, 2)), dma((n, 2)), dma((n, 2)), dma((n, 2)), dma((4,)), dma((5,)),
        ],
        compiler_params=pltpu.CompilerParams(
            collective_id=0, has_side_effects=True, vmem_limit_bytes=60 * 2**20),
    )(flat(queries), flat(new_keys), flat(new_values), cache_keys.reshape(cached, wide, head_dim),
      cache_values.reshape(cached, wide, head_dim),
      vertical_pool, vertical_lists, slash_lists, list_counts)
    return out.reshape(tokens, heads, groups, head_dim)


def solution(mesh):
    in_specs = (
        P(("grp", "ctx"), "kvh", "sub", None),
        P(("grp", "ctx"), "kvh", None),
        P(("grp", "ctx"), "kvh", None),
        P(("grp", "ctx"), "kvh", None),
        P(("grp", "ctx"), "kvh", None),
        P(("grp", "ctx")),
        P(("grp", "ctx"), None),
        P(("grp", "ctx"), None),
        P(("grp", "ctx"), None),
    )
    out_specs = P(("grp", "ctx"), "kvh", "sub", None)
    return jax.shard_map(functools.partial(shards, mesh.shape["ctx"]), mesh=mesh,
                         in_specs=in_specs, out_specs=out_specs, check_vma=False)
```

profile of v0, /device:TPU:0, one launch (start us, length us, event | category | flops | bytes accessed | tf_op | source)
XLA Modules:
  0.0 29.6 jit_solution(3327487444657057850)
XLA Ops:
  0.0 27.5 %shard_map.91 = bf16[2048,128]{1,0:T(8,128)(2,1)} custom-call(bf16[2048,128]{1,0:T(8,128)(2,1)} %bitcast.9, bf16[512,128]{1,0:T(8,128)(2,1)} %bitcast.10, bf16[512,128]{1,0:T(8,128)(2,1)} %bitcast.11, bf16[16,512,128]{2,1,0:T(8,128)(2,1)} %bitcast.6, bf16[16,512,128]{2,1,0:T(8,128)(2,1)} %bitcast.7, s32[2]{0:T(128)} %vp_ref.1, s32[1,6]{1,0:T(1,128)} %vl_ref.1, ...), custom_call_target="tpu_custom_call" | custom-call | tf_op jit(solution)/shard_map/pallas_call | solution.py:294
  27.5 2.0 %copy.11 = bf16[128,4,4,128]{3,2,1,0:T(4,128)(2,1)} copy(bf16[128,4,4,128]{3,2,1,0:T(4,128)(2,1)} %bitcast.8) | data formatting | bytes 1048576
where the time goes:
time: 30 us; the launch traced here: 29.6 us
  Pallas kernels  27.5 us (92%)
  local copies, waits for them, and re-layouts  2.02 us (7%)
    pallas_call x1, Pallas kernels, shards(): pl.pallas_call(functools.partial(attend, n), out_shape=jax.ShapeDtypeStru...  27.5 us
    unnamed x1, local copies, waits for them, and re-layouts  2.02 us

commit v1 on v0

--- a/solution.py
+++ b/solution.py
@@ -274,6 +274,499 @@
         slash_sib(s).wait_send()
 
 
+def plan():
+    def kv(src, h):
+        return (1, src * 4 + h)
+
+    def step(recv=(0, 0), unit=None, wait=True, half=None, result=0, extra=0):
+        code, block = 0, 0
+        if unit is not None:
+            slot, src, h = unit
+            code, block = slot + 1 + (0 if wait else 8), src * 4 + h
+        return (recv[0], recv[1], code, block, 0 if half is None else half + 1, result, extra)
+
+    def own(z, count=4):
+        return [step(unit=(h, z, h), wait=False) for h in range(count)]
+
+    def lagged(messages, steps):
+        late = None
+        for recv, extra in messages:
+            steps.append(step(recv, None if late is None else (late % 4, late // 4, late % 4), extra=extra))
+            late = recv[1] if recv[0] == 1 else None
+        if late is not None:
+            steps.append(step(unit=(late % 4, late // 4, late % 4)))
+        return steps
+
+    slash = (3, 0)
+    roles = [lagged([(kv(src, h), 0) for src in (1, 2, 3) for h in range(4)], own(0))]
+    one = lagged([(kv(0, 0), 0), (kv(2, 0), 0), (kv(0, 2), 0), (kv(2, 1), 0), (kv(0, 1), 1), (kv(2, 2), 0),
+                  (kv(0, 3), 2), (kv(2, 3), 0), (kv(3, 0), 0), (slash, 0), (kv(3, 1), 0), (kv(3, 2), 0),
+                  (kv(3, 3), 0)], own(1))
+    for h in range(4):
+        at = len(one) - 4 + h
+        one[at] = one[at][:4] + (h + 1,) + one[at][5:]
+    roles.append(one)
+    roles.append(own(2, 2) + [
+        step(kv(1, 0), (2, 2, 2), wait=False), step(kv(3, 0), (3, 2, 3), wait=False),
+        step(kv(1, 2), (0, 1, 0)), step(kv(1, 1), (0, 3, 0)), step((2, 0), (2, 1, 2)),
+        step(kv(0, 0), (4, 2, 2), wait=False, half=4), step(kv(3, 1), (1, 1, 1)),
+        step(kv(0, 2), (4, 1, 2), wait=False), step(unit=(0, 0, 0)),
+        step(unit=(4, 0, 2), result=1), step(kv(0, 1), (1, 3, 1)), step((2, 1), (2, 0, 2), wait=False),
+        step(kv(1, 3), (5, 2, 3), wait=False, half=5), step(kv(3, 2), (1, 0, 1)),
+        step(kv(0, 3), (5, 1, 3)), step(kv(3, 3), (3, 1, 3), wait=False),
+        step(unit=(5, 0, 3), result=2), step(unit=(2, 3, 2)), step(slash, (3, 0, 3), wait=False),
+        step(unit=(3, 3, 3), half=0), step(half=1), step(half=2), step(half=3)])
+    roles.append(own(3) + [
+        step(kv(2, 0)), step(slash, (0, 2, 0)), step(kv(2, 1), half=0), step(unit=(1, 2, 1), half=1),
+        step(kv(1, 0)), step(kv(1, 1), (0, 1, 0)), step(kv(0, 0), (1, 1, 1)), step((4, 0), (0, 0, 0)),
+        step(kv(0, 1)), step(unit=(1, 0, 1)), step((4, 1))])
+    return roles
+
+
+def chain(n, q_hbm, nk_hbm, nv_hbm, ck_hbm, cv_hbm, vp_ref, vl_ref, sl_ref, cnt_ref, o_ref,
+          q_raw, nk_raw, nv_raw, ck_raw, cv_raw, q_ref, slab, sort_kv, sort_q,
+          pool, acc, peak, total, mask, part_acc, part_stat,
+          hop_send, hop_recv, sib_send, sib_recv, sl_sem, q_sem, part_sem, in_sem):
+    z = lax.axis_index("ctx")
+    s = lax.axis_index("sub")
+    heads = pool.shape[1]
+    rows, head_dim = q_ref.shape[1:]
+    groups = rows // BLK
+    wide = heads * BLK
+    last = n - 1
+    guests = heads // 2
+    loads = [pltpu.make_async_copy(src, dst, in_sem.at[i]) for i, (src, dst) in enumerate(
+        [(ck_hbm, ck_raw), (cv_hbm, cv_raw), (nk_hbm, nk_raw), (nv_hbm, nv_raw), (q_hbm, q_raw)])]
+    for load in loads:
+        load.start()
+    c = math.log2(math.e) / math.sqrt(head_dim)
+    has_left = z > 0
+    has_right = z < last
+    sib_id = {"sub": 1 - s}
+
+    barrier = pltpu.get_barrier_semaphore()
+    pl.semaphore_signal(barrier, inc=1, device_id=sib_id, device_id_type=MESH)
+
+    @pl.when(has_left)
+    def _():
+        pl.semaphore_signal(barrier, inc=1, device_id={"ctx": z - 1}, device_id_type=MESH)
+
+    @pl.when(has_right)
+    def _():
+        pl.semaphore_signal(barrier, inc=1, device_id={"ctx": z + 1}, device_id_type=MESH)
+
+    ids = lax.broadcasted_iota(jnp.int32, (wide, wide), 0)
+    at = lax.broadcasted_iota(jnp.int32, (wide, wide), 1)
+    sort_kv[...] = jnp.where(at == (ids % BLK) * heads + ids // BLK, 1.0, 0.0).astype(jnp.bfloat16)
+    token = (ids % BLK) // groups
+    sort_q[...] = jnp.where(at == (token * heads + ids // BLK) * groups + ids % groups,
+                            1.0, 0.0).astype(jnp.bfloat16)
+
+    def unseen(hit):
+        return jnp.full((1, BLK), jnp.where(hit > 0, 0.0, jnp.inf), jnp.float32)
+
+    for slot in range(2 * n):
+        hit = jnp.int32(0)
+        for i in range(vl_ref.shape[1]):
+            hit = hit | jnp.where((vl_ref[0, i] == slot) & (i < cnt_ref[0, 0]), 1, 0)
+        mask[0, slot:slot + 1] = unseen(hit)
+    hit = jnp.int32(0)
+    for i in range(sl_ref.shape[1]):
+        hit = hit | jnp.where((sl_ref[0, i] == 1) & (i < cnt_ref[0, 1]), 1, 0)
+    mask[0, 2 * n:2 * n + 1] = unseen(hit)
+
+    def put_keys(raw, put):
+        ordered = jnp.dot(sort_kv[...], raw, preferred_element_type=jnp.float32).astype(jnp.bfloat16)
+        for h in range(heads):
+            put(h, ordered[h * BLK:(h + 1) * BLK])
+
+    def put_values(raw, put):
+        ordered = lax.dot_general(raw, sort_kv[...], (((0,), (1,)), ((), ())),
+                                  preferred_element_type=jnp.float32).astype(jnp.bfloat16)
+        for h in range(heads):
+            put(h, ordered[:, h * BLK:(h + 1) * BLK])
+
+    def put_pool(b, kv):
+        def put(h, block):
+            pool[z, h, b, kv] = block
+        return put
+
+    def put_slab(kv):
+        def put(h, block):
+            slab[0, kv, h] = block
+        return put
+
+    def hop(src, h, right):
+        return pltpu.make_async_remote_copy(
+            src_ref=pool.at[src, h, s], dst_ref=pool.at[src, h, s],
+            send_sem=hop_send.at[src, h, int(right)], recv_sem=hop_recv.at[src, h],
+            device_id={"ctx": z + 1 if right else z - 1}, device_id_type=MESH)
+
+    def sib(src, h, part=s):
+        return pltpu.make_async_remote_copy(
+            src_ref=pool.at[src, h, part], dst_ref=pool.at[src, h, part],
+            send_sem=sib_send.at[src, h], recv_sem=sib_recv.at[src, h],
+            device_id=sib_id, device_id_type=MESH)
+
+    def slash_hop(count):
+        return pltpu.make_async_remote_copy(
+            src_ref=slab.at[0, s, pl.ds(0, count)], dst_ref=slab.at[1, s, pl.ds(0, count)],
+            send_sem=sl_sem.at[0], recv_sem=sl_sem.at[1],
+            device_id={"ctx": z + 1}, device_id_type=MESH)
+
+    def slash_sib(count, part):
+        return pltpu.make_async_remote_copy(
+            src_ref=slab.at[1, part, pl.ds(0, count)], dst_ref=slab.at[1, part, pl.ds(0, count)],
+            send_sem=sl_sem.at[2], recv_sem=sl_sem.at[3],
+            device_id=sib_id, device_id_type=MESH)
+
+    def guest_q(g):
+        return pltpu.make_async_remote_copy(
+            src_ref=q_ref.at[heads - guests + g], dst_ref=q_ref.at[heads + g],
+            send_sem=q_sem.at[0, g], recv_sem=q_sem.at[1, g],
+            device_id={"ctx": z - 1}, device_id_type=MESH)
+
+    def guest_mask():
+        return pltpu.make_async_remote_copy(
+            src_ref=mask.at[0], dst_ref=mask.at[1],
+            send_sem=q_sem.at[0, guests], recv_sem=q_sem.at[1, guests],
+            device_id={"ctx": z - 1}, device_id_type=MESH)
+
+    def guest_part(g):
+        return [pltpu.make_async_remote_copy(
+            src_ref=ref.at[g], dst_ref=ref.at[g],
+            send_sem=part_sem.at[0, g, i], recv_sem=part_sem.at[1, g, i],
+            device_id={"ctx": z + 1}, device_id_type=MESH)
+            for i, ref in enumerate((part_acc, part_stat))]
+
+    loads[0].wait()
+    put_keys(ck_raw[vp_ref[s]], put_pool(s, 0))
+    loads[1].wait()
+    put_values(cv_raw[vp_ref[s]], put_pool(s, 1))
+    pl.semaphore_wait(barrier, 1 + has_left.astype(jnp.int32) + has_right.astype(jnp.int32))
+
+    @pl.when(z == 0)
+    def _():
+        for h in (0, 2, 1, 3):
+            hop(z, h, True).start()
+
+    @pl.when(z == 1)
+    def _():
+        for h in (0, 2, 1):
+            hop(z, h, True).start()
+
+    @pl.when(z == 2)
+    def _():
+        hop(z, 0, True).start()
+
+    @pl.when((z == 1) | (z == 2))
+    def _():
+        for h in range(heads):
+            hop(z, h, False).start()
+
+    @pl.when(z == last)
+    def _():
+        hop(z, 0, False).start()
+        guest_mask().start()
+
+    loads[2].wait()
+    loads[3].wait()
+    put_keys(nk_raw[...], put_slab(0))
+    put_values(nv_raw[...], put_slab(1))
+
+    @pl.when(z == 0)
+    def _():
+        slash_hop(heads).start()
+
+    @pl.when(z == 2)
+    def _():
+        slash_hop(heads - guests).start()
+        hop(z, 1, True).start()
+
+    loads[4].wait()
+    for part in range(rows // BLK):
+        ordered = jnp.dot(sort_q[...], q_raw[part * wide:(part + 1) * wide],
+                          preferred_element_type=jnp.float32).astype(jnp.bfloat16)
+        for h in range(heads):
+            q_ref[h, part * BLK:(part + 1) * BLK] = ordered[h * BLK:(h + 1) * BLK]
+
+    @pl.when(z == last)
+    def _():
+        guest_q(0).start()
+        hop(z, 1, False).start()
+        guest_q(1).start()
+        hop(z, 2, False).start()
+        hop(z, 3, False).start()
+
+    put_keys(ck_raw[vp_ref[1 - s]], put_pool(1 - s, 0))
+    put_values(cv_raw[vp_ref[1 - s]], put_pool(1 - s, 1))
+
+    @pl.when(z == last - 1)
+    def _():
+        for g in range(guests):
+            acc[heads + g] = jnp.zeros_like(acc[heads + g])
+            total[heads + g] = jnp.zeros_like(total[heads + g])
+            peak[heads + g] = jnp.full_like(peak[heads + g], -1e30)
+
+    def score(keys, q):
+        return lax.dot_general(keys, q, (((1,), (1,)), ((), ())),
+                               preferred_element_type=jnp.float32)
+
+    def diagonal(h, carry):
+        scores = score(slab[0, 0, h], q_ref[h])
+        key_id = lax.broadcasted_iota(jnp.int32, scores.shape, 0)
+        row_id = lax.broadcasted_iota(jnp.int32, scores.shape, 1) // groups
+        scores = jnp.where(key_id <= row_id, scores, -jnp.inf)
+        high = jnp.max(scores, axis=0, keepdims=True)
+        weights = jnp.exp2((scores - high) * c)
+        peak[h] = high
+        total[h] = jnp.sum(weights, axis=0, keepdims=True)
+        acc[h] = jnp.dot(slab[0, 1, h], weights.astype(jnp.bfloat16), preferred_element_type=jnp.float32)
+        return carry
+
+    lax.fori_loop(0, heads, diagonal, 0)
+
+    def spread(row):
+        return jnp.concatenate([row] * groups, 1)
+
+    def update(slot, blocks):
+        q = q_ref[slot]
+        old = peak[slot]
+        raw = [score(keys, q) for keys, _, _ in blocks]
+        hide = [spread(row) for _, _, row in blocks]
+        high = old
+        for scores, row in zip(raw, hide):
+            high = jnp.maximum(high, jnp.max(scores, axis=0, keepdims=True) - row)
+        factor = jnp.exp2((old - high) * c)
+        peak[slot] = high
+        weights = [jnp.exp2((scores - (high + row)) * c) for scores, row in zip(raw, hide)]
+        add = functools.reduce(jnp.add, [jnp.sum(w, axis=0, keepdims=True) for w in weights])
+        total[slot] = total[slot] * factor + add
+        rounded = jnp.concatenate([w.astype(jnp.bfloat16) for w in weights], 0)
+        values = jnp.concatenate([values for _, values, _ in blocks], 1)
+        acc[slot] = acc[slot] * factor + jnp.dot(values, rounded, preferred_element_type=jnp.float32)
+
+    roles = plan()
+    steps = max(len(role) for role in roles)
+
+    def by_role(values):
+        out = jnp.int32(values[-1])
+        for i in reversed(range(len(values) - 1)):
+            out = jnp.where(z == i, jnp.int32(values[i]), out)
+        return out
+
+    words = []
+    for field in range(7):
+        chunks = []
+        for start in range(0, steps, 7):
+            chunks.append(by_role([sum(step[field] << (4 * i) for i, step in enumerate(role[start:start + 7]))
+                                   for role in roles]))
+        words.append(chunks)
+
+    def step(t, carry):
+        group = t // 7
+        shift = 4 * (t % 7)
+
+        def look(field):
+            word = words[field][-1]
+            for i in reversed(range(len(words[field]) - 1)):
+                word = jnp.where(group == i, words[field][i], word)
+            return lax.shift_right_logical(word, shift) & 15
+
+        kind, message, unit, block, half, result, extra = [look(field) for field in range(7)]
+        src, h = message // 4, message % 4
+
+        @pl.when(kind == 1)
+        def _():
+            hop(src, h, True).wait_recv()
+
+            @pl.when((src < z) & ((z == 1) | ((z == 2) & (h < heads - guests))))
+            def _():
+                hop(src, h, True).start()
+
+            @pl.when((src > z) & has_left)
+            def _():
+                hop(src, h, False).start()
+
+            sib(src, h).start()
+
+            @pl.when(extra == 1)
+            def _():
+                hop(z, 3, True).start()
+
+            @pl.when(extra == 2)
+            def _():
+                slash_hop(heads).start()
+
+        @pl.when(kind == 2)
+        def _():
+            @pl.when(h == 0)
+            def _():
+                guest_mask().wait_recv()
+
+            guest_q(h).wait_recv()
+
+        @pl.when((kind == 3) & has_right)
+        def _():
+            slash_hop(heads).wait_recv()
+            slash_sib(heads, s).start()
+
+        @pl.when((kind == 3) & (z == last))
+        def _():
+            slash_hop(heads - guests).wait_recv()
+            slash_sib(heads - guests, s).start()
+
+        @pl.when(kind == 4)
+        def _():
+            for copy in guest_part(h):
+                copy.wait_recv()
+            slot = heads - guests + h
+            old, new = peak[slot], part_stat[h, 0:1]
+            high = jnp.maximum(old, new)
+            mine, theirs = jnp.exp2((old - high) * c), jnp.exp2((new - high) * c)
+            acc[slot] = acc[slot] * mine + part_acc[h].astype(jnp.float32) * theirs
+            total[slot] = total[slot] * mine + part_stat[h, 1:2] * theirs
+
+        @pl.when(unit > 0)
+        def _():
+            slot = (unit - 1) % 8
+            src, h = block // 4, block % 4
+
+            @pl.when(unit < 8)
+            def _():
+                sib(src, h, 1 - s).wait_recv()
+
+            guest = slot // heads
+            update(slot, [(pool[src, h, b, 0], pool[src, h, b, 1], mask[guest, pl.ds(2 * src + b, 1)])
+                          for b in range(2)])
+
+        @pl.when(half > 0)
+        def _():
+            slot = half - 1
+            guest = slot // heads
+
+            @pl.when((slot == 0) & has_right)
+            def _():
+                slash_sib(heads, 1 - s).wait_recv()
+
+            @pl.when((slot == 0) & (z == last))
+            def _():
+                slash_sib(heads - guests, 1 - s).wait_recv()
+
+            h = slot - guest * guests
+            update(slot, [(slab[1 - guest, 0, h], slab[1 - guest, 1, h], mask[guest, 2 * n:2 * n + 1])])
+
+        @pl.when(result > 0)
+        def _():
+            g = result - 1
+            part_acc[g] = acc[heads + g].astype(jnp.bfloat16)
+            part_stat[g, 0:1] = peak[heads + g]
+            part_stat[g, 1:2] = total[heads + g]
+            for copy in guest_part(g):
+                copy.start()
+
+        return carry
+
+    lax.fori_loop(0, by_role([len(role) for role in roles]), step, 0)
+
+    for part in range(rows // BLK):
+        lanes = slice(part * BLK, (part + 1) * BLK)
+        done = jnp.concatenate(
+            [(acc[h, :, lanes] / total[h, :, lanes]).astype(jnp.bfloat16) for h in range(heads)], 1)
+        o_ref[part * wide:(part + 1) * wide] = lax.dot_general(
+            sort_q[...], done, (((0,), (1,)), ((), ())),
+            preferred_element_type=jnp.float32).astype(o_ref.dtype)
+
+    def drain(i, carry):
+        src, h = i // heads, i % heads
+
+        @pl.when((src <= z) & (z < last) & ((z < last - 1) | (h < heads - guests)))
+        def _():
+            hop(src, h, True).wait_send()
+
+        @pl.when((src >= z) & has_left)
+        def _():
+            hop(src, h, False).wait_send()
+
+        @pl.when((src != z) & ((z < last) | (h < heads - guests)))
+        def _():
+            sib(src, h).wait_send()
+        return carry
+
+    lax.fori_loop(0, n * heads, drain, 0)
+
+    @pl.when(z < last - 1)
+    def _():
+        slash_hop(heads).wait_send()
+
+    @pl.when(z == last - 1)
+    def _():
+        slash_hop(heads - guests).wait_send()
+        for g in range(guests):
+            for copy in guest_part(g):
+                copy.wait_send()
+
+    @pl.when(has_left & has_right)
+    def _():
+        slash_sib(heads, s).wait_send()
+
+    @pl.when(z == last)
+    def _():
+        slash_sib(heads - guests, s).wait_send()
+        guest_mask().wait_send()
+        for g in range(guests):
+            guest_q(g).wait_send()
+
+
+def store(o_vmem, o_hbm, sem):
+    copy = pltpu.make_async_copy(o_vmem, o_hbm, sem)
+    copy.start()
+    copy.wait()
+
+
+def chain_call(n, q, nk, nv, ck, cv, tables, heads, rows, head_dim):
+    def vmem(*shape):
+        return pltpu.VMEM(shape, jnp.bfloat16)
+
+    hbm = pl.BlockSpec(memory_space=pltpu.HBM)
+    smem = pl.BlockSpec(memory_space=pltpu.SMEM)
+    in_vmem = pl.BlockSpec(memory_space=pltpu.VMEM)
+    dma = pltpu.SemaphoreType.DMA
+    cached, wide = ck.shape[:2]
+    guests = heads // 2
+    f32 = jnp.float32
+    out = pl.pallas_call(
+        functools.partial(chain, n),
+        out_shape=pltpu.VMEM((heads * rows, head_dim), jnp.bfloat16),
+        in_specs=[hbm] * 5 + [smem] * 4,
+        out_specs=in_vmem,
+        scratch_shapes=[
+            vmem(heads * rows, head_dim), vmem(wide, head_dim), vmem(wide, head_dim),
+            vmem(cached, wide, head_dim), vmem(cached, wide, head_dim),
+            vmem(heads + guests, rows, head_dim), vmem(2, 2, heads, BLK, head_dim),
+            vmem(wide, wide), vmem(wide, wide),
+            vmem(n, heads, 2, 2, BLK, head_dim),
+            pltpu.VMEM((heads + guests, head_dim, rows), f32),
+            pltpu.VMEM((heads + guests, 1, rows), f32),
+            pltpu.VMEM((heads + guests, 1, rows), f32),
+            pltpu.VMEM((2, 16, BLK), f32),
+            vmem(guests, head_dim, rows), pltpu.VMEM((guests, 8, rows), f32),
+            dma((n, heads, 2)), dma((n, heads)), dma((n, heads)), dma((n, heads)), dma((4,)),
+            dma((2, guests + 1)), dma((2, guests, 2)), dma((5,)),
+        ],
+        compiler_params=pltpu.CompilerParams(
+            collective_id=0, has_side_effects=True, vmem_limit_bytes=40 * 2**20),
+    )(q, nk, nv, ck, cv, *tables)
+    return pl.pallas_call(
+        store,
+        out_shape=jax.ShapeDtypeStruct(out.shape, out.dtype),
+        in_specs=[in_vmem],
+        out_specs=hbm,
+        scratch_shapes=[dma],
+        compiler_params=pltpu.CompilerParams(vmem_limit_bytes=2**20),
+    )(out)
+
+
 def shards(n, queries, new_keys, new_values, cache_keys, cache_values,
            vertical_pool, vertical_lists, slash_lists, list_counts):
     tokens, heads, groups, head_dim = queries.shape
@@ -291,6 +784,11 @@
     dma = pltpu.SemaphoreType.DMA
     wide = heads * BLK
     cached = cache_keys.shape[0] // BLK
+    if n == 4 and heads == 4 and picked == 2:
+        out = chain_call(n, flat(queries), flat(new_keys), flat(new_values),
+                         cache_keys.reshape(cached, wide, head_dim), cache_values.reshape(cached, wide, head_dim),
+                         (vertical_pool, vertical_lists, slash_lists, list_counts), heads, rows, head_dim)
+        return out.reshape(tokens, heads, groups, head_dim)
     out = pl.pallas_call(
         functools.partial(attend, n),
         out_shape=jax.ShapeDtypeStruct((tokens * heads * groups, head_dim), jnp.bfloat16),

time: 30 us -> 41.2 us (1.37)
  local copies, waits for them, and re-layouts: 2.02 us -> 8.65 us
  Pallas kernels: 27.5 us -> 32 us
    unnamed x1 -> x18, local copies, waits for them, and re-layouts: 2.02 us -> 8.65 us
    pallas_call x1 -> x2, Pallas kernels: 27.5 us -> 32 us  [the longest x1 31.2 us: chain_call(): pl.pallas_call(functools.partial(chain, n), out_shape=pltpu.VMEM((heads *...]
where the time goes in v1:
time: 41.2 us; the launch traced here: 40.7 us
  Pallas kernels  32 us (78%)
  local copies, waits for them, and re-layouts  8.65 us (21%)
    pallas_call x1, Pallas kernels, chain_call(): pl.pallas_call(functools.partial(chain, n), out_shape=pltpu.VMEM((heads *...  31.2 us
    unnamed x18, local copies, waits for them, and re-layouts  8.65 us

profile of v1, /device:TPU:0, one launch (start us, length us, event | category | flops | bytes accessed | tf_op | source)
XLA Modules:
  0.0 40.7 jit_solution(4882253693354649725)
XLA Ops:
  0.0 0.0 copy-start
  0.0 1.6 %copy-done = bf16[2048,4,128]{2,1,0:T(4,128)(2,1)S(1)} copy-done((bf16[2048,4,128]{2,1,0:T(4,128)(2,1)S(1)}, bf16[2048,4,128]{2,1,0:T(4,128)(2,1)}, u32[]{:S(2)}) %copy-start) | copy-done | bytes 2097176
  1.6 0.0 copy-start.1
  1.6 1.6 %copy-done.1 = bf16[2048,4,128]{2,1,0:T(4,128)(2,1)S(1)} copy-done((bf16[2048,4,128]{2,1,0:T(4,128)(2,1)S(1)}, bf16[2048,4,128]{2,1,0:T(4,128)(2,1)}, u32[]{:S(2)}) %copy-start.1) | copy-done | bytes 2097176
  3.2 0.0 copy-start.2
  3.2 1.0 %copy-done.2 = bf16[128,4,4,128]{3,2,1,0:T(4,128)(2,1)S(1)} copy-done((bf16[128,4,4,128]{3,2,1,0:T(4,128)(2,1)S(1)}, bf16[128,4,4,128]{3,2,1,0:T(4,128)(2,1)}, u32[]{:S(2)}) %copy-start.2) | copy-done | bytes 524312
  4.2 0.0 copy-start.3
  4.2 0.9 %copy-done.3 = bf16[128,4,128]{2,1,0:T(4,128)(2,1)S(1)} copy-done((bf16[128,4,128]{2,1,0:T(4,128)(2,1)S(1)}, bf16[128,4,128]{2,1,0:T(4,128)(2,1)}, u32[]{:S(2)}) %copy-start.3) | copy-done | bytes 131096
  5.1 0.0 copy-start.4
  5.1 0.9 %copy-done.4 = bf16[128,4,128]{2,1,0:T(4,128)(2,1)S(1)} copy-done((bf16[128,4,128]{2,1,0:T(4,128)(2,1)S(1)}, bf16[128,4,128]{2,1,0:T(4,128)(2,1)}, u32[]{:S(2)}) %copy-start.4) | copy-done | bytes 131096
  6.0 0.0 copy-start.5
  6.0 0.7 %copy-done.5 = s32[2]{0:T(128)S(1)} copy-done((s32[2]{0:T(128)S(1)}, s32[2]{0:T(128)}, u32[]{:S(2)}) %copy-start.5) | copy-done | bytes 32
  6.7 0.0 copy-start.6
  6.7 0.7 %copy-done.6 = s32[1,6]{1,0:T(1,128)S(1)} copy-done((s32[1,6]{1,0:T(1,128)S(1)}, s32[1,6]{1,0:T(1,128)}, u32[]{:S(2)}) %copy-start.6) | copy-done | bytes 48
  7.3 0.0 copy-start.7
  7.3 0.7 %copy-done.7 = s32[1,2]{1,0:T(1,128)S(1)} copy-done((s32[1,2]{1,0:T(1,128)S(1)}, s32[1,2]{1,0:T(1,128)}, u32[]{:S(2)}) %copy-start.7) | copy-done | bytes 32
  8.0 0.0 copy-start.8
  8.0 0.7 %copy-done.8 = s32[1,2]{1,0:T(1,128)S(1)} copy-done((s32[1,2]{1,0:T(1,128)S(1)}, s32[1,2]{1,0:T(1,128)}, u32[]{:S(2)}) %copy-start.8) | copy-done | bytes 32
  8.7 31.2 %shard_map.91.o_vmem = bf16[2048,128]{1,0:T(8,128)(2,1)S(1)} custom-call(bf16[2048,128]{1,0:T(8,128)(2,1)S(1)} %bitcast.8, bf16[512,128]{1,0:T(8,128)(2,1)S(1)} %bitcast.9, bf16[512,128]{1,0:T(8,128)(2,1)S(1)} %bitcast.10, bf16[16,512,128]{2,1,0:T(8,128)(2,1)S(1)} %bitcast.6, bf16[16,512,128]{2,1,0:T(8,128)(2,1)S(1)} %bitcast.7, s32[2]{0:T(128)S(1)} %copy-done.5, ...), custom_call_target="tpu_custom_call" | custom-call | tf_op jit(solution)/shard_map/pallas_call | solution.py:738
  39.9 0.8 %shard_map.92 = bf16[2048,128]{1,0:T(8,128)(2,1)} custom-call(bf16[2048,128]{1,0:T(8,128)(2,1)S(1)} %shard_map.91.o_vmem), custom_call_target="tpu_custom_call" | custom-call | tf_op jit(solution)/shard_map/pallas_call | solution.py:760
Async XLA Ops:
  0.0 1.6 %copy-start = (bf16[2048,4,128]{2,1,0:T(4,128)(2,1)S(1)}, bf16[2048,4,128]{2,1,0:T(4,128)(2,1)}, u32[]{:S(2)}) copy-start(bf16[2048,4,128]{2,1,0:T(4,128)(2,1)} %param.12) | copy-start | bytes 6291460
  1.6 1.6 %copy-start.1 = (bf16[2048,4,128]{2,1,0:T(4,128)(2,1)S(1)}, bf16[2048,4,128]{2,1,0:T(4,128)(2,1)}, u32[]{:S(2)}) copy-start(bf16[2048,4,128]{2,1,0:T(4,128)(2,1)} %param.13) | copy-start | bytes 6291460
  3.2 1.0 %copy-start.2 = (bf16[128,4,4,128]{3,2,1,0:T(4,128)(2,1)S(1)}, bf16[128,4,4,128]{3,2,1,0:T(4,128)(2,1)}, u32[]{:S(2)}) copy-start(bf16[128,4,4,128]{3,2,1,0:T(4,128)(2,1)} %param.9) | copy-start | bytes 1572868
  4.2 0.9 %copy-start.3 = (bf16[128,4,128]{2,1,0:T(4,128)(2,1)S(1)}, bf16[128,4,128]{2,1,0:T(4,128)(2,1)}, u32[]{:S(2)}) copy-start(bf16[128,4,128]{2,1,0:T(4,128)(2,1)} %param.10) | copy-start | bytes 393220
  5.1 0.9 %copy-start.4 = (bf16[128,4,128]{2,1,0:T(4,128)(2,1)S(1)}, bf16[128,4,128]{2,1,0:T(4,128)(2,1)}, u32[]{:S(2)}) copy-start(bf16[128,4,128]{2,1,0:T(4,128)(2,1)} %param.11) | copy-start | bytes 393220
  6.0 0.7 %copy-start.5 = (s32[2]{0:T(128)S(1)}, s32[2]{0:T(128)}, u32[]{:S(2)}) copy-start(s32[2]{0:T(128)} %vp_ref.1) | copy-start | bytes 28
  6.7 0.7 %copy-start.6 = (s32[1,6]{1,0:T(1,128)S(1)}, s32[1,6]{1,0:T(1,128)}, u32[]{:S(2)}) copy-start(s32[1,6]{1,0:T(1,128)} %vl_ref.1) | copy-start | bytes 76
  7.3 0.7 %copy-start.7 = (s32[1,2]{1,0:T(1,128)S(1)}, s32[1,2]{1,0:T(1,128)}, u32[]{:S(2)}) copy-start(s32[1,2]{1,0:T(1,128)} %sl_ref.1) | copy-start | bytes 28
  8.0 0.7 %copy-start.8 = (s32[1,2]{1,0:T(1,128)S(1)}, s32[1,2]{1,0:T(1,128)}, u32[]{:S(2)}) copy-start(s32[1,2]{1,0:T(1,128)} %cnt_ref.1) | copy-start | bytes 28

commit v2 on v1

--- a/solution.py
+++ b/solution.py
@@ -273,68 +273,82 @@
     def _():
         slash_sib(s).wait_send()
 
-
-def plan():
+BITS = 5
+PACK = 6
+OWN, GUEST, ALONE = 4, 5, 6
+IDLE = (6, 4 * GUEST)
+GUESTS = 1
+
+
+def plan(heads):
     def kv(src, h):
         return (1, src * 4 + h)
 
-    def step(recv=(0, 0), unit=None, wait=True, half=None, result=0, extra=0):
-        code, block = 0, 0
-        if unit is not None:
-            slot, src, h = unit
-            code, block = slot + 1 + (0 if wait else 8), src * 4 + h
-        return (recv[0], recv[1], code, block, 0 if half is None else half + 1, result, extra)
-
-    def own(z, count=4):
-        return [step(unit=(h, z, h), wait=False) for h in range(count)]
-
-    def lagged(messages, steps):
-        late = None
-        for recv, extra in messages:
-            steps.append(step(recv, None if late is None else (late % 4, late // 4, late % 4), extra=extra))
-            late = recv[1] if recv[0] == 1 else None
-        if late is not None:
-            steps.append(step(unit=(late % 4, late // 4, late % 4)))
-        return steps
-
-    slash = (3, 0)
-    roles = [lagged([(kv(src, h), 0) for src in (1, 2, 3) for h in range(4)], own(0))]
-    one = lagged([(kv(0, 0), 0), (kv(2, 0), 0), (kv(0, 2), 0), (kv(2, 1), 0), (kv(0, 1), 1), (kv(2, 2), 0),
-                  (kv(0, 3), 2), (kv(2, 3), 0), (kv(3, 0), 0), (slash, 0), (kv(3, 1), 0), (kv(3, 2), 0),
-                  (kv(3, 3), 0)], own(1))
-    for h in range(4):
-        at = len(one) - 4 + h
-        one[at] = one[at][:4] + (h + 1,) + one[at][5:]
-    roles.append(one)
-    roles.append(own(2, 2) + [
-        step(kv(1, 0), (2, 2, 2), wait=False), step(kv(3, 0), (3, 2, 3), wait=False),
-        step(kv(1, 2), (0, 1, 0)), step(kv(1, 1), (0, 3, 0)), step((2, 0), (2, 1, 2)),
-        step(kv(0, 0), (4, 2, 2), wait=False, half=4), step(kv(3, 1), (1, 1, 1)),
-        step(kv(0, 2), (4, 1, 2), wait=False), step(unit=(0, 0, 0)),
-        step(unit=(4, 0, 2), result=1), step(kv(0, 1), (1, 3, 1)), step((2, 1), (2, 0, 2), wait=False),
-        step(kv(1, 3), (5, 2, 3), wait=False, half=5), step(kv(3, 2), (1, 0, 1)),
-        step(kv(0, 3), (5, 1, 3)), step(kv(3, 3), (3, 1, 3), wait=False),
-        step(unit=(5, 0, 3), result=2), step(unit=(2, 3, 2)), step(slash, (3, 0, 3), wait=False),
-        step(unit=(3, 3, 3), half=0), step(half=1), step(half=2), step(half=3)])
-    roles.append(own(3) + [
-        step(kv(2, 0)), step(slash, (0, 2, 0)), step(kv(2, 1), half=0), step(unit=(1, 2, 1), half=1),
-        step(kv(1, 0)), step(kv(1, 1), (0, 1, 0)), step(kv(0, 0), (1, 1, 1)), step((4, 0), (0, 0, 0)),
-        step(kv(0, 1)), step(unit=(1, 0, 1)), step((4, 1))])
-    return roles
+    def unit(slot, src, h, wait=True):
+        return (slot + (8 if wait else 0), src * 4 + h)
+
+    def mine(h, src):
+        return unit(h, src, h)
+
+    def early(z):
+        return [(None, unit(h, z, h, False)) for h in range(heads)]
+
+    def build(steps):
+        out, before = [], None
+        for recv, now, *more in steps + [(None, None)]:
+            busy = now is not None or before is not None
+            code = now if now is not None else IDLE
+            out.append((recv or (0, 0)) + code + (int(busy) | sum(more),))
+            before = now
+        return out
+
+    quest, slash, part = (2, 0), (3, 0), (4, 0)
+
+    def local(h, src=OWN):
+        return unit(h, src, h, src == OWN and h == 0)
+
+    zero = early(0) + [(None, local(h, ALONE)) for h in range(heads)]
+    late = None
+    for src in (1, 2, 3):
+        for h in range(heads):
+            zero.append((kv(src, h), late))
+            late = mine(h, src)
+    zero.append((None, late))
+
+    one = early(1) + [
+        (kv(2, 0), None), (kv(0, 0), mine(0, 2)), (kv(2, 1), mine(0, 0)), (kv(0, 3), mine(1, 2)),
+        (kv(2, 2), mine(3, 0)), (kv(0, 1), mine(2, 2), 4), (kv(2, 3), mine(1, 0)), (kv(0, 2), mine(3, 2), 8),
+        (kv(3, 0), mine(2, 0)), (kv(3, 1), mine(0, 3)), (slash, mine(1, 3)), (kv(3, 2), local(0)),
+        (None, local(1)), (None, local(2)), (kv(3, 3), mine(2, 3)), (None, local(3)), (None, mine(3, 3))]
+
+    two = early(2) + [
+        (kv(3, 0), None), (kv(1, 0), mine(0, 3)), (kv(1, 3), mine(0, 1)), (quest, mine(3, 1)),
+        (kv(1, 1), unit(4, 2, 3, False)), (kv(3, 1), unit(4, GUEST, 3, False)), (kv(0, 0), mine(1, 1)),
+        (None, unit(4, 1, 3, False)), (kv(3, 2), mine(1, 3)), (kv(0, 3), mine(0, 0)), (kv(3, 3), mine(2, 3)),
+        (None, unit(4, 0, 3)), (None, mine(3, 3), 2), (kv(0, 1), unit(3, 0, 3, False)), (kv(1, 2), mine(1, 0)),
+        (kv(0, 2), mine(2, 1)), (None, mine(2, 0)), (slash, None), (None, local(0)),
+        (None, local(1)), (None, local(2)), (None, local(3))]
+
+    three = early(3) + [(None, local(3, ALONE)),
+        (kv(2, 0), None), (slash, mine(0, 2)), (kv(2, 1), local(0)), (None, mine(1, 2)), (None, local(1)),
+        (kv(2, 2), local(2)), (kv(1, 0), mine(2, 2)), (kv(1, 1), mine(0, 1)), (kv(0, 0), mine(1, 1)),
+        (None, mine(0, 0)), (part, None), (kv(0, 1), None), (kv(1, 2), mine(1, 0)), (kv(0, 2), mine(2, 1)),
+        (None, mine(2, 0))]
+    return [build(role) for role in (zero, one, two, three)]
 
 
 def chain(n, q_hbm, nk_hbm, nv_hbm, ck_hbm, cv_hbm, vp_ref, vl_ref, sl_ref, cnt_ref, o_ref,
-          q_raw, nk_raw, nv_raw, ck_raw, cv_raw, q_ref, slab, sort_kv, sort_q,
-          pool, acc, peak, total, mask, part_acc, part_stat,
-          hop_send, hop_recv, sib_send, sib_recv, sl_sem, q_sem, part_sem, in_sem):
+          q_raw, nk_raw, nv_raw, ck_raw, cv_raw, q_ref, sort_kv, sort_q, ext,
+          pool, acc, peak, total, mask, part_acc, part_stat, scores_a, scores_b, top_a, top_b,
+          hop_send, hop_recv, sib_send, sib_recv, sl_sem, q_sem, part_sem, in_sem, ready):
     z = lax.axis_index("ctx")
     s = lax.axis_index("sub")
     heads = pool.shape[1]
-    rows, head_dim = q_ref.shape[1:]
+    head_dim, rows = acc.shape[1:]
     groups = rows // BLK
     wide = heads * BLK
     last = n - 1
-    guests = heads // 2
+    stay = heads - GUESTS
     loads = [pltpu.make_async_copy(src, dst, in_sem.at[i]) for i, (src, dst) in enumerate(
         [(ck_hbm, ck_raw), (cv_hbm, cv_raw), (nk_hbm, nk_raw), (nv_hbm, nv_raw), (q_hbm, q_raw)])]
     for load in loads:
@@ -347,10 +361,6 @@
     barrier = pltpu.get_barrier_semaphore()
     pl.semaphore_signal(barrier, inc=1, device_id=sib_id, device_id_type=MESH)
 
-    @pl.when(has_left)
-    def _():
-        pl.semaphore_signal(barrier, inc=1, device_id={"ctx": z - 1}, device_id_type=MESH)
-
     @pl.when(has_right)
     def _():
         pl.semaphore_signal(barrier, inc=1, device_id={"ctx": z + 1}, device_id_type=MESH)
@@ -358,9 +368,136 @@
     ids = lax.broadcasted_iota(jnp.int32, (wide, wide), 0)
     at = lax.broadcasted_iota(jnp.int32, (wide, wide), 1)
     sort_kv[...] = jnp.where(at == (ids % BLK) * heads + ids // BLK, 1.0, 0.0).astype(jnp.bfloat16)
+
+    pl.semaphore_wait(barrier, 1 + has_left.astype(jnp.int32))
+
+    @pl.when(has_left)
+    def _():
+        pl.semaphore_signal(ready, inc=1, device_id={"ctx": z - 1}, device_id_type=MESH)
+
+    def put_keys(raw, put):
+        ordered = jnp.dot(sort_kv[...], raw, preferred_element_type=jnp.float32).astype(jnp.bfloat16)
+        for h in range(heads):
+            put(h, ordered[h * BLK:(h + 1) * BLK])
+
+    def put_values(raw, put):
+        ordered = lax.dot_general(raw, sort_kv[...], (((0,), (1,)), ((), ())),
+                                  preferred_element_type=jnp.float32).astype(jnp.bfloat16)
+        for h in range(heads):
+            put(h, ordered[:, h * BLK:(h + 1) * BLK])
+
+    def put_pool(b, kv):
+        def put(h, block):
+            pool[z, h, b, kv] = block
+        return put
+
+    def put_new(kv):
+        def put(h, block):
+            pool[OWN, h, 0, kv] = block
+            pool[GUEST, h, 0, kv] = block
+            pool[GUEST, h, 1, kv] = jnp.zeros_like(block)
+        return put
+
+    def hop(src, h, right):
+        return pltpu.make_async_remote_copy(
+            src_ref=pool.at[src, h, s], dst_ref=pool.at[src, h, s],
+            send_sem=hop_send.at[src, h, int(right)], recv_sem=hop_recv.at[src, h],
+            device_id={"ctx": z + 1 if right else z - 1}, device_id_type=MESH)
+
+    def sib(src, h, part):
+        return pltpu.make_async_remote_copy(
+            src_ref=pool.at[src, h, part], dst_ref=pool.at[src, h, part],
+            send_sem=sib_send.at[src, h], recv_sem=sib_recv.at[src, h],
+            device_id=sib_id, device_id_type=MESH)
+
+    def slash_hop(count):
+        return pltpu.make_async_remote_copy(
+            src_ref=pool.at[OWN, pl.ds(0, count), 0, s], dst_ref=pool.at[OWN, pl.ds(0, count), 1, s],
+            send_sem=sl_sem.at[0], recv_sem=sl_sem.at[1],
+            device_id={"ctx": z + 1}, device_id_type=MESH)
+
+    def slash_sib(count, part):
+        block = pool.at[OWN, pl.ds(0, count), 1, part]
+        return pltpu.make_async_remote_copy(
+            src_ref=block, dst_ref=block,
+            send_sem=sl_sem.at[2], recv_sem=sl_sem.at[3],
+            device_id=sib_id, device_id_type=MESH)
+
+    def guest_q(g):
+        return pltpu.make_async_remote_copy(
+            src_ref=q_ref.at[stay + g, pl.ds(0, head_dim)], dst_ref=q_ref.at[heads + g, pl.ds(0, head_dim)],
+            send_sem=q_sem.at[0, g], recv_sem=q_sem.at[1, g],
+            device_id={"ctx": z - 1}, device_id_type=MESH)
+
+    def guest_mask():
+        return pltpu.make_async_remote_copy(
+            src_ref=mask.at[0], dst_ref=mask.at[1],
+            send_sem=q_sem.at[0, GUESTS], recv_sem=q_sem.at[1, GUESTS],
+            device_id={"ctx": z - 1}, device_id_type=MESH)
+
+    def guest_part(g):
+        return [pltpu.make_async_remote_copy(
+            src_ref=ref.at[g], dst_ref=ref.at[g],
+            send_sem=part_sem.at[0, g, i], recv_sem=part_sem.at[1, g, i],
+            device_id={"ctx": z + 1}, device_id_type=MESH)
+            for i, ref in enumerate((part_acc, part_stat))]
+
+    loads[0].wait()
+    put_keys(ck_raw[vp_ref[s]], put_pool(s, 0))
+    loads[1].wait()
+    put_values(cv_raw[vp_ref[s]], put_pool(s, 1))
+
+    @pl.when((z == 1) | (z == 2))
+    def _():
+        for h in range(heads):
+            hop(z, h, False).start()
+
+    @pl.when(z == last)
+    def _():
+        hop(z, 0, False).start()
+
+    @pl.when(has_right)
+    def _():
+        pl.semaphore_wait(ready, 1)
+
+    @pl.when(z == 0)
+    def _():
+        for h in (0, 3, 1, 2):
+            hop(z, h, True).start()
+
+    @pl.when(z == 1)
+    def _():
+        for h in (0, 3, 1):
+            hop(z, h, True).start()
+
+    @pl.when(z == 2)
+    def _():
+        hop(z, 0, True).start()
+
+    loads[2].wait()
+    loads[3].wait()
+    put_keys(nk_raw[...], put_new(0))
+    put_values(nv_raw[...], put_new(1))
+
+    @pl.when(z == 0)
+    def _():
+        slash_hop(heads).start()
+
+    @pl.when(z == 2)
+    def _():
+        slash_hop(stay).start()
+        hop(z, 1, True).start()
+        hop(z, 2, True).start()
+
     token = (ids % BLK) // groups
     sort_q[...] = jnp.where(at == (token * heads + ids // BLK) * groups + ids % groups,
                             1.0, 0.0).astype(jnp.bfloat16)
+    loads[4].wait()
+    for part in range(rows // BLK):
+        ordered = lax.dot_general(q_raw[part * wide:(part + 1) * wide], sort_q[...], (((0,), (1,)), ((), ())),
+                                  preferred_element_type=jnp.float32).astype(jnp.bfloat16)
+        for h in range(heads):
+            q_ref[h, 0:head_dim, part * BLK:(part + 1) * BLK] = ordered[:, h * BLK:(h + 1) * BLK]
 
     def unseen(hit):
         return jnp.full((1, BLK), jnp.where(hit > 0, 0.0, jnp.inf), jnp.float32)
@@ -373,181 +510,78 @@
     hit = jnp.int32(0)
     for i in range(sl_ref.shape[1]):
         hit = hit | jnp.where((sl_ref[0, i] == 1) & (i < cnt_ref[0, 1]), 1, 0)
-    mask[0, 2 * n:2 * n + 1] = unseen(hit)
-
-    def put_keys(raw, put):
-        ordered = jnp.dot(sort_kv[...], raw, preferred_element_type=jnp.float32).astype(jnp.bfloat16)
-        for h in range(heads):
-            put(h, ordered[h * BLK:(h + 1) * BLK])
-
-    def put_values(raw, put):
-        ordered = lax.dot_general(raw, sort_kv[...], (((0,), (1,)), ((), ())),
-                                  preferred_element_type=jnp.float32).astype(jnp.bfloat16)
-        for h in range(heads):
-            put(h, ordered[:, h * BLK:(h + 1) * BLK])
-
-    def put_pool(b, kv):
-        def put(h, block):
-            pool[z, h, b, kv] = block
-        return put
-
-    def put_slab(kv):
-        def put(h, block):
-            slab[0, kv, h] = block
-        return put
-
-    def hop(src, h, right):
-        return pltpu.make_async_remote_copy(
-            src_ref=pool.at[src, h, s], dst_ref=pool.at[src, h, s],
-            send_sem=hop_send.at[src, h, int(right)], recv_sem=hop_recv.at[src, h],
-            device_id={"ctx": z + 1 if right else z - 1}, device_id_type=MESH)
-
-    def sib(src, h, part=s):
-        return pltpu.make_async_remote_copy(
-            src_ref=pool.at[src, h, part], dst_ref=pool.at[src, h, part],
-            send_sem=sib_send.at[src, h], recv_sem=sib_recv.at[src, h],
-            device_id=sib_id, device_id_type=MESH)
-
-    def slash_hop(count):
-        return pltpu.make_async_remote_copy(
-            src_ref=slab.at[0, s, pl.ds(0, count)], dst_ref=slab.at[1, s, pl.ds(0, count)],
-            send_sem=sl_sem.at[0], recv_sem=sl_sem.at[1],
-            device_id={"ctx": z + 1}, device_id_type=MESH)
-
-    def slash_sib(count, part):
-        return pltpu.make_async_remote_copy(
-            src_ref=slab.at[1, part, pl.ds(0, count)], dst_ref=slab.at[1, part, pl.ds(0, count)],
-            send_sem=sl_sem.at[2], recv_sem=sl_sem.at[3],
-            device_id=sib_id, device_id_type=MESH)
-
-    def guest_q(g):
-        return pltpu.make_async_remote_copy(
-            src_ref=q_ref.at[heads - guests + g], dst_ref=q_ref.at[heads + g],
-            send_sem=q_sem.at[0, g], recv_sem=q_sem.at[1, g],
-            device_id={"ctx": z - 1}, device_id_type=MESH)
-
-    def guest_mask():
-        return pltpu.make_async_remote_copy(
-            src_ref=mask.at[0], dst_ref=mask.at[1],
-            send_sem=q_sem.at[0, guests], recv_sem=q_sem.at[1, guests],
-            device_id={"ctx": z - 1}, device_id_type=MESH)
-
-    def guest_part(g):
-        return [pltpu.make_async_remote_copy(
-            src_ref=ref.at[g], dst_ref=ref.at[g],
-            send_sem=part_sem.at[0, g, i], recv_sem=part_sem.at[1, g, i],
-            device_id={"ctx": z + 1}, device_id_type=MESH)
-            for i, ref in enumerate((part_acc, part_stat))]
-
-    loads[0].wait()
-    put_keys(ck_raw[vp_ref[s]], put_pool(s, 0))
-    loads[1].wait()
-    put_values(cv_raw[vp_ref[s]], put_pool(s, 1))
-    pl.semaphore_wait(barrier, 1 + has_left.astype(jnp.int32) + has_right.astype(jnp.int32))
-
-    @pl.when(z == 0)
-    def _():
-        for h in (0, 2, 1, 3):
-            hop(z, h, True).start()
-
-    @pl.when(z == 1)
-    def _():
-        for h in (0, 2, 1):
-            hop(z, h, True).start()
-
-    @pl.when(z == 2)
-    def _():
-        hop(z, 0, True).start()
-
-    @pl.when((z == 1) | (z == 2))
-    def _():
-        for h in range(heads):
+    mask[0, 2 * OWN:2 * OWN + 2] = jnp.concatenate([jnp.zeros((1, BLK), jnp.float32), unseen(hit)], 0)
+    mask[0, 2 * GUEST:2 * GUEST + 2] = jnp.concatenate([unseen(hit), jnp.full((1, BLK), jnp.inf, jnp.float32)], 0)
+    mask[0, 2 * ALONE:2 * ALONE + 2] = jnp.concatenate(
+        [jnp.zeros((1, BLK), jnp.float32), jnp.full((1, BLK), jnp.inf, jnp.float32)], 0)
+
+    @pl.when(z == last)
+    def _():
+        for g in range(GUESTS):
+            guest_q(g).start()
+        guest_mask().start()
+        for h in range(1, heads):
             hop(z, h, False).start()
-
-    @pl.when(z == last)
-    def _():
-        hop(z, 0, False).start()
-        guest_mask().start()
-
-    loads[2].wait()
-    loads[3].wait()
-    put_keys(nk_raw[...], put_slab(0))
-    put_values(nv_raw[...], put_slab(1))
-
-    @pl.when(z == 0)
-    def _():
-        slash_hop(heads).start()
-
-    @pl.when(z == 2)
-    def _():
-        slash_hop(heads - guests).start()
-        hop(z, 1, True).start()
-
-    loads[4].wait()
-    for part in range(rows // BLK):
-        ordered = jnp.dot(sort_q[...], q_raw[part * wide:(part + 1) * wide],
-                          preferred_element_type=jnp.float32).astype(jnp.bfloat16)
-        for h in range(heads):
-            q_ref[h, part * BLK:(part + 1) * BLK] = ordered[h * BLK:(h + 1) * BLK]
-
-    @pl.when(z == last)
-    def _():
-        guest_q(0).start()
-        hop(z, 1, False).start()
-        guest_q(1).start()
-        hop(z, 2, False).start()
-        hop(z, 3, False).start()
 
     put_keys(ck_raw[vp_ref[1 - s]], put_pool(1 - s, 0))
     put_values(cv_raw[vp_ref[1 - s]], put_pool(1 - s, 1))
 
-    @pl.when(z == last - 1)
-    def _():
-        for g in range(guests):
-            acc[heads + g] = jnp.zeros_like(acc[heads + g])
-            total[heads + g] = jnp.zeros_like(total[heads + g])
-            peak[heads + g] = jnp.full_like(peak[heads + g], -1e30)
-
-    def score(keys, q):
-        return lax.dot_general(keys, q, (((1,), (1,)), ((), ())),
-                               preferred_element_type=jnp.float32)
-
-    def diagonal(h, carry):
-        scores = score(slab[0, 0, h], q_ref[h])
-        key_id = lax.broadcasted_iota(jnp.int32, scores.shape, 0)
-        row_id = lax.broadcasted_iota(jnp.int32, scores.shape, 1) // groups
-        scores = jnp.where(key_id <= row_id, scores, -jnp.inf)
-        high = jnp.max(scores, axis=0, keepdims=True)
-        weights = jnp.exp2((scores - high) * c)
-        peak[h] = high
-        total[h] = jnp.sum(weights, axis=0, keepdims=True)
-        acc[h] = jnp.dot(slab[0, 1, h], weights.astype(jnp.bfloat16), preferred_element_type=jnp.float32)
-        return carry
-
-    lax.fori_loop(0, heads, diagonal, 0)
+    key_id = lax.broadcasted_iota(jnp.int32, (BLK, rows), 0)
+    row_id = lax.broadcasted_iota(jnp.int32, (BLK, rows), 1) // groups
+    later = jnp.where(key_id > row_id, -1e30, 0.0).astype(jnp.bfloat16)
+    slots = acc.shape[0]
+    for slot in range(slots):
+        q_ref[slot, head_dim:] = later if slot < heads else jnp.zeros_like(later)
+        acc[slot] = jnp.zeros_like(acc[slot])
+        total[slot] = jnp.zeros_like(total[slot])
+        peak[slot] = jnp.full_like(peak[slot], -1e30)
+    q_ref[slots - 1, 0:head_dim] = jnp.zeros_like(later)
+    one_at = lax.broadcasted_iota(jnp.int32, (BLK, BLK), 0) == lax.broadcasted_iota(jnp.int32, (BLK, BLK), 1)
+    ext[0] = jnp.zeros((BLK, BLK), jnp.bfloat16)
+    ext[1] = jnp.where(one_at, 1.0, 0.0).astype(jnp.bfloat16)
+    scores_b[...] = jnp.zeros_like(scores_b)
+    top_b[...] = jnp.zeros_like(top_b)
 
     def spread(row):
         return jnp.concatenate([row] * groups, 1)
 
-    def update(slot, blocks):
+    def place(src):
+        return src - src // ALONE
+
+    def hidden(slot, src, b):
+        return spread(mask[(slot // heads) % 2 * (1 - slot // (slots - 1)), pl.ds(2 * src + b, 1)])
+
+    def ahead(unit, scores, top):
+        slot, src, h = unit
         q = q_ref[slot]
+        high = None
+        for b in range(2):
+            causal = (src // OWN) * (1 - src % 2) if b == 0 else 0
+            keys = jnp.concatenate([pool[place(src), h, b, 0], ext[causal]], 1)
+            found = jnp.dot(keys, q, preferred_element_type=jnp.float32)
+            scores[b * BLK:(b + 1) * BLK] = found
+            part = jnp.max(found, axis=0, keepdims=True) - hidden(slot, src, b)
+            high = part if high is None else jnp.maximum(high, part)
+        top[...] = high
+
+    def behind(unit, scores, top):
+        slot, src, h = unit
         old = peak[slot]
-        raw = [score(keys, q) for keys, _, _ in blocks]
-        hide = [spread(row) for _, _, row in blocks]
-        high = old
-        for scores, row in zip(raw, hide):
-            high = jnp.maximum(high, jnp.max(scores, axis=0, keepdims=True) - row)
+        high = jnp.maximum(old, top[...])
         factor = jnp.exp2((old - high) * c)
         peak[slot] = high
-        weights = [jnp.exp2((scores - (high + row)) * c) for scores, row in zip(raw, hide)]
-        add = functools.reduce(jnp.add, [jnp.sum(w, axis=0, keepdims=True) for w in weights])
-        total[slot] = total[slot] * factor + add
-        rounded = jnp.concatenate([w.astype(jnp.bfloat16) for w in weights], 0)
-        values = jnp.concatenate([values for _, values, _ in blocks], 1)
-        acc[slot] = acc[slot] * factor + jnp.dot(values, rounded, preferred_element_type=jnp.float32)
-
-    roles = plan()
+        weights = [jnp.exp2((scores[b * BLK:(b + 1) * BLK] - (high + hidden(slot, src, b))) * c)
+                   .astype(jnp.bfloat16) for b in range(2)]
+        values = jnp.concatenate([pool[place(src), h, b, 1] for b in range(2)], 1)
+        values = jnp.concatenate([values, jnp.ones((16, 2 * BLK), jnp.bfloat16)], 0)
+        add = jnp.dot(values, jnp.concatenate(weights, 0), preferred_element_type=jnp.float32)
+        acc[slot] = acc[slot] * factor + add[:head_dim]
+        total[slot] = total[slot] * factor + add[head_dim:head_dim + 1]
+
+    roles = plan(heads)
     steps = max(len(role) for role in roles)
+    steps += steps % 2
+    roles = [role + [(0, 0) + IDLE + (0,)] * (steps - len(role)) for role in roles]
 
     def by_role(values):
         out = jnp.int32(values[-1])
@@ -555,56 +589,46 @@
             out = jnp.where(z == i, jnp.int32(values[i]), out)
         return out
 
-    words = []
-    for field in range(7):
-        chunks = []
-        for start in range(0, steps, 7):
-            chunks.append(by_role([sum(step[field] << (4 * i) for i, step in enumerate(role[start:start + 7]))
-                                   for role in roles]))
-        words.append(chunks)
-
-    def step(t, carry):
-        group = t // 7
-        shift = 4 * (t % 7)
-
+    words = [[by_role([sum(step[field] << (BITS * i) for i, step in enumerate(role[start:start + PACK]))
+                       for role in roles]) for start in range(0, steps, PACK)] for field in range(5)]
+
+    def step(t, before, bufs, old_bufs):
         def look(field):
             word = words[field][-1]
             for i in reversed(range(len(words[field]) - 1)):
-                word = jnp.where(group == i, words[field][i], word)
-            return lax.shift_right_logical(word, shift) & 15
-
-        kind, message, unit, block, half, result, extra = [look(field) for field in range(7)]
+                word = jnp.where(t // PACK == i, words[field][i], word)
+            return lax.shift_right_logical(word, BITS * (t % PACK)) & (2 ** BITS - 1)
+
+        kind, message, code, block, flags = [look(field) for field in range(5)]
         src, h = message // 4, message % 4
 
         @pl.when(kind == 1)
         def _():
             hop(src, h, True).wait_recv()
-
-            @pl.when((src < z) & ((z == 1) | ((z == 2) & (h < heads - guests))))
-            def _():
-                hop(src, h, True).start()
 
             @pl.when((src > z) & has_left)
             def _():
                 hop(src, h, False).start()
 
-            sib(src, h).start()
-
-            @pl.when(extra == 1)
+            @pl.when((src < z) & ((z < last - 1) | ((z == last - 1) & (h < stay))))
             def _():
-                hop(z, 3, True).start()
-
-            @pl.when(extra == 2)
-            def _():
-                slash_hop(heads).start()
+                hop(src, h, True).start()
+
+            sib(src, h, s).start()
+
+        @pl.when((flags // 4) % 2 == 1)
+        def _():
+            hop(z, 2, True).start()
+
+        @pl.when(flags // 8 == 1)
+        def _():
+            slash_hop(heads).start()
 
         @pl.when(kind == 2)
         def _():
-            @pl.when(h == 0)
-            def _():
-                guest_mask().wait_recv()
-
-            guest_q(h).wait_recv()
+            guest_mask().wait_recv()
+            for g in range(GUESTS):
+                guest_q(g).wait_recv()
 
         @pl.when((kind == 3) & has_right)
         def _():
@@ -613,61 +637,57 @@
 
         @pl.when((kind == 3) & (z == last))
         def _():
-            slash_hop(heads - guests).wait_recv()
-            slash_sib(heads - guests, s).start()
+            slash_hop(stay).wait_recv()
+            slash_sib(stay, s).start()
 
         @pl.when(kind == 4)
         def _():
             for copy in guest_part(h):
                 copy.wait_recv()
-            slot = heads - guests + h
+            slot = stay + h
             old, new = peak[slot], part_stat[h, 0:1]
             high = jnp.maximum(old, new)
             mine, theirs = jnp.exp2((old - high) * c), jnp.exp2((new - high) * c)
             acc[slot] = acc[slot] * mine + part_acc[h].astype(jnp.float32) * theirs
             total[slot] = total[slot] * mine + part_stat[h, 1:2] * theirs
 
-        @pl.when(unit > 0)
-        def _():
-            slot = (unit - 1) % 8
-            src, h = block // 4, block % 4
-
-            @pl.when(unit < 8)
-            def _():
-                sib(src, h, 1 - s).wait_recv()
-
-            guest = slot // heads
-            update(slot, [(pool[src, h, b, 0], pool[src, h, b, 1], mask[guest, pl.ds(2 * src + b, 1)])
-                          for b in range(2)])
-
-        @pl.when(half > 0)
-        def _():
-            slot = half - 1
-            guest = slot // heads
-
-            @pl.when((slot == 0) & has_right)
-            def _():
-                slash_sib(heads, 1 - s).wait_recv()
-
-            @pl.when((slot == 0) & (z == last))
-            def _():
-                slash_sib(heads - guests, 1 - s).wait_recv()
-
-            h = slot - guest * guests
-            update(slot, [(slab[1 - guest, 0, h], slab[1 - guest, 1, h], mask[guest, 2 * n:2 * n + 1])])
-
-        @pl.when(result > 0)
-        def _():
-            g = result - 1
+        unit = (code % 8, block // 4, block % 4)
+
+        @pl.when((code > 7) & (unit[1] < OWN))
+        def _():
+            sib(unit[1], unit[2], 1 - s).wait_recv()
+
+        @pl.when((code > 7) & (unit[1] == OWN) & has_right)
+        def _():
+            slash_sib(heads, 1 - s).wait_recv()
+
+        @pl.when((code > 7) & (unit[1] == OWN) & (z == last))
+        def _():
+            slash_sib(stay, 1 - s).wait_recv()
+
+        @pl.when(flags % 2 == 1)
+        def _():
+            ahead(unit, *bufs)
+            behind(before, *old_bufs)
+
+        @pl.when((flags // 2) % 2 == 1)
+        def _():
+            g = 0
             part_acc[g] = acc[heads + g].astype(jnp.bfloat16)
             part_stat[g, 0:1] = peak[heads + g]
             part_stat[g, 1:2] = total[heads + g]
             for copy in guest_part(g):
                 copy.start()
 
-        return carry
-
-    lax.fori_loop(0, by_role([len(role) for role in roles]), step, 0)
+        return unit
+
+    def two_steps(i, before):
+        mid = step(2 * i, before, (scores_a, top_a), (scores_b, top_b))
+        return step(2 * i + 1, mid, (scores_b, top_b), (scores_a, top_a))
+
+    lengths = [max(t for t, step in enumerate(role) if step[0] or step[4]) + 1 for role in roles]
+    idle = (jnp.int32(IDLE[0]), jnp.int32(GUEST), jnp.int32(0))
+    lax.fori_loop(0, by_role([(length + 1) // 2 for length in lengths]), two_steps, idle)
 
     for part in range(rows // BLK):
         lanes = slice(part * BLK, (part + 1) * BLK)
@@ -680,7 +700,7 @@
     def drain(i, carry):
         src, h = i // heads, i % heads
 
-        @pl.when((src <= z) & (z < last) & ((z < last - 1) | (h < heads - guests)))
+        @pl.when((src <= z) & (z < last) & ((z < last - 1) | (h < stay)))
         def _():
             hop(src, h, True).wait_send()
 
@@ -688,9 +708,9 @@
         def _():
             hop(src, h, False).wait_send()
 
-        @pl.when((src != z) & ((z < last) | (h < heads - guests)))
-        def _():
-            sib(src, h).wait_send()
+        @pl.when((src != z) & ((z < last) | (h < stay)))
+        def _():
+            sib(src, h, s).wait_send()
         return carry
 
     lax.fori_loop(0, n * heads, drain, 0)
@@ -701,8 +721,8 @@
 
     @pl.when(z == last - 1)
     def _():
-        slash_hop(heads - guests).wait_send()
-        for g in range(guests):
+        slash_hop(stay).wait_send()
+        for g in range(GUESTS):
             for copy in guest_part(g):
                 copy.wait_send()
 
@@ -712,9 +732,9 @@
 
     @pl.when(z == last)
     def _():
-        slash_sib(heads - guests, s).wait_send()
+        slash_sib(stay, s).wait_send()
         guest_mask().wait_send()
-        for g in range(guests):
+        for g in range(GUESTS):
             guest_q(g).wait_send()
 
 
@@ -727,14 +747,16 @@
 def chain_call(n, q, nk, nv, ck, cv, tables, heads, rows, head_dim):
     def vmem(*shape):
         return pltpu.VMEM(shape, jnp.bfloat16)
+
+    def wide_vmem(*shape):
+        return pltpu.VMEM(shape, jnp.float32)
 
     hbm = pl.BlockSpec(memory_space=pltpu.HBM)
     smem = pl.BlockSpec(memory_space=pltpu.SMEM)
     in_vmem = pl.BlockSpec(memory_space=pltpu.VMEM)
     dma = pltpu.SemaphoreType.DMA
     cached, wide = ck.shape[:2]
-    guests = heads // 2
-    f32 = jnp.float32
+    slots = 7
     out = pl.pallas_call(
         functools.partial(chain, n),
         out_shape=pltpu.VMEM((heads * rows, head_dim), jnp.bfloat16),
@@ -743,20 +765,17 @@
         scratch_shapes=[
             vmem(heads * rows, head_dim), vmem(wide, head_dim), vmem(wide, head_dim),
             vmem(cached, wide, head_dim), vmem(cached, wide, head_dim),
-            vmem(heads + guests, rows, head_dim), vmem(2, 2, heads, BLK, head_dim),
-            vmem(wide, wide), vmem(wide, wide),
-            vmem(n, heads, 2, 2, BLK, head_dim),
-            pltpu.VMEM((heads + guests, head_dim, rows), f32),
-            pltpu.VMEM((heads + guests, 1, rows), f32),
-            pltpu.VMEM((heads + guests, 1, rows), f32),
-            pltpu.VMEM((2, 16, BLK), f32),
-            vmem(guests, head_dim, rows), pltpu.VMEM((guests, 8, rows), f32),
+            vmem(slots, 2 * head_dim, rows), vmem(wide, wide), vmem(wide, wide), vmem(2, BLK, BLK),
+            vmem(n + 2, heads, 2, 2, BLK, head_dim),
+            wide_vmem(slots, head_dim, rows), wide_vmem(slots, 1, rows), wide_vmem(slots, 1, rows),
+            wide_vmem(2, 16, BLK), vmem(GUESTS, head_dim, rows), wide_vmem(GUESTS, 8, rows),
+            wide_vmem(2 * BLK, rows), wide_vmem(2 * BLK, rows), wide_vmem(1, rows), wide_vmem(1, rows),
             dma((n, heads, 2)), dma((n, heads)), dma((n, heads)), dma((n, heads)), dma((4,)),
-            dma((2, guests + 1)), dma((2, guests, 2)), dma((5,)),
+            dma((2, GUESTS + 1)), dma((2, GUESTS, 2)), dma((5,)), pltpu.SemaphoreType.REGULAR,
         ],
         compiler_params=pltpu.CompilerParams(
-            collective_id=0, has_side_effects=True, vmem_limit_bytes=40 * 2**20),
-    )(q, nk, nv, ck, cv, *tables)
+            collective_id=0, has_side_effects=True, vmem_limit_bytes=60 * 2**20),
+    )(*[pltpu.with_memory_space_constraint(x, pltpu.HBM) for x in (q, nk, nv, ck, cv)], *tables)
     return pl.pallas_call(
         store,
         out_shape=jax.ShapeDtypeStruct(out.shape, out.dtype),

time: 41.2 us -> 30 us (0.73)
  the two profiles are of different devices: /device:TPU:0 before, /device:TPU:27 now
where the time goes in v2:
time: 30 us; the launch traced here: 29.9 us
  Pallas kernels  29.9 us (100%)
    pallas_call x1, Pallas kernels, chain_call(): pl.pallas_call(functools.partial(chain, n), out_shape=pltpu.VMEM((heads *...  29.1 us
    pallas_call x1, Pallas kernels, chain_call(): pl.pallas_call(store, out_shape=jax.ShapeDtypeStruct(out.shape, out.dtype...  0.8 us

profile of v2, /device:TPU:27, one launch (start us, length us, event | category | flops | bytes accessed | tf_op | source)
XLA Modules:
  0.0 29.9 jit_solution(5926762845339005560)
XLA Ops:
  0.0 29.1 %shard_map.91.o_vmem = bf16[2048,128]{1,0:T(8,128)(2,1)S(1)} custom-call(bf16[2048,128]{1,0:T(8,128)(2,1)} %bitcast.8, bf16[512,128]{1,0:T(8,128)(2,1)} %bitcast.9, bf16[512,128]{1,0:T(8,128)(2,1)} %bitcast.10, bf16[16,512,128]{2,1,0:T(8,128)(2,1)} %bitcast.6, bf16[16,512,128]{2,1,0:T(8,128)(2,1)} %bitcast.7, s32[2]{0:T(128)} %vp_ref.1, s32[1,6]{1,0:T(1,128)} %vl_ref.1, ...), custom_call_target="tpu_custom_call" | custom-call | tf_op jit(solution)/shard_map/pallas_call | solution.py:760
  29.1 0.8 %shard_map.92 = bf16[2048,128]{1,0:T(8,128)(2,1)} custom-call(bf16[2048,128]{1,0:T(8,128)(2,1)S(1)} %shard_map.91.o_vmem), custom_call_target="tpu_custom_call" | custom-call | tf_op jit(solution)/shard_map/pallas_call | solution.py:779

commit v3 on v2

--- a/solution.py
+++ b/solution.py
@@ -302,7 +302,7 @@
             before = now
         return out
 
-    quest, slash, part = (2, 0), (3, 0), (4, 0)
+    quest, slash = (2, 0), (3, 0)
 
     def local(h, src=OWN):
         return unit(h, src, h, src == OWN and h == 0)
@@ -310,7 +310,7 @@
     zero = early(0) + [(None, local(h, ALONE)) for h in range(heads)]
     late = None
     for src in (1, 2, 3):
-        for h in range(heads):
+        for h in range(heads - GUESTS):
             zero.append((kv(src, h), late))
             late = mine(h, src)
     zero.append((None, late))
@@ -318,28 +318,30 @@
     one = early(1) + [
         (kv(2, 0), None), (kv(0, 0), mine(0, 2)), (kv(2, 1), mine(0, 0)), (kv(0, 3), mine(1, 2)),
         (kv(2, 2), mine(3, 0)), (kv(0, 1), mine(2, 2), 4), (kv(2, 3), mine(1, 0)), (kv(0, 2), mine(3, 2), 8),
-        (kv(3, 0), mine(2, 0)), (kv(3, 1), mine(0, 3)), (slash, mine(1, 3)), (kv(3, 2), local(0)),
-        (None, local(1)), (None, local(2)), (kv(3, 3), mine(2, 3)), (None, local(3)), (None, mine(3, 3))]
+        (quest, unit(4, 2, 3, False)), (kv(3, 0), unit(4, 1, 3, False)), (kv(3, 3), mine(2, 0)),
+        (kv(3, 1), mine(0, 3)), (None, unit(4, 3, 3)),
+        (kv(3, 2), unit(3, 3, 3, False), 2), (slash, mine(1, 3)), (None, local(0)), (None, local(1)),
+        (None, local(2)), (None, local(3)), (None, mine(2, 3))]
 
     two = early(2) + [
-        (kv(3, 0), None), (kv(1, 0), mine(0, 3)), (kv(1, 3), mine(0, 1)), (quest, mine(3, 1)),
-        (kv(1, 1), unit(4, 2, 3, False)), (kv(3, 1), unit(4, GUEST, 3, False)), (kv(0, 0), mine(1, 1)),
-        (None, unit(4, 1, 3, False)), (kv(3, 2), mine(1, 3)), (kv(0, 3), mine(0, 0)), (kv(3, 3), mine(2, 3)),
-        (None, unit(4, 0, 3)), (None, mine(3, 3), 2), (kv(0, 1), unit(3, 0, 3, False)), (kv(1, 2), mine(1, 0)),
-        (kv(0, 2), mine(2, 1)), (None, mine(2, 0)), (slash, None), (None, local(0)),
-        (None, local(1)), (None, local(2)), (None, local(3))]
-
-    three = early(3) + [(None, local(3, ALONE)),
-        (kv(2, 0), None), (slash, mine(0, 2)), (kv(2, 1), local(0)), (None, mine(1, 2)), (None, local(1)),
-        (kv(2, 2), local(2)), (kv(1, 0), mine(2, 2)), (kv(1, 1), mine(0, 1)), (kv(0, 0), mine(1, 1)),
-        (None, mine(0, 0)), (part, None), (kv(0, 1), None), (kv(1, 2), mine(1, 0)), (kv(0, 2), mine(2, 1)),
+        (kv(3, 0), None), (kv(1, 0), mine(0, 3)), (kv(3, 3), mine(0, 1)), (kv(1, 3), mine(3, 3)),
+        (kv(1, 1), mine(3, 1)), (kv(0, 0), mine(1, 1)), (quest, mine(0, 0)), (kv(3, 1), unit(4, 2, 3, False)),
+        (kv(0, 3), unit(4, GUEST, 3, False)), (kv(3, 2), unit(4, 1, 3, False)), (None, mine(1, 3)),
+        (kv(0, 1), unit(4, 0, 3)), (kv(1, 2), unit(3, 0, 3, False)), (None, mine(2, 3)), (None, mine(1, 0)),
+        (kv(0, 2), mine(2, 1), 2), (None, mine(2, 0)), (slash, None), (None, local(0)), (None, local(1)),
+        (None, local(2)), (None, local(3))]
+
+    three = early(3) + [
+        (None, local(3, ALONE)), (kv(2, 0), None), (slash, mine(0, 2)), (kv(2, 1), local(0)), (None, mine(1, 2)),
+        (None, local(1)), (kv(2, 2), local(2)), (kv(1, 0), mine(2, 2)), (kv(1, 1), mine(0, 1)),
+        (kv(0, 0), mine(1, 1)), (kv(0, 1), mine(0, 0)), (kv(1, 2), mine(1, 0)), (kv(0, 2), mine(2, 1)),
         (None, mine(2, 0))]
     return [build(role) for role in (zero, one, two, three)]
 
 
 def chain(n, q_hbm, nk_hbm, nv_hbm, ck_hbm, cv_hbm, vp_ref, vl_ref, sl_ref, cnt_ref, o_ref,
           q_raw, nk_raw, nv_raw, ck_raw, cv_raw, q_ref, sort_kv, sort_q, ext,
-          pool, acc, peak, total, mask, part_acc, part_stat, scores_a, scores_b, top_a, top_b,
+          pool, acc, peak, total, mask, part_acc, part_stat, scores_a, scores_b, top_a, top_b, most,
           hop_send, hop_recv, sib_send, sib_recv, sl_sem, q_sem, part_sem, in_sem, ready):
     z = lax.axis_index("ctx")
     s = lax.axis_index("sub")
@@ -351,12 +353,14 @@
     stay = heads - GUESTS
     loads = [pltpu.make_async_copy(src, dst, in_sem.at[i]) for i, (src, dst) in enumerate(
         [(ck_hbm, ck_raw), (cv_hbm, cv_raw), (nk_hbm, nk_raw), (nv_hbm, nv_raw), (q_hbm, q_raw)])]
-    for load in loads:
-        load.start()
+    loads[0].start()
     c = math.log2(math.e) / math.sqrt(head_dim)
     has_left = z > 0
     has_right = z < last
     sib_id = {"sub": 1 - s}
+    inner = has_left & has_right
+    host_id = {"ctx": jnp.where(z == 0, 1, last - 1)}
+    guest_id = {"ctx": jnp.where(z == 1, 0, last)}
 
     barrier = pltpu.get_barrier_semaphore()
     pl.semaphore_signal(barrier, inc=1, device_id=sib_id, device_id_type=MESH)
@@ -404,6 +408,12 @@
             send_sem=hop_send.at[src, h, int(right)], recv_sem=hop_recv.at[src, h],
             device_id={"ctx": z + 1 if right else z - 1}, device_id_type=MESH)
 
+    def first_hop(h, kv, right):
+        return pltpu.make_async_remote_copy(
+            src_ref=pool.at[z, h, s, kv], dst_ref=pool.at[z, h, s, kv],
+            send_sem=hop_send.at[z, h, int(right)], recv_sem=hop_recv.at[z, h],
+            device_id={"ctx": z + 1 if right else z - 1}, device_id_type=MESH)
+
     def sib(src, h, part):
         return pltpu.make_async_remote_copy(
             src_ref=pool.at[src, h, part], dst_ref=pool.at[src, h, part],
@@ -427,34 +437,46 @@
         return pltpu.make_async_remote_copy(
             src_ref=q_ref.at[stay + g, pl.ds(0, head_dim)], dst_ref=q_ref.at[heads + g, pl.ds(0, head_dim)],
             send_sem=q_sem.at[0, g], recv_sem=q_sem.at[1, g],
-            device_id={"ctx": z - 1}, device_id_type=MESH)
+            device_id=host_id, device_id_type=MESH)
 
     def guest_mask():
         return pltpu.make_async_remote_copy(
             src_ref=mask.at[0], dst_ref=mask.at[1],
             send_sem=q_sem.at[0, GUESTS], recv_sem=q_sem.at[1, GUESTS],
-            device_id={"ctx": z - 1}, device_id_type=MESH)
+            device_id=host_id, device_id_type=MESH)
 
     def guest_part(g):
         return [pltpu.make_async_remote_copy(
             src_ref=ref.at[g], dst_ref=ref.at[g],
             send_sem=part_sem.at[0, g, i], recv_sem=part_sem.at[1, g, i],
-            device_id={"ctx": z + 1}, device_id_type=MESH)
+            device_id=guest_id, device_id_type=MESH)
             for i, ref in enumerate((part_acc, part_stat))]
 
+    def leftward(kv):
+        @pl.when(inner)
+        def _():
+            for h in range(stay):
+                first_hop(h, kv, False).start()
+
+        @pl.when(z == 2)
+        def _():
+            for h in range(stay, heads):
+                first_hop(h, kv, False).start()
+
+        @pl.when(z == last)
+        def _():
+            for h in (0, 3):
+                first_hop(h, kv, False).start()
+
     loads[0].wait()
+    loads[1].start()
     put_keys(ck_raw[vp_ref[s]], put_pool(s, 0))
+    leftward(0)
+    for load in loads[2:]:
+        load.start()
     loads[1].wait()
     put_values(cv_raw[vp_ref[s]], put_pool(s, 1))
-
-    @pl.when((z == 1) | (z == 2))
-    def _():
-        for h in range(heads):
-            hop(z, h, False).start()
-
-    @pl.when(z == last)
-    def _():
-        hop(z, 0, False).start()
+    leftward(1)
 
     @pl.when(has_right)
     def _():
@@ -463,31 +485,31 @@
     @pl.when(z == 0)
     def _():
         for h in (0, 3, 1, 2):
-            hop(z, h, True).start()
+            for kv in range(2):
+                first_hop(h, kv, True).start()
 
     @pl.when(z == 1)
     def _():
         for h in (0, 3, 1):
-            hop(z, h, True).start()
+            for kv in range(2):
+                first_hop(h, kv, True).start()
 
     @pl.when(z == 2)
     def _():
-        hop(z, 0, True).start()
+        for kv in range(2):
+            first_hop(0, kv, True).start()
 
     loads[2].wait()
     loads[3].wait()
     put_keys(nk_raw[...], put_new(0))
     put_values(nv_raw[...], put_new(1))
 
-    @pl.when(z == 0)
-    def _():
-        slash_hop(heads).start()
-
     @pl.when(z == 2)
     def _():
         slash_hop(stay).start()
-        hop(z, 1, True).start()
-        hop(z, 2, True).start()
+        for h in range(1, stay):
+            for kv in range(2):
+                first_hop(h, kv, True).start()
 
     token = (ids % BLK) // groups
     sort_q[...] = jnp.where(at == (token * heads + ids // BLK) * groups + ids % groups,
@@ -515,13 +537,21 @@
     mask[0, 2 * ALONE:2 * ALONE + 2] = jnp.concatenate(
         [jnp.zeros((1, BLK), jnp.float32), jnp.full((1, BLK), jnp.inf, jnp.float32)], 0)
 
-    @pl.when(z == last)
+    @pl.when((z == 0) | (z == last))
     def _():
         for g in range(GUESTS):
             guest_q(g).start()
         guest_mask().start()
-        for h in range(1, heads):
-            hop(z, h, False).start()
+
+    @pl.when(z == 0)
+    def _():
+        slash_hop(heads).start()
+
+    @pl.when(z == last)
+    def _():
+        for h in (1, 2):
+            for kv in range(2):
+                first_hop(h, kv, False).start()
 
     put_keys(ck_raw[vp_ref[1 - s]], put_pool(1 - s, 0))
     put_values(cv_raw[vp_ref[1 - s]], put_pool(1 - s, 1))
@@ -606,7 +636,7 @@
         def _():
             hop(src, h, True).wait_recv()
 
-            @pl.when((src > z) & has_left)
+            @pl.when((src > z) & ((z > 1) | ((z == 1) & (h < stay))))
             def _():
                 hop(src, h, False).start()
 
@@ -618,7 +648,8 @@
 
         @pl.when((flags // 4) % 2 == 1)
         def _():
-            hop(z, 2, True).start()
+            for kv in range(2):
+                first_hop(2, kv, True).start()
 
         @pl.when(flags // 8 == 1)
         def _():
@@ -639,17 +670,6 @@
         def _():
             slash_hop(stay).wait_recv()
             slash_sib(stay, s).start()
-
-        @pl.when(kind == 4)
-        def _():
-            for copy in guest_part(h):
-                copy.wait_recv()
-            slot = stay + h
-            old, new = peak[slot], part_stat[h, 0:1]
-            high = jnp.maximum(old, new)
-            mine, theirs = jnp.exp2((old - high) * c), jnp.exp2((new - high) * c)
-            acc[slot] = acc[slot] * mine + part_acc[h].astype(jnp.float32) * theirs
-            total[slot] = total[slot] * mine + part_stat[h, 1:2] * theirs
 
         unit = (code % 8, block // 4, block % 4)
 
@@ -689,13 +709,31 @@
     idle = (jnp.int32(IDLE[0]), jnp.int32(GUEST), jnp.int32(0))
     lax.fori_loop(0, by_role([(length + 1) // 2 for length in lengths]), two_steps, idle)
 
-    for part in range(rows // BLK):
+    def ordered(part, those):
         lanes = slice(part * BLK, (part + 1) * BLK)
         done = jnp.concatenate(
-            [(acc[h, :, lanes] / total[h, :, lanes]).astype(jnp.bfloat16) for h in range(heads)], 1)
-        o_ref[part * wide:(part + 1) * wide] = lax.dot_general(
-            sort_q[...], done, (((0,), (1,)), ((), ())),
-            preferred_element_type=jnp.float32).astype(o_ref.dtype)
+            [(acc[h, :, lanes] / total[h, :, lanes]).astype(jnp.bfloat16) for h in those], 1)
+        return lax.dot_general(sort_q[those.start * BLK:those.stop * BLK], done, (((0,), (1,)), ((), ())),
+                               preferred_element_type=jnp.float32)
+
+    for part in range(rows // BLK):
+        most[part * wide:(part + 1) * wide] = ordered(part, range(stay)).astype(o_ref.dtype)
+
+    @pl.when((z == 0) | (z == last))
+    def _():
+        for g in range(GUESTS):
+            for copy in guest_part(g):
+                copy.wait_recv()
+            slot = stay + g
+            old, new = peak[slot], part_stat[g, 0:1]
+            high = jnp.maximum(old, new)
+            mine, theirs = jnp.exp2((old - high) * c), jnp.exp2((new - high) * c)
+            acc[slot] = acc[slot] * mine + part_acc[g].astype(jnp.float32) * theirs
+            total[slot] = total[slot] * mine + part_stat[g, 1:2] * theirs
+
+    for part in range(rows // BLK):
+        lines = slice(part * wide, (part + 1) * wide)
+        o_ref[lines] = most[lines] + ordered(part, range(stay, heads)).astype(o_ref.dtype)
 
     def drain(i, carry):
         src, h = i // heads, i % heads
@@ -704,11 +742,11 @@
         def _():
             hop(src, h, True).wait_send()
 
-        @pl.when((src >= z) & has_left)
+        @pl.when((src >= z) & ((z > 1) | ((z == 1) & (h < stay))))
         def _():
             hop(src, h, False).wait_send()
 
-        @pl.when((src != z) & ((z < last) | (h < stay)))
+        @pl.when((src != z) & (inner | (h < stay)))
         def _():
             sib(src, h, s).wait_send()
         return carry
@@ -722,26 +760,34 @@
     @pl.when(z == last - 1)
     def _():
         slash_hop(stay).wait_send()
+
+    @pl.when(inner)
+    def _():
+        slash_sib(heads, s).wait_send()
         for g in range(GUESTS):
             for copy in guest_part(g):
                 copy.wait_send()
 
-    @pl.when(has_left & has_right)
-    def _():
-        slash_sib(heads, s).wait_send()
-
     @pl.when(z == last)
     def _():
         slash_sib(stay, s).wait_send()
+
+    @pl.when((z == 0) | (z == last))
+    def _():
         guest_mask().wait_send()
         for g in range(GUESTS):
             guest_q(g).wait_send()
 
 
 def store(o_vmem, o_hbm, sem):
-    copy = pltpu.make_async_copy(o_vmem, o_hbm, sem)
-    copy.start()
-    copy.wait()
+    copies = sem.shape[0]
+    rows = o_vmem.shape[0] // copies
+    for i in range(copies):
+        lines = pl.ds(i * rows, rows)
+        pltpu.make_async_copy(o_vmem.at[lines], o_hbm.at[lines], sem.at[i]).start()
+    for i in range(copies):
+        lines = pl.ds(i * rows, rows)
+        pltpu.make_async_copy(o_vmem.at[lines], o_hbm.at[lines], sem.at[i]).wait()
 
 
 def chain_call(n, q, nk, nv, ck, cv, tables, heads, rows, head_dim):
@@ -770,6 +816,7 @@
             wide_vmem(slots, head_dim, rows), wide_vmem(slots, 1, rows), wide_vmem(slots, 1, rows),
             wide_vmem(2, 16, BLK), vmem(GUESTS, head_dim, rows), wide_vmem(GUESTS, 8, rows),
             wide_vmem(2 * BLK, rows), wide_vmem(2 * BLK, rows), wide_vmem(1, rows), wide_vmem(1, rows),
+            vmem(heads * rows, head_dim),
             dma((n, heads, 2)), dma((n, heads)), dma((n, heads)), dma((n, heads)), dma((4,)),
             dma((2, GUESTS + 1)), dma((2, GUESTS, 2)), dma((5,)), pltpu.SemaphoreType.REGULAR,
         ],
@@ -781,7 +828,7 @@
         out_shape=jax.ShapeDtypeStruct(out.shape, out.dtype),
         in_specs=[in_vmem],
         out_specs=hbm,
-        scratch_shapes=[dma],
+        scratch_shapes=[dma((4,))],
         compiler_params=pltpu.CompilerParams(vmem_limit_bytes=2**20),
     )(out)
 

time: 30 us -> 30.5 us (1.017)
  the two profiles are of different devices: /device:TPU:27 before, /device:TPU:0 now
where the time goes in v3:
time: 30.5 us; the launch traced here: 30.3 us
  Pallas kernels  30.3 us (99%)
    pallas_call x1, Pallas kernels, chain_call(): pl.pallas_call(functools.partial(chain, n), out_shape=pltpu.VMEM((heads *...  29.5 us
    pallas_call x1, Pallas kernels, chain_call(): pl.pallas_call(store, out_shape=jax.ShapeDtypeStruct(out.shape, out.dtype...  0.82 us

profile of v3, /device:TPU:0, one launch (start us, length us, event | category | flops | bytes accessed | tf_op | source)
XLA Modules:
  0.0 30.3 jit_solution(4047399273752346232)
XLA Ops:
  0.0 29.5 %shard_map.91.o_vmem = bf16[2048,128]{1,0:T(8,128)(2,1)S(1)} custom-call(bf16[2048,128]{1,0:T(8,128)(2,1)} %bitcast.8, bf16[512,128]{1,0:T(8,128)(2,1)} %bitcast.9, bf16[512,128]{1,0:T(8,128)(2,1)} %bitcast.10, bf16[16,512,128]{2,1,0:T(8,128)(2,1)} %bitcast.6, bf16[16,512,128]{2,1,0:T(8,128)(2,1)} %bitcast.7, s32[2]{0:T(128)} %vp_ref.1, s32[1,6]{1,0:T(1,128)} %vl_ref.1, ...), custom_call_target="tpu_custom_call" | custom-call | tf_op jit(solution)/shard_map/pallas_call | solution.py:806
  29.5 0.8 %shard_map.92 = bf16[2048,128]{1,0:T(8,128)(2,1)} custom-call(bf16[2048,128]{1,0:T(8,128)(2,1)S(1)} %shard_map.91.o_vmem), custom_call_target="tpu_custom_call" | custom-call | tf_op jit(solution)/shard_map/pallas_call | solution.py:826

commit v4 on v3

--- a/solution.py
+++ b/solution.py
@@ -280,63 +280,55 @@
 GUESTS = 1
 
 
+NONE = (-1, -1)
+QUEST = (-2, 0)
+SLASH = (-3, 0)
+
+
 def plan(heads):
-    def kv(src, h):
-        return (1, src * 4 + h)
-
-    def unit(slot, src, h, wait=True):
-        return (slot + (8 if wait else 0), src * 4 + h)
-
-    def mine(h, src):
-        return unit(h, src, h)
-
-    def early(z):
-        return [(None, unit(h, z, h, False)) for h in range(heads)]
-
-    def build(steps):
-        out, before = [], None
-        for recv, now, *more in steps + [(None, None)]:
-            busy = now is not None or before is not None
-            code = now if now is not None else IDLE
-            out.append((recv or (0, 0)) + code + (int(busy) | sum(more),))
+    zero = [(NONE, (0, 0), 0), (NONE, (0, ALONE), 0), (NONE, (1, 0), 0), ((1, 0), (1, ALONE), 0), (NONE, (2, 0), 0),
+        (NONE, (2, ALONE), 0), ((1, 1), (0, 1), 0), (NONE, (3, 0), 0), (NONE, (3, ALONE), 0), ((1, 2), (1, 1), 0),
+        (NONE, NONE, 0), ((1, 3), NONE, 0), (NONE, (2, 1), 0), (NONE, NONE, 0), (NONE, (3, 1), 0), ((2, 0), NONE, 0),
+        ((2, 1), NONE, 0), (NONE, (0, 2), 0), (NONE, NONE, 0), (NONE, (1, 2), 0), ((2, 2), NONE, 0),
+        ((2, 3), NONE, 0), (NONE, (2, 2), 0), (NONE, NONE, 0), (NONE, (3, 2), 0), ((3, 0), NONE, 0),
+        ((3, 1), NONE, 0), (NONE, (0, 3), 0), (NONE, NONE, 0), (NONE, (1, 3), 0), ((3, 2), NONE, 0),
+        ((3, 3), NONE, 0), (NONE, (2, 3), 0), (NONE, NONE, 16), (NONE, (3, 3), 0), (NONE, NONE, 0)]
+    one = [((0, 0), (0, 1), 0), ((2, 0), (1, 1), 0), ((0, 3), (2, 1), 0), (NONE, (0, 0), 0), ((2, 1), (0, 2), 0),
+        ((0, 1), (3, 0), 4), (NONE, (3, 1), 0), (NONE, (1, 2), 0), ((2, 2), (1, 0), 0), ((0, 2), NONE, 8),
+        ((2, 3), NONE, 0), (NONE, (2, 2), 0), (NONE, (2, 0), 0), (NONE, NONE, 0), ((3, 0), (3, 2), 0),
+        (SLASH, NONE, 0), ((3, 1), NONE, 0), (NONE, (0, 3), 0), (NONE, NONE, 0), (NONE, (0, OWN), 0),
+        ((3, 2), (1, 3), 0), (NONE, (1, OWN), 0), (NONE, (2, OWN), 0), ((3, 3), (2, 3), 0), (NONE, (3, OWN), 16),
+        (NONE, NONE, 0), (NONE, (3, 3), 0), (NONE, NONE, 0)]
+    two = [((1, 0), (0, 2), 0), ((3, 0), (1, 2), 0), (NONE, (2, 2), 0), ((1, 3), (0, 1), 0), ((3, 1), (0, 3), 0),
+        (NONE, (3, 2), 0), ((1, 1), (3, 1), 0), ((3, 2), (1, 3), 0), (NONE, NONE, 0), ((0, 0), (1, 1), 0),
+        ((3, 3), (2, 3), 0), (NONE, NONE, 0), ((0, 3), (0, 0), 0), (NONE, (3, 3), 0), (NONE, NONE, 0),
+        (NONE, (3, 0), 0), ((0, 1), NONE, 0), (QUEST, NONE, 0), (NONE, (4, 2), 0), ((1, 2), (4, GUEST), 0),
+        (NONE, (4, 1), 0), (NONE, (4, 0), 0), (NONE, (1, 0), 0), ((0, 2), (2, 1), 2), (NONE, NONE, 0),
+        (NONE, (2, 0), 0), (NONE, NONE, 0), (SLASH, NONE, 0), (NONE, (0, OWN), 0), (NONE, (1, OWN), 0),
+        (NONE, (2, OWN), 0), (NONE, (3, OWN), 16), (NONE, NONE, 0)]
+    three = [(NONE, (0, 3), 0), ((2, 0), (1, 3), 0), (NONE, (2, 3), 0), (NONE, (3, 3), 0), (NONE, (0, 2), 0),
+        (SLASH, (3, ALONE), 0), (NONE, NONE, 0), (NONE, (0, OWN), 0), ((2, 1), (1, OWN), 0), (NONE, (2, OWN), 0),
+        (NONE, NONE, 0), ((2, 2), (1, 2), 0), (NONE, NONE, 0), ((1, 0), NONE, 0), (NONE, (2, 2), 0), (NONE, NONE, 0),
+        (NONE, (0, 1), 0), ((1, 1), NONE, 0), ((0, 0), NONE, 0), (NONE, (1, 1), 0), (NONE, NONE, 0),
+        (NONE, (0, 0), 0), ((0, 1), NONE, 0), ((1, 2), NONE, 0), (NONE, (1, 0), 0), (NONE, NONE, 0),
+        (NONE, (2, 1), 0), ((0, 2), NONE, 0), (NONE, (2, 0), 0), (NONE, NONE, 16)]
+
+    def build(z, table):
+        out, before, used = [], NONE, set()
+        for recv, now, flags in table + [(NONE, NONE, 0)]:
+            kind, message = (1, recv[0] * 4 + recv[1]) if recv[0] >= 0 else (-recv[0] if recv != NONE else 0, 0)
+            slot, src = now
+            h = slot if slot < heads else slot - GUESTS
+            key = OWN if src == OWN else (src, h)
+            first = now != NONE and key not in used and src not in (z, GUEST, ALONE)
+            used.add(key)
+            code = (slot + (8 if first else 0), src * 4 + h) if now != NONE else IDLE
+            busy = now != NONE or before != NONE
+            out.append((kind, message) + code + (int(busy) | flags,))
             before = now
         return out
 
-    quest, slash = (2, 0), (3, 0)
-
-    def local(h, src=OWN):
-        return unit(h, src, h, src == OWN and h == 0)
-
-    zero = early(0) + [(None, local(h, ALONE)) for h in range(heads)]
-    late = None
-    for src in (1, 2, 3):
-        for h in range(heads - GUESTS):
-            zero.append((kv(src, h), late))
-            late = mine(h, src)
-    zero.append((None, late))
-
-    one = early(1) + [
-        (kv(2, 0), None), (kv(0, 0), mine(0, 2)), (kv(2, 1), mine(0, 0)), (kv(0, 3), mine(1, 2)),
-        (kv(2, 2), mine(3, 0)), (kv(0, 1), mine(2, 2), 4), (kv(2, 3), mine(1, 0)), (kv(0, 2), mine(3, 2), 8),
-        (quest, unit(4, 2, 3, False)), (kv(3, 0), unit(4, 1, 3, False)), (kv(3, 3), mine(2, 0)),
-        (kv(3, 1), mine(0, 3)), (None, unit(4, 3, 3)),
-        (kv(3, 2), unit(3, 3, 3, False), 2), (slash, mine(1, 3)), (None, local(0)), (None, local(1)),
-        (None, local(2)), (None, local(3)), (None, mine(2, 3))]
-
-    two = early(2) + [
-        (kv(3, 0), None), (kv(1, 0), mine(0, 3)), (kv(3, 3), mine(0, 1)), (kv(1, 3), mine(3, 3)),
-        (kv(1, 1), mine(3, 1)), (kv(0, 0), mine(1, 1)), (quest, mine(0, 0)), (kv(3, 1), unit(4, 2, 3, False)),
-        (kv(0, 3), unit(4, GUEST, 3, False)), (kv(3, 2), unit(4, 1, 3, False)), (None, mine(1, 3)),
-        (kv(0, 1), unit(4, 0, 3)), (kv(1, 2), unit(3, 0, 3, False)), (None, mine(2, 3)), (None, mine(1, 0)),
-        (kv(0, 2), mine(2, 1), 2), (None, mine(2, 0)), (slash, None), (None, local(0)), (None, local(1)),
-        (None, local(2)), (None, local(3))]
-
-    three = early(3) + [
-        (None, local(3, ALONE)), (kv(2, 0), None), (slash, mine(0, 2)), (kv(2, 1), local(0)), (None, mine(1, 2)),
-        (None, local(1)), (kv(2, 2), local(2)), (kv(1, 0), mine(2, 2)), (kv(1, 1), mine(0, 1)),
-        (kv(0, 0), mine(1, 1)), (kv(0, 1), mine(0, 0)), (kv(1, 2), mine(1, 0)), (kv(0, 2), mine(2, 1)),
-        (None, mine(2, 0))]
-    return [build(role) for role in (zero, one, two, three)]
+    return [build(z, table) for z, table in enumerate((zero, one, two, three))]
 
 
 def chain(n, q_hbm, nk_hbm, nv_hbm, ck_hbm, cv_hbm, vp_ref, vl_ref, sl_ref, cnt_ref, o_ref,
@@ -354,13 +346,12 @@
     loads = [pltpu.make_async_copy(src, dst, in_sem.at[i]) for i, (src, dst) in enumerate(
         [(ck_hbm, ck_raw), (cv_hbm, cv_raw), (nk_hbm, nk_raw), (nv_hbm, nv_raw), (q_hbm, q_raw)])]
     loads[0].start()
+    loads[1].start()
     c = math.log2(math.e) / math.sqrt(head_dim)
     has_left = z > 0
     has_right = z < last
     sib_id = {"sub": 1 - s}
     inner = has_left & has_right
-    host_id = {"ctx": jnp.where(z == 0, 1, last - 1)}
-    guest_id = {"ctx": jnp.where(z == 1, 0, last)}
 
     barrier = pltpu.get_barrier_semaphore()
     pl.semaphore_signal(barrier, inc=1, device_id=sib_id, device_id_type=MESH)
@@ -437,46 +428,35 @@
         return pltpu.make_async_remote_copy(
             src_ref=q_ref.at[stay + g, pl.ds(0, head_dim)], dst_ref=q_ref.at[heads + g, pl.ds(0, head_dim)],
             send_sem=q_sem.at[0, g], recv_sem=q_sem.at[1, g],
-            device_id=host_id, device_id_type=MESH)
+            device_id={"ctx": z - 1}, device_id_type=MESH)
 
     def guest_mask():
         return pltpu.make_async_remote_copy(
             src_ref=mask.at[0], dst_ref=mask.at[1],
             send_sem=q_sem.at[0, GUESTS], recv_sem=q_sem.at[1, GUESTS],
-            device_id=host_id, device_id_type=MESH)
+            device_id={"ctx": z - 1}, device_id_type=MESH)
 
     def guest_part(g):
         return [pltpu.make_async_remote_copy(
             src_ref=ref.at[g], dst_ref=ref.at[g],
             send_sem=part_sem.at[0, g, i], recv_sem=part_sem.at[1, g, i],
-            device_id=guest_id, device_id_type=MESH)
+            device_id={"ctx": z + 1}, device_id_type=MESH)
             for i, ref in enumerate((part_acc, part_stat))]
 
-    def leftward(kv):
-        @pl.when(inner)
-        def _():
-            for h in range(stay):
+    def leftward(*blocks):
+        @pl.when(has_left)
+        def _():
+            for h, kv in blocks:
                 first_hop(h, kv, False).start()
 
-        @pl.when(z == 2)
-        def _():
-            for h in range(stay, heads):
-                first_hop(h, kv, False).start()
-
-        @pl.when(z == last)
-        def _():
-            for h in (0, 3):
-                first_hop(h, kv, False).start()
-
     loads[0].wait()
-    loads[1].start()
     put_keys(ck_raw[vp_ref[s]], put_pool(s, 0))
-    leftward(0)
+    leftward((0, 0), (1, 0))
     for load in loads[2:]:
         load.start()
     loads[1].wait()
     put_values(cv_raw[vp_ref[s]], put_pool(s, 1))
-    leftward(1)
+    leftward((0, 1), (1, 1), *[(h, kv) for h in range(2, heads) for kv in range(2)])
 
     @pl.when(has_right)
     def _():
@@ -537,21 +517,15 @@
     mask[0, 2 * ALONE:2 * ALONE + 2] = jnp.concatenate(
         [jnp.zeros((1, BLK), jnp.float32), jnp.full((1, BLK), jnp.inf, jnp.float32)], 0)
 
-    @pl.when((z == 0) | (z == last))
+    @pl.when(z == 0)
+    def _():
+        slash_hop(heads).start()
+
+    @pl.when(z == last)
     def _():
         for g in range(GUESTS):
             guest_q(g).start()
         guest_mask().start()
-
-    @pl.when(z == 0)
-    def _():
-        slash_hop(heads).start()
-
-    @pl.when(z == last)
-    def _():
-        for h in (1, 2):
-            for kv in range(2):
-                first_hop(h, kv, False).start()
 
     put_keys(ck_raw[vp_ref[1 - s]], put_pool(1 - s, 0))
     put_values(cv_raw[vp_ref[1 - s]], put_pool(1 - s, 1))
@@ -608,6 +582,36 @@
         acc[slot] = acc[slot] * factor + add[:head_dim]
         total[slot] = total[slot] * factor + add[head_dim:head_dim + 1]
 
+    def ordered(part, those):
+        lanes = slice(part * BLK, (part + 1) * BLK)
+        done = jnp.concatenate(
+            [(acc[h, :, lanes] / total[h, :, lanes]).astype(jnp.bfloat16) for h in those], 1)
+        return lax.dot_general(sort_q[those.start * BLK:those.stop * BLK], done, (((0,), (1,)), ((), ())),
+                               preferred_element_type=jnp.float32)
+
+    def drain():
+        for index in range(n):
+            right = heads if index < last - 1 else stay if index < last else 0
+
+            @pl.when(z == index)
+            def _():
+                for src in range(n):
+                    for h in range(heads):
+                        if src <= index and h < right:
+                            hop(src, h, True).wait_send()
+                        if src >= index and index > 0:
+                            hop(src, h, False).wait_send()
+                        if src != index and (index < last or h < stay):
+                            sib(src, h, s).wait_send()
+                if right:
+                    slash_hop(right).wait_send()
+                if index > 0:
+                    slash_sib(heads if index < last else stay, s).wait_send()
+                if index == last:
+                    guest_mask().wait_send()
+                    for g in range(GUESTS):
+                        guest_q(g).wait_send()
+
     roles = plan(heads)
     steps = max(len(role) for role in roles)
     steps += steps % 2
@@ -636,7 +640,7 @@
         def _():
             hop(src, h, True).wait_recv()
 
-            @pl.when((src > z) & ((z > 1) | ((z == 1) & (h < stay))))
+            @pl.when((src > z) & has_left)
             def _():
                 hop(src, h, False).start()
 
@@ -651,7 +655,7 @@
             for kv in range(2):
                 first_hop(2, kv, True).start()
 
-        @pl.when(flags // 8 == 1)
+        @pl.when((flags // 8) % 2 == 1)
         def _():
             slash_hop(heads).start()
 
@@ -689,6 +693,11 @@
         def _():
             ahead(unit, *bufs)
             behind(before, *old_bufs)
+
+        @pl.when(flags // 16 == 1)
+        def _():
+            for part in range(rows // BLK):
+                most[part * wide:(part + 1) * wide] = ordered(part, range(stay)).astype(o_ref.dtype)
 
         @pl.when((flags // 2) % 2 == 1)
         def _():
@@ -709,17 +718,9 @@
     idle = (jnp.int32(IDLE[0]), jnp.int32(GUEST), jnp.int32(0))
     lax.fori_loop(0, by_role([(length + 1) // 2 for length in lengths]), two_steps, idle)
 
-    def ordered(part, those):
-        lanes = slice(part * BLK, (part + 1) * BLK)
-        done = jnp.concatenate(
-            [(acc[h, :, lanes] / total[h, :, lanes]).astype(jnp.bfloat16) for h in those], 1)
-        return lax.dot_general(sort_q[those.start * BLK:those.stop * BLK], done, (((0,), (1,)), ((), ())),
-                               preferred_element_type=jnp.float32)
-
-    for part in range(rows // BLK):
-        most[part * wide:(part + 1) * wide] = ordered(part, range(stay)).astype(o_ref.dtype)
-
-    @pl.when((z == 0) | (z == last))
+    drain()
+
+    @pl.when(z == last)
     def _():
         for g in range(GUESTS):
             for copy in guest_part(g):
@@ -735,48 +736,11 @@
         lines = slice(part * wide, (part + 1) * wide)
         o_ref[lines] = most[lines] + ordered(part, range(stay, heads)).astype(o_ref.dtype)
 
-    def drain(i, carry):
-        src, h = i // heads, i % heads
-
-        @pl.when((src <= z) & (z < last) & ((z < last - 1) | (h < stay)))
-        def _():
-            hop(src, h, True).wait_send()
-
-        @pl.when((src >= z) & ((z > 1) | ((z == 1) & (h < stay))))
-        def _():
-            hop(src, h, False).wait_send()
-
-        @pl.when((src != z) & (inner | (h < stay)))
-        def _():
-            sib(src, h, s).wait_send()
-        return carry
-
-    lax.fori_loop(0, n * heads, drain, 0)
-
-    @pl.when(z < last - 1)
-    def _():
-        slash_hop(heads).wait_send()
-
     @pl.when(z == last - 1)
     def _():
-        slash_hop(stay).wait_send()
-
-    @pl.when(inner)
-    def _():
-        slash_sib(heads, s).wait_send()
         for g in range(GUESTS):
             for copy in guest_part(g):
                 copy.wait_send()
-
-    @pl.when(z == last)
-    def _():
-        slash_sib(stay, s).wait_send()
-
-    @pl.when((z == 0) | (z == last))
-    def _():
-        guest_mask().wait_send()
-        for g in range(GUESTS):
-            guest_q(g).wait_send()
 
 
 def store(o_vmem, o_hbm, sem):

time: 30.5 us -> 28 us (0.918)
  Pallas kernels: 30.3 us -> 27.8 us
    pallas_call x1, Pallas kernels: 29.5 us -> 27 us  [chain_call(): pl.pallas_call(functools.partial(chain, n), out_shape=pltpu.VMEM((heads *...]
where the time goes in v4:
time: 28 us; the launch traced here: 27.8 us
  Pallas kernels  27.8 us (99%)
    pallas_call x1, Pallas kernels, chain_call(): pl.pallas_call(functools.partial(chain, n), out_shape=pltpu.VMEM((heads *...  27 us
    pallas_call x1, Pallas kernels, chain_call(): pl.pallas_call(store, out_shape=jax.ShapeDtypeStruct(out.shape, out.dtype...  0.82 us

profile of v4, /device:TPU:0, one launch (start us, length us, event | category | flops | bytes accessed | tf_op | source)
XLA Modules:
  0.0 27.8 jit_solution(16280921134868577968)
XLA Ops:
  0.0 27.0 %shard_map.91.o_vmem = bf16[2048,128]{1,0:T(8,128)(2,1)S(1)} custom-call(bf16[2048,128]{1,0:T(8,128)(2,1)} %bitcast.8, bf16[512,128]{1,0:T(8,128)(2,1)} %bitcast.9, bf16[512,128]{1,0:T(8,128)(2,1)} %bitcast.10, bf16[16,512,128]{2,1,0:T(8,128)(2,1)} %bitcast.6, bf16[16,512,128]{2,1,0:T(8,128)(2,1)} %bitcast.7, s32[2]{0:T(128)} %vp_ref.1, s32[1,6]{1,0:T(1,128)} %vl_ref.1, ...), custom_call_target="tpu_custom_call" | custom-call | tf_op jit(solution)/shard_map/pallas_call | solution.py:770
  27.0 0.8 %shard_map.92 = bf16[2048,128]{1,0:T(8,128)(2,1)} custom-call(bf16[2048,128]{1,0:T(8,128)(2,1)S(1)} %shard_map.91.o_vmem), custom_call_target="tpu_custom_call" | custom-call | tf_op jit(solution)/shard_map/pallas_call | solution.py:790

commit v5 on v4

--- a/solution.py
+++ b/solution.py
@@ -278,6 +278,7 @@
 OWN, GUEST, ALONE = 4, 5, 6
 IDLE = (6, 4 * GUEST)
 GUESTS = 1
+EARLY = 2
 
 
 NONE = (-1, -1)
@@ -291,13 +292,13 @@
         (NONE, NONE, 0), ((1, 3), NONE, 0), (NONE, (2, 1), 0), (NONE, NONE, 0), (NONE, (3, 1), 0), ((2, 0), NONE, 0),
         ((2, 1), NONE, 0), (NONE, (0, 2), 0), (NONE, NONE, 0), (NONE, (1, 2), 0), ((2, 2), NONE, 0),
         ((2, 3), NONE, 0), (NONE, (2, 2), 0), (NONE, NONE, 0), (NONE, (3, 2), 0), ((3, 0), NONE, 0),
-        ((3, 1), NONE, 0), (NONE, (0, 3), 0), (NONE, NONE, 0), (NONE, (1, 3), 0), ((3, 2), NONE, 0),
-        ((3, 3), NONE, 0), (NONE, (2, 3), 0), (NONE, NONE, 16), (NONE, (3, 3), 0), (NONE, NONE, 0)]
+        ((3, 1), NONE, 0), (NONE, (0, 3), 0), (NONE, NONE, 0), (NONE, (1, 3), 0), ((3, 2), NONE, 16),
+        ((3, 3), NONE, 0), (NONE, (2, 3), 0), (NONE, NONE, 0), (NONE, (3, 3), 0), (NONE, NONE, 0)]
     one = [((0, 0), (0, 1), 0), ((2, 0), (1, 1), 0), ((0, 3), (2, 1), 0), (NONE, (0, 0), 0), ((2, 1), (0, 2), 0),
         ((0, 1), (3, 0), 4), (NONE, (3, 1), 0), (NONE, (1, 2), 0), ((2, 2), (1, 0), 0), ((0, 2), NONE, 8),
         ((2, 3), NONE, 0), (NONE, (2, 2), 0), (NONE, (2, 0), 0), (NONE, NONE, 0), ((3, 0), (3, 2), 0),
         (SLASH, NONE, 0), ((3, 1), NONE, 0), (NONE, (0, 3), 0), (NONE, NONE, 0), (NONE, (0, OWN), 0),
-        ((3, 2), (1, 3), 0), (NONE, (1, OWN), 0), (NONE, (2, OWN), 0), ((3, 3), (2, 3), 0), (NONE, (3, OWN), 16),
+        ((3, 2), (1, 3), 0), (NONE, (1, OWN), 0), (NONE, (2, OWN), 16), ((3, 3), (2, 3), 0), (NONE, (3, OWN), 0),
         (NONE, NONE, 0), (NONE, (3, 3), 0), (NONE, NONE, 0)]
     two = [((1, 0), (0, 2), 0), ((3, 0), (1, 2), 0), (NONE, (2, 2), 0), ((1, 3), (0, 1), 0), ((3, 1), (0, 3), 0),
         (NONE, (3, 2), 0), ((1, 1), (3, 1), 0), ((3, 2), (1, 3), 0), (NONE, NONE, 0), ((0, 0), (1, 1), 0),
@@ -305,13 +306,13 @@
         (NONE, (3, 0), 0), ((0, 1), NONE, 0), (QUEST, NONE, 0), (NONE, (4, 2), 0), ((1, 2), (4, GUEST), 0),
         (NONE, (4, 1), 0), (NONE, (4, 0), 0), (NONE, (1, 0), 0), ((0, 2), (2, 1), 2), (NONE, NONE, 0),
         (NONE, (2, 0), 0), (NONE, NONE, 0), (SLASH, NONE, 0), (NONE, (0, OWN), 0), (NONE, (1, OWN), 0),
-        (NONE, (2, OWN), 0), (NONE, (3, OWN), 16), (NONE, NONE, 0)]
+        (NONE, (2, OWN), 16), (NONE, (3, OWN), 0), (NONE, NONE, 0)]
     three = [(NONE, (0, 3), 0), ((2, 0), (1, 3), 0), (NONE, (2, 3), 0), (NONE, (3, 3), 0), (NONE, (0, 2), 0),
         (SLASH, (3, ALONE), 0), (NONE, NONE, 0), (NONE, (0, OWN), 0), ((2, 1), (1, OWN), 0), (NONE, (2, OWN), 0),
         (NONE, NONE, 0), ((2, 2), (1, 2), 0), (NONE, NONE, 0), ((1, 0), NONE, 0), (NONE, (2, 2), 0), (NONE, NONE, 0),
         (NONE, (0, 1), 0), ((1, 1), NONE, 0), ((0, 0), NONE, 0), (NONE, (1, 1), 0), (NONE, NONE, 0),
-        (NONE, (0, 0), 0), ((0, 1), NONE, 0), ((1, 2), NONE, 0), (NONE, (1, 0), 0), (NONE, NONE, 0),
-        (NONE, (2, 1), 0), ((0, 2), NONE, 0), (NONE, (2, 0), 0), (NONE, NONE, 16)]
+        (NONE, (0, 0), 0), ((0, 1), NONE, 0), ((1, 2), NONE, 0), (NONE, (1, 0), 0), (NONE, NONE, 16),
+        (NONE, (2, 1), 0), ((0, 2), NONE, 0), (NONE, (2, 0), 0), (NONE, NONE, 0)]
 
     def build(z, table):
         out, before, used = [], NONE, set()
@@ -331,10 +332,11 @@
     return [build(z, table) for z, table in enumerate((zero, one, two, three))]
 
 
-def chain(n, q_hbm, nk_hbm, nv_hbm, ck_hbm, cv_hbm, vp_ref, vl_ref, sl_ref, cnt_ref, o_ref,
+def chain(n, q_hbm, nk_hbm, nv_hbm, ck_hbm, cv_hbm, vp_hbm, vl_hbm, sl_hbm, cnt_hbm, o_ref,
+          vp_ref, vl_ref, sl_ref, cnt_ref,
           q_raw, nk_raw, nv_raw, ck_raw, cv_raw, q_ref, sort_kv, sort_q, ext,
           pool, acc, peak, total, mask, part_acc, part_stat, scores_a, scores_b, top_a, top_b, most,
-          hop_send, hop_recv, sib_send, sib_recv, sl_sem, q_sem, part_sem, in_sem, ready):
+          send_sem, hop_recv, sib_recv, sl_sem, q_sem, part_sem, in_sem, table_sem, ready):
     z = lax.axis_index("ctx")
     s = lax.axis_index("sub")
     heads = pool.shape[1]
@@ -345,8 +347,12 @@
     stay = heads - GUESTS
     loads = [pltpu.make_async_copy(src, dst, in_sem.at[i]) for i, (src, dst) in enumerate(
         [(ck_hbm, ck_raw), (cv_hbm, cv_raw), (nk_hbm, nk_raw), (nv_hbm, nv_raw), (q_hbm, q_raw)])]
+    tables = [pltpu.make_async_copy(src, dst, table_sem.at[i]) for i, (src, dst) in enumerate(
+        [(vp_hbm, vp_ref), (vl_hbm, vl_ref), (sl_hbm, sl_ref), (cnt_hbm, cnt_ref)])]
     loads[0].start()
     loads[1].start()
+    for table in tables:
+        table.start()
     c = math.log2(math.e) / math.sqrt(head_dim)
     has_left = z > 0
     has_right = z < last
@@ -396,19 +402,19 @@
     def hop(src, h, right):
         return pltpu.make_async_remote_copy(
             src_ref=pool.at[src, h, s], dst_ref=pool.at[src, h, s],
-            send_sem=hop_send.at[src, h, int(right)], recv_sem=hop_recv.at[src, h],
+            send_sem=send_sem.at[int(right)], recv_sem=hop_recv.at[src if right else src - 1, h],
             device_id={"ctx": z + 1 if right else z - 1}, device_id_type=MESH)
 
     def first_hop(h, kv, right):
         return pltpu.make_async_remote_copy(
             src_ref=pool.at[z, h, s, kv], dst_ref=pool.at[z, h, s, kv],
-            send_sem=hop_send.at[z, h, int(right)], recv_sem=hop_recv.at[z, h],
+            send_sem=send_sem.at[int(right)], recv_sem=hop_recv.at[z if right else z - 1, h],
             device_id={"ctx": z + 1 if right else z - 1}, device_id_type=MESH)
 
     def sib(src, h, part):
         return pltpu.make_async_remote_copy(
             src_ref=pool.at[src, h, part], dst_ref=pool.at[src, h, part],
-            send_sem=sib_send.at[src, h], recv_sem=sib_recv.at[src, h],
+            send_sem=send_sem.at[2], recv_sem=sib_recv.at[src - (src > z).astype(jnp.int32), h],
             device_id=sib_id, device_id_type=MESH)
 
     def slash_hop(count):
@@ -449,6 +455,8 @@
             for h, kv in blocks:
                 first_hop(h, kv, False).start()
 
+    for table in tables:
+        table.wait()
     loads[0].wait()
     put_keys(ck_raw[vp_ref[s]], put_pool(s, 0))
     leftward((0, 0), (1, 0))
@@ -585,28 +593,27 @@
     def ordered(part, those):
         lanes = slice(part * BLK, (part + 1) * BLK)
         done = jnp.concatenate(
-            [(acc[h, :, lanes] / total[h, :, lanes]).astype(jnp.bfloat16) for h in those], 1)
+            [(acc[h, :, lanes] * (1.0 / total[h, :, lanes])).astype(jnp.bfloat16) for h in those], 1)
         return lax.dot_general(sort_q[those.start * BLK:those.stop * BLK], done, (((0,), (1,)), ((), ())),
                                preferred_element_type=jnp.float32)
 
     def drain():
+        def sent(kind, sources, count):
+            blocks = pool.at[pl.ds(0, sources), pl.ds(0, count), s]
+            pltpu.make_async_copy(blocks, blocks, send_sem.at[kind]).wait()
+
         for index in range(n):
             right = heads if index < last - 1 else stay if index < last else 0
 
             @pl.when(z == index)
             def _():
-                for src in range(n):
-                    for h in range(heads):
-                        if src <= index and h < right:
-                            hop(src, h, True).wait_send()
-                        if src >= index and index > 0:
-                            hop(src, h, False).wait_send()
-                        if src != index and (index < last or h < stay):
-                            sib(src, h, s).wait_send()
                 if right:
+                    sent(1, index + 1, right)
                     slash_hop(right).wait_send()
                 if index > 0:
+                    sent(0, n - index, heads)
                     slash_sib(heads if index < last else stay, s).wait_send()
+                sent(2, n - 1, heads if index < last else stay)
                 if index == last:
                     guest_mask().wait_send()
                     for g in range(GUESTS):
@@ -638,7 +645,8 @@
 
         @pl.when(kind == 1)
         def _():
-            hop(src, h, True).wait_recv()
+            block = pool.at[src, h, s]
+            pltpu.make_async_copy(block, block, hop_recv.at[src - (src > z).astype(jnp.int32), h]).wait()
 
             @pl.when((src > z) & has_left)
             def _():
@@ -697,7 +705,7 @@
         @pl.when(flags // 16 == 1)
         def _():
             for part in range(rows // BLK):
-                most[part * wide:(part + 1) * wide] = ordered(part, range(stay)).astype(o_ref.dtype)
+                most[part * wide:(part + 1) * wide] = ordered(part, range(EARLY)).astype(o_ref.dtype)
 
         @pl.when((flags // 2) % 2 == 1)
         def _():
@@ -734,7 +742,7 @@
 
     for part in range(rows // BLK):
         lines = slice(part * wide, (part + 1) * wide)
-        o_ref[lines] = most[lines] + ordered(part, range(stay, heads)).astype(o_ref.dtype)
+        o_ref[lines] = most[lines] + ordered(part, range(EARLY, heads)).astype(o_ref.dtype)
 
     @pl.when(z == last - 1)
     def _():
@@ -762,7 +770,6 @@
         return pltpu.VMEM(shape, jnp.float32)
 
     hbm = pl.BlockSpec(memory_space=pltpu.HBM)
-    smem = pl.BlockSpec(memory_space=pltpu.SMEM)
     in_vmem = pl.BlockSpec(memory_space=pltpu.VMEM)
     dma = pltpu.SemaphoreType.DMA
     cached, wide = ck.shape[:2]
@@ -770,9 +777,10 @@
     out = pl.pallas_call(
         functools.partial(chain, n),
         out_shape=pltpu.VMEM((heads * rows, head_dim), jnp.bfloat16),
-        in_specs=[hbm] * 5 + [smem] * 4,
+        in_specs=[hbm] * 9,
         out_specs=in_vmem,
         scratch_shapes=[
+            *[pltpu.SMEM(table.shape, table.dtype) for table in tables],
             vmem(heads * rows, head_dim), vmem(wide, head_dim), vmem(wide, head_dim),
             vmem(cached, wide, head_dim), vmem(cached, wide, head_dim),
             vmem(slots, 2 * head_dim, rows), vmem(wide, wide), vmem(wide, wide), vmem(2, BLK, BLK),
@@ -781,12 +789,12 @@
             wide_vmem(2, 16, BLK), vmem(GUESTS, head_dim, rows), wide_vmem(GUESTS, 8, rows),
             wide_vmem(2 * BLK, rows), wide_vmem(2 * BLK, rows), wide_vmem(1, rows), wide_vmem(1, rows),
             vmem(heads * rows, head_dim),
-            dma((n, heads, 2)), dma((n, heads)), dma((n, heads)), dma((n, heads)), dma((4,)),
-            dma((2, GUESTS + 1)), dma((2, GUESTS, 2)), dma((5,)), pltpu.SemaphoreType.REGULAR,
+            dma((3,)), dma((n - 1, heads)), dma((n - 1, heads)), dma((4,)),
+            dma((2, GUESTS + 1)), dma((2, GUESTS, 2)), dma((5,)), dma((4,)), pltpu.SemaphoreType.REGULAR,
         ],
         compiler_params=pltpu.CompilerParams(
             collective_id=0, has_side_effects=True, vmem_limit_bytes=60 * 2**20),
-    )(*[pltpu.with_memory_space_constraint(x, pltpu.HBM) for x in (q, nk, nv, ck, cv)], *tables)
+    )(*[pltpu.with_memory_space_constraint(x, pltpu.HBM) for x in (q, nk, nv, ck, cv, *tables)])
     return pl.pallas_call(
         store,
         out_shape=jax.ShapeDtypeStruct(out.shape, out.dtype),

time: 28 us -> 26.4 us (0.943)
  Pallas kernels: 27.8 us -> 26.2 us
    pallas_call x1, Pallas kernels: 27 us -> 25.4 us  [chain_call(): pl.pallas_call(functools.partial(chain, n), out_shape=pltpu.VMEM((heads *...]
where the time goes in v5:
time: 26.4 us; the launch traced here: 26.2 us
  Pallas kernels  26.2 us (99%)
    pallas_call x1, Pallas kernels, chain_call(): pl.pallas_call(functools.partial(chain, n), out_shape=pltpu.VMEM((heads *...  25.4 us
    pallas_call x1, Pallas kernels, chain_call(): pl.pallas_call(store, out_shape=jax.ShapeDtypeStruct(out.shape, out.dtype...  0.82 us

profile of v5, /device:TPU:0, one launch (start us, length us, event | category | flops | bytes accessed | tf_op | source)
XLA Modules:
  0.0 26.2 jit_solution(17547176284623203694)
XLA Ops:
  0.0 25.4 %shard_map.91.o_vmem = bf16[2048,128]{1,0:T(8,128)(2,1)S(1)} custom-call(bf16[2048,128]{1,0:T(8,128)(2,1)} %bitcast.8, bf16[512,128]{1,0:T(8,128)(2,1)} %bitcast.9, bf16[512,128]{1,0:T(8,128)(2,1)} %bitcast.10, bf16[16,512,128]{2,1,0:T(8,128)(2,1)} %bitcast.6, bf16[16,512,128]{2,1,0:T(8,128)(2,1)} %bitcast.7, s32[2]{0:T(128)} %vp_hbm.1, s32[1,6]{1,0:T(1,128)} %vl_hbm.1, ...), custom_call_target="tpu_custom_call" | custom-call | tf_op jit(solution)/shard_map/pallas_call | solution.py:777
  25.4 0.8 %shard_map.92 = bf16[2048,128]{1,0:T(8,128)(2,1)} custom-call(bf16[2048,128]{1,0:T(8,128)(2,1)S(1)} %shard_map.91.o_vmem), custom_call_target="tpu_custom_call" | custom-call | tf_op jit(solution)/shard_map/pallas_call | solution.py:798

commit v6 on v5

--- a/solution.py
+++ b/solution.py
@@ -284,6 +284,8 @@
 NONE = (-1, -1)
 QUEST = (-2, 0)
 SLASH = (-3, 0)
+VALUES = (-4, 0)
+READY = (-5, 0)
 
 
 def plan(heads):
@@ -293,7 +295,7 @@
         ((2, 1), NONE, 0), (NONE, (0, 2), 0), (NONE, NONE, 0), (NONE, (1, 2), 0), ((2, 2), NONE, 0),
         ((2, 3), NONE, 0), (NONE, (2, 2), 0), (NONE, NONE, 0), (NONE, (3, 2), 0), ((3, 0), NONE, 0),
         ((3, 1), NONE, 0), (NONE, (0, 3), 0), (NONE, NONE, 0), (NONE, (1, 3), 0), ((3, 2), NONE, 16),
-        ((3, 3), NONE, 0), (NONE, (2, 3), 0), (NONE, NONE, 0), (NONE, (3, 3), 0), (NONE, NONE, 0)]
+        ((3, 3), NONE, 0), (NONE, (2, 3), 0), (VALUES, (3, 3), 0), (READY, NONE, 0)]
     one = [((0, 0), (0, 1), 0), ((2, 0), (1, 1), 0), ((0, 3), (2, 1), 0), (NONE, (0, 0), 0), ((2, 1), (0, 2), 0),
         ((0, 1), (3, 0), 4), (NONE, (3, 1), 0), (NONE, (1, 2), 0), ((2, 2), (1, 0), 0), ((0, 2), NONE, 8),
         ((2, 3), NONE, 0), (NONE, (2, 2), 0), (NONE, (2, 0), 0), (NONE, NONE, 0), ((3, 0), (3, 2), 0),
@@ -336,7 +338,7 @@
           vp_ref, vl_ref, sl_ref, cnt_ref,
           q_raw, nk_raw, nv_raw, ck_raw, cv_raw, q_ref, sort_kv, sort_q, ext,
           pool, acc, peak, total, mask, part_acc, part_stat, scores_a, scores_b, top_a, top_b, most,
-          send_sem, hop_recv, sib_recv, sl_sem, q_sem, part_sem, in_sem, table_sem, ready):
+          send_sem, hop_recv, sib_recv, sl_sem, q_sem, part_sem, in_sem, table_sem, end_sem, ready):
     z = lax.axis_index("ctx")
     s = lax.axis_index("sub")
     heads = pool.shape[1]
@@ -376,10 +378,11 @@
     def _():
         pl.semaphore_signal(ready, inc=1, device_id={"ctx": z - 1}, device_id_type=MESH)
 
-    def put_keys(raw, put):
-        ordered = jnp.dot(sort_kv[...], raw, preferred_element_type=jnp.float32).astype(jnp.bfloat16)
-        for h in range(heads):
-            put(h, ordered[h * BLK:(h + 1) * BLK])
+    def put_keys(raw, put, those=range(heads)):
+        ordered = jnp.dot(sort_kv[those.start * BLK:those.stop * BLK], raw,
+                          preferred_element_type=jnp.float32).astype(jnp.bfloat16)
+        for i, h in enumerate(those):
+            put(h, ordered[i * BLK:(i + 1) * BLK])
 
     def put_values(raw, put):
         ordered = lax.dot_general(raw, sort_kv[...], (((0,), (1,)), ((), ())),
@@ -417,6 +420,19 @@
             send_sem=send_sem.at[2], recv_sem=sib_recv.at[src - (src > z).astype(jnp.int32), h],
             device_id=sib_id, device_id_type=MESH)
 
+    def end_hop(kv):
+        return pltpu.make_async_remote_copy(
+            src_ref=pool.at[last, heads - 1, s, kv], dst_ref=pool.at[last, heads - 1, s, kv],
+            send_sem=send_sem.at[0], recv_sem=end_sem.at[0] if kv else hop_recv.at[last - 1, heads - 1],
+            device_id={"ctx": z - 1}, device_id_type=MESH)
+
+    def end_sib(kv, part):
+        block = pool.at[last, heads - 1, part, kv]
+        return pltpu.make_async_remote_copy(
+            src_ref=block, dst_ref=block,
+            send_sem=send_sem.at[2], recv_sem=end_sem.at[1] if kv else sib_recv.at[last - 1, heads - 1],
+            device_id=sib_id, device_id_type=MESH)
+
     def slash_hop(count):
         return pltpu.make_async_remote_copy(
             src_ref=pool.at[OWN, pl.ds(0, count), 0, s], dst_ref=pool.at[OWN, pl.ds(0, count), 1, s],
@@ -458,8 +474,9 @@
     for table in tables:
         table.wait()
     loads[0].wait()
-    put_keys(ck_raw[vp_ref[s]], put_pool(s, 0))
-    leftward((0, 0), (1, 0))
+    put_keys(ck_raw[vp_ref[s]], put_pool(s, 0), range(EARLY))
+    leftward(*[(h, 0) for h in range(EARLY)])
+    put_keys(ck_raw[vp_ref[s]], put_pool(s, 0), range(EARLY, heads))
     for load in loads[2:]:
         load.start()
     loads[1].wait()
@@ -643,14 +660,35 @@
         kind, message, code, block, flags = [look(field) for field in range(5)]
         src, h = message // 4, message % 4
 
-        @pl.when(kind == 1)
+        end = (src == last) & (h == heads - 1)
+
+        @pl.when((kind == 1) & end & (z == 0))
+        def _():
+            end_hop(0).wait_recv()
+            end_sib(0, s).start()
+
+        @pl.when(kind == 4)
+        def _():
+            end_hop(1).wait_recv()
+            end_sib(1, s).start()
+
+        @pl.when(kind == 5)
+        def _():
+            end_sib(1, 1 - s).wait_recv()
+
+        @pl.when((kind == 1) & jnp.logical_not(end & (z == 0)))
         def _():
             block = pool.at[src, h, s]
             pltpu.make_async_copy(block, block, hop_recv.at[src - (src > z).astype(jnp.int32), h]).wait()
 
-            @pl.when((src > z) & has_left)
+            @pl.when((src > z) & ((z > 1) | ((z == 1) & jnp.logical_not(end))))
             def _():
                 hop(src, h, False).start()
+
+            @pl.when((z == 1) & end)
+            def _():
+                end_hop(0).start()
+                end_hop(1).start()
 
             @pl.when((src < z) & ((z < last - 1) | ((z == last - 1) & (h < stay))))
             def _():
@@ -685,7 +723,13 @@
 
         unit = (code % 8, block // 4, block % 4)
 
-        @pl.when((code > 7) & (unit[1] < OWN))
+        late = (unit[1] == last) & (unit[2] == heads - 1) & (z == 0)
+
+        @pl.when((code > 7) & late)
+        def _():
+            end_sib(0, 1 - s).wait_recv()
+
+        @pl.when((code > 7) & (unit[1] < OWN) & jnp.logical_not(late))
         def _():
             sib(unit[1], unit[2], 1 - s).wait_recv()
 
@@ -790,7 +834,7 @@
             wide_vmem(2 * BLK, rows), wide_vmem(2 * BLK, rows), wide_vmem(1, rows), wide_vmem(1, rows),
             vmem(heads * rows, head_dim),
             dma((3,)), dma((n - 1, heads)), dma((n - 1, heads)), dma((4,)),
-            dma((2, GUESTS + 1)), dma((2, GUESTS, 2)), dma((5,)), dma((4,)), pltpu.SemaphoreType.REGULAR,
+            dma((2, GUESTS + 1)), dma((2, GUESTS, 2)), dma((5,)), dma((4,)), dma((2,)), pltpu.SemaphoreType.REGULAR,
         ],
         compiler_params=pltpu.CompilerParams(
             collective_id=0, has_side_effects=True, vmem_limit_bytes=60 * 2**20),

time: 26.4 us -> 26.6 us (level)
  Pallas kernels: 26.2 us -> 26.5 us
    pallas_call x1, Pallas kernels: 25.4 us -> 25.6 us  [chain_call(): pl.pallas_call(functools.partial(chain, n), out_shape=pltpu.VMEM((heads *...]
where the time goes in v6:
time: 26.6 us; the launch traced here: 26.5 us
  Pallas kernels  26.5 us (100%)
    pallas_call x1, Pallas kernels, chain_call(): pl.pallas_call(functools.partial(chain, n), out_shape=pltpu.VMEM((heads *...  25.6 us
    pallas_call x1, Pallas kernels, chain_call(): pl.pallas_call(store, out_shape=jax.ShapeDtypeStruct(out.shape, out.dtype...  0.82 us

profile of v6, /device:TPU:0, one launch (start us, length us, event | category | flops | bytes accessed | tf_op | source)
XLA Modules:
  0.0 26.5 jit_solution(6913112042556554617)
XLA Ops:
  0.0 25.6 %shard_map.91.o_vmem = bf16[2048,128]{1,0:T(8,128)(2,1)S(1)} custom-call(bf16[2048,128]{1,0:T(8,128)(2,1)} %bitcast.8, bf16[512,128]{1,0:T(8,128)(2,1)} %bitcast.9, bf16[512,128]{1,0:T(8,128)(2,1)} %bitcast.10, bf16[16,512,128]{2,1,0:T(8,128)(2,1)} %bitcast.6, bf16[16,512,128]{2,1,0:T(8,128)(2,1)} %bitcast.7, s32[2]{0:T(128)} %vp_hbm.1, s32[1,6]{1,0:T(1,128)} %vl_hbm.1, ...), custom_call_target="tpu_custom_call" | custom-call | tf_op jit(solution)/shard_map/pallas_call | solution.py:821
  25.7 0.8 %shard_map.92 = bf16[2048,128]{1,0:T(8,128)(2,1)} custom-call(bf16[2048,128]{1,0:T(8,128)(2,1)S(1)} %shard_map.91.o_vmem), custom_call_target="tpu_custom_call" | custom-call | tf_op jit(solution)/shard_map/pallas_call | solution.py:842

commit v7 on v5

--- a/solution.py
+++ b/solution.py
@@ -274,11 +274,11 @@
         slash_sib(s).wait_send()
 
 BITS = 5
-PACK = 6
 OWN, GUEST, ALONE = 4, 5, 6
 IDLE = (6, 4 * GUEST)
 GUESTS = 1
 EARLY = 2
+PACK = 6
 
 
 NONE = (-1, -1)
@@ -335,7 +335,7 @@
 def chain(n, q_hbm, nk_hbm, nv_hbm, ck_hbm, cv_hbm, vp_hbm, vl_hbm, sl_hbm, cnt_hbm, o_ref,
           vp_ref, vl_ref, sl_ref, cnt_ref,
           q_raw, nk_raw, nv_raw, ck_raw, cv_raw, q_ref, sort_kv, sort_q, ext,
-          pool, acc, peak, total, mask, part_acc, part_stat, scores_a, scores_b, top_a, top_b, most,
+          pool, acc, peak, total, mask, part_acc, part_stat, scores_a, scores_b, top_a, top_b, most, sort_o,
           send_sem, hop_recv, sib_recv, sl_sem, q_sem, part_sem, in_sem, table_sem, ready):
     z = lax.axis_index("ctx")
     s = lax.axis_index("sub")
@@ -366,6 +366,16 @@
     def _():
         pl.semaphore_signal(barrier, inc=1, device_id={"ctx": z + 1}, device_id_type=MESH)
 
+    def by_role(values):
+        out = jnp.int32(values[-1])
+        for i in reversed(range(len(values) - 1)):
+            out = jnp.where(z == i, jnp.int32(values[i]), out)
+        return out
+
+    roles = plan(heads)
+    lengths = [max(t for t, step in enumerate(role) if step[0] or step[4]) + 1 for role in roles]
+    steps = -(-max(lengths) // PACK) * PACK
+    roles = [(role + [(0, 0) + IDLE + (0,)] * steps)[:steps] for role in roles]
     ids = lax.broadcasted_iota(jnp.int32, (wide, wide), 0)
     at = lax.broadcasted_iota(jnp.int32, (wide, wide), 1)
     sort_kv[...] = jnp.where(at == (ids % BLK) * heads + ids // BLK, 1.0, 0.0).astype(jnp.bfloat16)
@@ -376,10 +386,11 @@
     def _():
         pl.semaphore_signal(ready, inc=1, device_id={"ctx": z - 1}, device_id_type=MESH)
 
-    def put_keys(raw, put):
-        ordered = jnp.dot(sort_kv[...], raw, preferred_element_type=jnp.float32).astype(jnp.bfloat16)
-        for h in range(heads):
-            put(h, ordered[h * BLK:(h + 1) * BLK])
+    def put_keys(raw, put, those=range(heads)):
+        ordered = jnp.dot(sort_kv[those.start * BLK:those.stop * BLK], raw,
+                          preferred_element_type=jnp.float32).astype(jnp.bfloat16)
+        for i, h in enumerate(those):
+            put(h, ordered[i * BLK:(i + 1) * BLK])
 
     def put_values(raw, put):
         ordered = lax.dot_general(raw, sort_kv[...], (((0,), (1,)), ((), ())),
@@ -458,8 +469,9 @@
     for table in tables:
         table.wait()
     loads[0].wait()
-    put_keys(ck_raw[vp_ref[s]], put_pool(s, 0))
-    leftward((0, 0), (1, 0))
+    put_keys(ck_raw[vp_ref[s]], put_pool(s, 0), range(EARLY))
+    leftward(*[(h, 0) for h in range(EARLY)])
+    put_keys(ck_raw[vp_ref[s]], put_pool(s, 0), range(EARLY, heads))
     for load in loads[2:]:
         load.start()
     loads[1].wait()
@@ -501,6 +513,11 @@
 
     token = (ids % BLK) // groups
     sort_q[...] = jnp.where(at == (token * heads + ids // BLK) * groups + ids % groups,
+                            1.0, 0.0).astype(jnp.bfloat16)
+    half = EARLY * BLK
+    ids = lax.broadcasted_iota(jnp.int32, (half, half), 0)
+    at = lax.broadcasted_iota(jnp.int32, (half, half), 1)
+    sort_o[...] = jnp.where(at == ((ids % BLK) // groups * EARLY + ids // BLK) * groups + ids % groups,
                             1.0, 0.0).astype(jnp.bfloat16)
     loads[4].wait()
     for part in range(rows // BLK):
@@ -594,8 +611,7 @@
         lanes = slice(part * BLK, (part + 1) * BLK)
         done = jnp.concatenate(
             [(acc[h, :, lanes] * (1.0 / total[h, :, lanes])).astype(jnp.bfloat16) for h in those], 1)
-        return lax.dot_general(sort_q[those.start * BLK:those.stop * BLK], done, (((0,), (1,)), ((), ())),
-                               preferred_element_type=jnp.float32)
+        return lax.dot_general(sort_o[...], done, (((0,), (1,)), ((), ())), preferred_element_type=jnp.float32)
 
     def drain():
         def sent(kind, sources, count):
@@ -619,28 +635,11 @@
                     for g in range(GUESTS):
                         guest_q(g).wait_send()
 
-    roles = plan(heads)
-    steps = max(len(role) for role in roles)
-    steps += steps % 2
-    roles = [role + [(0, 0) + IDLE + (0,)] * (steps - len(role)) for role in roles]
-
-    def by_role(values):
-        out = jnp.int32(values[-1])
-        for i in reversed(range(len(values) - 1)):
-            out = jnp.where(z == i, jnp.int32(values[i]), out)
-        return out
-
     words = [[by_role([sum(step[field] << (BITS * i) for i, step in enumerate(role[start:start + PACK]))
                        for role in roles]) for start in range(0, steps, PACK)] for field in range(5)]
 
-    def step(t, before, bufs, old_bufs):
-        def look(field):
-            word = words[field][-1]
-            for i in reversed(range(len(words[field]) - 1)):
-                word = jnp.where(t // PACK == i, words[field][i], word)
-            return lax.shift_right_logical(word, BITS * (t % PACK)) & (2 ** BITS - 1)
-
-        kind, message, code, block, flags = [look(field) for field in range(5)]
+    def step(here, t, before, bufs, old_bufs):
+        kind, message, code, block, flags = [(word >> (BITS * t)) & (2 ** BITS - 1) for word in here]
         src, h = message // 4, message % 4
 
         @pl.when(kind == 1)
@@ -658,73 +657,90 @@
 
             sib(src, h, s).start()
 
-        @pl.when((flags // 4) % 2 == 1)
-        def _():
-            for kv in range(2):
-                first_hop(2, kv, True).start()
-
-        @pl.when((flags // 8) % 2 == 1)
-        def _():
-            slash_hop(heads).start()
-
-        @pl.when(kind == 2)
-        def _():
-            guest_mask().wait_recv()
-            for g in range(GUESTS):
-                guest_q(g).wait_recv()
-
-        @pl.when((kind == 3) & has_right)
-        def _():
-            slash_hop(heads).wait_recv()
-            slash_sib(heads, s).start()
-
-        @pl.when((kind == 3) & (z == last))
-        def _():
-            slash_hop(stay).wait_recv()
-            slash_sib(stay, s).start()
+        @pl.when(kind > 1)
+        def _():
+            @pl.when(kind == 2)
+            def _():
+                guest_mask().wait_recv()
+                for g in range(GUESTS):
+                    guest_q(g).wait_recv()
+
+            @pl.when((kind == 3) & has_right)
+            def _():
+                slash_hop(heads).wait_recv()
+                slash_sib(heads, s).start()
+
+            @pl.when((kind == 3) & (z == last))
+            def _():
+                slash_hop(stay).wait_recv()
+                slash_sib(stay, s).start()
 
         unit = (code % 8, block // 4, block % 4)
 
-        @pl.when((code > 7) & (unit[1] < OWN))
-        def _():
-            sib(unit[1], unit[2], 1 - s).wait_recv()
-
-        @pl.when((code > 7) & (unit[1] == OWN) & has_right)
-        def _():
-            slash_sib(heads, 1 - s).wait_recv()
-
-        @pl.when((code > 7) & (unit[1] == OWN) & (z == last))
-        def _():
-            slash_sib(stay, 1 - s).wait_recv()
+        @pl.when(code > 7)
+        def _():
+            @pl.when(unit[1] < OWN)
+            def _():
+                sib(unit[1], unit[2], 1 - s).wait_recv()
+
+            @pl.when((unit[1] == OWN) & has_right)
+            def _():
+                slash_sib(heads, 1 - s).wait_recv()
+
+            @pl.when((unit[1] == OWN) & (z == last))
+            def _():
+                slash_sib(stay, 1 - s).wait_recv()
 
         @pl.when(flags % 2 == 1)
         def _():
             ahead(unit, *bufs)
             behind(before, *old_bufs)
 
-        @pl.when(flags // 16 == 1)
-        def _():
-            for part in range(rows // BLK):
-                most[part * wide:(part + 1) * wide] = ordered(part, range(EARLY)).astype(o_ref.dtype)
-
-        @pl.when((flags // 2) % 2 == 1)
-        def _():
-            g = 0
-            part_acc[g] = acc[heads + g].astype(jnp.bfloat16)
-            part_stat[g, 0:1] = peak[heads + g]
-            part_stat[g, 1:2] = total[heads + g]
-            for copy in guest_part(g):
-                copy.start()
+        @pl.when(flags > 1)
+        def _():
+            @pl.when((flags // 4) % 2 == 1)
+            def _():
+                for kv in range(2):
+                    first_hop(2, kv, True).start()
+
+            @pl.when((flags // 8) % 2 == 1)
+            def _():
+                slash_hop(heads).start()
+
+            @pl.when((flags // 2) % 2 == 1)
+            def _():
+                g = 0
+                part_acc[g] = acc[heads + g].astype(jnp.bfloat16)
+                part_stat[g, 0:1] = peak[heads + g]
+                part_stat[g, 1:2] = total[heads + g]
+                for copy in guest_part(g):
+                    copy.start()
+
+            @pl.when(flags // 16 == 1)
+            def _():
+                for part in range(rows // BLK):
+                    most[part] = ordered(part, range(EARLY))
 
         return unit
 
-    def two_steps(i, before):
-        mid = step(2 * i, before, (scores_a, top_a), (scores_b, top_b))
-        return step(2 * i + 1, mid, (scores_b, top_b), (scores_a, top_a))
-
-    lengths = [max(t for t, step in enumerate(role) if step[0] or step[4]) + 1 for role in roles]
+    pairs = by_role([(length + 1) // 2 for length in lengths])
+
+    def some_steps(group, before):
+        here = []
+        for chunks in words:
+            word = chunks[-1]
+            for i in reversed(range(len(chunks) - 1)):
+                word = jnp.where(group == i, chunks[i], word)
+            here.append(word)
+
+        def two_steps(i, before):
+            mid = step(here, 2 * i, before, (scores_a, top_a), (scores_b, top_b))
+            return step(here, 2 * i + 1, mid, (scores_b, top_b), (scores_a, top_a))
+
+        return lax.fori_loop(0, jnp.minimum(PACK // 2, pairs - group * (PACK // 2)), two_steps, before)
+
     idle = (jnp.int32(IDLE[0]), jnp.int32(GUEST), jnp.int32(0))
-    lax.fori_loop(0, by_role([(length + 1) // 2 for length in lengths]), two_steps, idle)
+    lax.fori_loop(0, by_role([-(-length // PACK) for length in lengths]), some_steps, idle)
 
     drain()
 
@@ -740,9 +756,10 @@
             acc[slot] = acc[slot] * mine + part_acc[g].astype(jnp.float32) * theirs
             total[slot] = total[slot] * mine + part_stat[g, 1:2] * theirs
 
+    tile = EARLY * groups
     for part in range(rows // BLK):
-        lines = slice(part * wide, (part + 1) * wide)
-        o_ref[lines] = most[lines] + ordered(part, range(EARLY, heads)).astype(o_ref.dtype)
+        pair = [half.reshape(-1, tile, head_dim) for half in (most[part], ordered(part, range(EARLY, heads)))]
+        o_ref[part * wide:(part + 1) * wide] = jnp.concatenate(pair, 1).reshape(wide, head_dim).astype(o_ref.dtype)
 
     @pl.when(z == last - 1)
     def _():
@@ -788,7 +805,7 @@
             wide_vmem(slots, head_dim, rows), wide_vmem(slots, 1, rows), wide_vmem(slots, 1, rows),
             wide_vmem(2, 16, BLK), vmem(GUESTS, head_dim, rows), wide_vmem(GUESTS, 8, rows),
             wide_vmem(2 * BLK, rows), wide_vmem(2 * BLK, rows), wide_vmem(1, rows), wide_vmem(1, rows),
-            vmem(heads * rows, head_dim),
+            wide_vmem(rows // BLK, EARLY * BLK, head_dim), vmem(EARLY * BLK, EARLY * BLK),
             dma((3,)), dma((n - 1, heads)), dma((n - 1, heads)), dma((4,)),
             dma((2, GUESTS + 1)), dma((2, GUESTS, 2)), dma((5,)), dma((4,)), pltpu.SemaphoreType.REGULAR,
         ],

time: 26.4 us -> 25.7 us (0.973)
  Pallas kernels: 26.2 us -> 25.5 us
    pallas_call x1, Pallas kernels: 25.4 us -> 24.7 us  [chain_call(): pl.pallas_call(functools.partial(chain, n), out_shape=pltpu.VMEM((heads *...]
where the time goes in v7:
time: 25.7 us; the launch traced here: 25.5 us
  Pallas kernels  25.5 us (99%)
    pallas_call x1, Pallas kernels, chain_call(): pl.pallas_call(functools.partial(chain, n), out_shape=pltpu.VMEM((heads *...  24.7 us
    pallas_call x1, Pallas kernels, chain_call(): pl.pallas_call(store, out_shape=jax.ShapeDtypeStruct(out.shape, out.dtype...  0.82 us

profile of v7, /device:TPU:0, one launch (start us, length us, event | category | flops | bytes accessed | tf_op | source)
XLA Modules:
  0.0 25.5 jit_solution(14455595997737364457)
XLA Ops:
  0.0 24.7 %shard_map.91.o_vmem = bf16[2048,128]{1,0:T(8,128)(2,1)S(1)} custom-call(bf16[2048,128]{1,0:T(8,128)(2,1)} %bitcast.8, bf16[512,128]{1,0:T(8,128)(2,1)} %bitcast.9, bf16[512,128]{1,0:T(8,128)(2,1)} %bitcast.10, bf16[16,512,128]{2,1,0:T(8,128)(2,1)} %bitcast.6, bf16[16,512,128]{2,1,0:T(8,128)(2,1)} %bitcast.7, s32[2]{0:T(128)} %vp_hbm.1, s32[1,6]{1,0:T(1,128)} %vl_hbm.1, ...), custom_call_target="tpu_custom_call" | custom-call | tf_op jit(solution)/shard_map/pallas_call | solution.py:794
  24.7 0.8 %shard_map.92 = bf16[2048,128]{1,0:T(8,128)(2,1)} custom-call(bf16[2048,128]{1,0:T(8,128)(2,1)S(1)} %shard_map.91.o_vmem), custom_call_target="tpu_custom_call" | custom-call | tf_op jit(solution)/shard_map/pallas_call | solution.py:815

commit v8 on v7

--- a/solution.py
+++ b/solution.py
@@ -293,7 +293,7 @@
         ((2, 1), NONE, 0), (NONE, (0, 2), 0), (NONE, NONE, 0), (NONE, (1, 2), 0), ((2, 2), NONE, 0),
         ((2, 3), NONE, 0), (NONE, (2, 2), 0), (NONE, NONE, 0), (NONE, (3, 2), 0), ((3, 0), NONE, 0),
         ((3, 1), NONE, 0), (NONE, (0, 3), 0), (NONE, NONE, 0), (NONE, (1, 3), 0), ((3, 2), NONE, 16),
-        ((3, 3), NONE, 0), (NONE, (2, 3), 0), (NONE, NONE, 0), (NONE, (3, 3), 0), (NONE, NONE, 0)]
+        ((3, 3), NONE, 0), (NONE, (2, 3), 0)]
     one = [((0, 0), (0, 1), 0), ((2, 0), (1, 1), 0), ((0, 3), (2, 1), 0), (NONE, (0, 0), 0), ((2, 1), (0, 2), 0),
         ((0, 1), (3, 0), 4), (NONE, (3, 1), 0), (NONE, (1, 2), 0), ((2, 2), (1, 0), 0), ((0, 2), NONE, 8),
         ((2, 3), NONE, 0), (NONE, (2, 2), 0), (NONE, (2, 0), 0), (NONE, NONE, 0), ((3, 0), (3, 2), 0),
@@ -743,6 +743,13 @@
     lax.fori_loop(0, by_role([-(-length // PACK) for length in lengths]), some_steps, idle)
 
     drain()
+
+    @pl.when(z == 0)
+    def _():
+        unit = (heads - 1, last, heads - 1)
+        sib(*unit[1:], 1 - s).wait_recv()
+        ahead(unit, scores_a, top_a)
+        behind(unit, scores_a, top_a)
 
     @pl.when(z == last)
     def _():

time: 25.7 us -> 25.6 us (level)
  no operation moved by 1% of the time
where the time goes in v8:
time: 25.6 us; the launch traced here: 25.4 us
  Pallas kernels  25.4 us (99%)
    pallas_call x1, Pallas kernels, chain_call(): pl.pallas_call(functools.partial(chain, n), out_shape=pltpu.VMEM((heads *...  24.6 us
    pallas_call x1, Pallas kernels, chain_call(): pl.pallas_call(store, out_shape=jax.ShapeDtypeStruct(out.shape, out.dtype...  0.82 us

profile of v8, /device:TPU:0, one launch (start us, length us, event | category | flops | bytes accessed | tf_op | source)
XLA Modules:
  0.0 25.4 jit_solution(15864638522553512587)
XLA Ops:
  0.0 24.6 %shard_map.91.o_vmem = bf16[2048,128]{1,0:T(8,128)(2,1)S(1)} custom-call(bf16[2048,128]{1,0:T(8,128)(2,1)} %bitcast.8, bf16[512,128]{1,0:T(8,128)(2,1)} %bitcast.9, bf16[512,128]{1,0:T(8,128)(2,1)} %bitcast.10, bf16[16,512,128]{2,1,0:T(8,128)(2,1)} %bitcast.6, bf16[16,512,128]{2,1,0:T(8,128)(2,1)} %bitcast.7, s32[2]{0:T(128)} %vp_hbm.1, s32[1,6]{1,0:T(1,128)} %vl_hbm.1, ...), custom_call_target="tpu_custom_call" | custom-call | tf_op jit(solution)/shard_map/pallas_call | solution.py:801
  24.6 0.8 %shard_map.92 = bf16[2048,128]{1,0:T(8,128)(2,1)} custom-call(bf16[2048,128]{1,0:T(8,128)(2,1)S(1)} %shard_map.91.o_vmem), custom_call_target="tpu_custom_call" | custom-call | tf_op jit(solution)/shard_map/pallas_call | solution.py:822

commit v9 on v8

--- a/solution.py
+++ b/solution.py
@@ -292,8 +292,7 @@
         (NONE, NONE, 0), ((1, 3), NONE, 0), (NONE, (2, 1), 0), (NONE, NONE, 0), (NONE, (3, 1), 0), ((2, 0), NONE, 0),
         ((2, 1), NONE, 0), (NONE, (0, 2), 0), (NONE, NONE, 0), (NONE, (1, 2), 0), ((2, 2), NONE, 0),
         ((2, 3), NONE, 0), (NONE, (2, 2), 0), (NONE, NONE, 0), (NONE, (3, 2), 0), ((3, 0), NONE, 0),
-        ((3, 1), NONE, 0), (NONE, (0, 3), 0), (NONE, NONE, 0), (NONE, (1, 3), 0), ((3, 2), NONE, 16),
-        ((3, 3), NONE, 0), (NONE, (2, 3), 0)]
+        ((3, 1), NONE, 0), (NONE, (0, 3), 0), (NONE, NONE, 0), (NONE, (1, 3), 0), ((3, 2), NONE, 16)]
     one = [((0, 0), (0, 1), 0), ((2, 0), (1, 1), 0), ((0, 3), (2, 1), 0), (NONE, (0, 0), 0), ((2, 1), (0, 2), 0),
         ((0, 1), (3, 0), 4), (NONE, (3, 1), 0), (NONE, (1, 2), 0), ((2, 2), (1, 0), 0), ((0, 2), NONE, 8),
         ((2, 3), NONE, 0), (NONE, (2, 2), 0), (NONE, (2, 0), 0), (NONE, NONE, 0), ((3, 0), (3, 2), 0),
@@ -336,7 +335,7 @@
           vp_ref, vl_ref, sl_ref, cnt_ref,
           q_raw, nk_raw, nv_raw, ck_raw, cv_raw, q_ref, sort_kv, sort_q, ext,
           pool, acc, peak, total, mask, part_acc, part_stat, scores_a, scores_b, top_a, top_b, most, sort_o,
-          send_sem, hop_recv, sib_recv, sl_sem, q_sem, part_sem, in_sem, table_sem, ready):
+          send_sem, hop_recv, sib_recv, sl_sem, q_sem, part_sem, in_sem, table_sem, end_sem, ready):
     z = lax.axis_index("ctx")
     s = lax.axis_index("sub")
     heads = pool.shape[1]
@@ -428,6 +427,27 @@
             send_sem=send_sem.at[2], recv_sem=sib_recv.at[src - (src > z).astype(jnp.int32), h],
             device_id=sib_id, device_id_type=MESH)
 
+    end = heads - 1
+
+    def end_hop(kv):
+        block = pool.at[last, end, s, kv]
+        return pltpu.make_async_remote_copy(
+            src_ref=block, dst_ref=block,
+            send_sem=send_sem.at[0], recv_sem=end_sem.at[0] if kv else hop_recv.at[last - 1, end],
+            device_id={"ctx": z - 1}, device_id_type=MESH)
+
+    def end_across():
+        block = pool.at[last, end, s, 1]
+        return pltpu.make_async_remote_copy(
+            src_ref=block, dst_ref=block, send_sem=end_sem.at[2], recv_sem=end_sem.at[1],
+            device_id={"ctx": z - 1, "sub": 1 - s}, device_id_type=MESH)
+
+    def end_sib(part):
+        block = pool.at[last, end, part, 0]
+        return pltpu.make_async_remote_copy(
+            src_ref=block, dst_ref=block, send_sem=end_sem.at[3], recv_sem=sib_recv.at[last - 1, end],
+            device_id=sib_id, device_id_type=MESH)
+
     def slash_hop(count):
         return pltpu.make_async_remote_copy(
             src_ref=pool.at[OWN, pl.ds(0, count), 0, s], dst_ref=pool.at[OWN, pl.ds(0, count), 1, s],
@@ -629,7 +649,13 @@
                 if index > 0:
                     sent(0, n - index, heads)
                     slash_sib(heads if index < last else stay, s).wait_send()
-                sent(2, n - 1, heads if index < last else stay)
+                if index > 0:
+                    sent(2, n - 1, heads if index < last else stay)
+                else:
+                    copied = q_ref.at[pl.ds(0, heads), pl.ds(0, ((n - 1) * heads - 1) * (2 * BLK * head_dim // rows) // heads)]
+                    pltpu.make_async_copy(copied, copied, send_sem.at[2]).wait()
+                if index == 1:
+                    end_across().wait_send()
                 if index == last:
                     guest_mask().wait_send()
                     for g in range(GUESTS):
@@ -647,9 +673,17 @@
             block = pool.at[src, h, s]
             pltpu.make_async_copy(block, block, hop_recv.at[src - (src > z).astype(jnp.int32), h]).wait()
 
-            @pl.when((src > z) & has_left)
+            split = (z == 1) & (message == last * 4 + end)
+
+            @pl.when((src > z) & has_left & jnp.logical_not(split))
             def _():
                 hop(src, h, False).start()
+
+            @pl.when(split)
+            def _():
+                end_hop(0).start()
+                end_hop(1).start()
+                end_across().start()
 
             @pl.when((src < z) & ((z < last - 1) | ((z == last - 1) & (h < stay))))
             def _():
@@ -746,10 +780,19 @@
 
     @pl.when(z == 0)
     def _():
-        unit = (heads - 1, last, heads - 1)
-        sib(*unit[1:], 1 - s).wait_recv()
+        end_hop(0).wait_recv()
+        end_sib(s).start()
+        sib(last, end - 1, 1 - s).wait_recv()
+        unit = (end - 1, last, end - 1)
         ahead(unit, scores_a, top_a)
         behind(unit, scores_a, top_a)
+        end_sib(1 - s).wait_recv()
+        unit = (end, last, end)
+        ahead(unit, scores_b, top_b)
+        end_hop(1).wait_recv()
+        block = pool.at[last, end, 1 - s, 1]
+        pltpu.make_async_copy(block, block, end_sem.at[1]).wait()
+        behind(unit, scores_b, top_b)
 
     @pl.when(z == last)
     def _():
@@ -767,6 +810,10 @@
     for part in range(rows // BLK):
         pair = [half.reshape(-1, tile, head_dim) for half in (most[part], ordered(part, range(EARLY, heads)))]
         o_ref[part * wide:(part + 1) * wide] = jnp.concatenate(pair, 1).reshape(wide, head_dim).astype(o_ref.dtype)
+
+    @pl.when(z == 0)
+    def _():
+        end_sib(s).wait_send()
 
     @pl.when(z == last - 1)
     def _():
@@ -814,7 +861,7 @@
             wide_vmem(2 * BLK, rows), wide_vmem(2 * BLK, rows), wide_vmem(1, rows), wide_vmem(1, rows),
             wide_vmem(rows // BLK, EARLY * BLK, head_dim), vmem(EARLY * BLK, EARLY * BLK),
             dma((3,)), dma((n - 1, heads)), dma((n - 1, heads)), dma((4,)),
-            dma((2, GUESTS + 1)), dma((2, GUESTS, 2)), dma((5,)), dma((4,)), pltpu.SemaphoreType.REGULAR,
+            dma((2, GUESTS + 1)), dma((2, GUESTS, 2)), dma((5,)), dma((4,)), dma((4,)), pltpu.SemaphoreType.REGULAR,
         ],
         compiler_params=pltpu.CompilerParams(
             collective_id=0, has_side_effects=True, vmem_limit_bytes=60 * 2**20),

time: 25.6 us -> 25.6 us (level)
  no operation moved by 1% of the time
where the time goes in v9:
time: 25.6 us; the launch traced here: 25.4 us
  Pallas kernels  25.4 us (99%)
    pallas_call x1, Pallas kernels, chain_call(): pl.pallas_call(functools.partial(chain, n), out_shape=pltpu.VMEM((heads *...  24.6 us
    pallas_call x1, Pallas kernels, chain_call(): pl.pallas_call(store, out_shape=jax.ShapeDtypeStruct(out.shape, out.dtype...  0.82 us

profile of v9, /device:TPU:0, one launch (start us, length us, event | category | flops | bytes accessed | tf_op | source)
XLA Modules:
  0.0 25.4 jit_solution(7240291836098270042)
XLA Ops:
  0.0 24.6 %shard_map.91.o_vmem = bf16[2048,128]{1,0:T(8,128)(2,1)S(1)} custom-call(bf16[2048,128]{1,0:T(8,128)(2,1)} %bitcast.8, bf16[512,128]{1,0:T(8,128)(2,1)} %bitcast.9, bf16[512,128]{1,0:T(8,128)(2,1)} %bitcast.10, bf16[16,512,128]{2,1,0:T(8,128)(2,1)} %bitcast.6, bf16[16,512,128]{2,1,0:T(8,128)(2,1)} %bitcast.7, s32[2]{0:T(128)} %vp_hbm.1, s32[1,6]{1,0:T(1,128)} %vl_hbm.1, ...), custom_call_target="tpu_custom_call" | custom-call | tf_op jit(solution)/shard_map/pallas_call | solution.py:848
  24.6 0.8 %shard_map.92 = bf16[2048,128]{1,0:T(8,128)(2,1)} custom-call(bf16[2048,128]{1,0:T(8,128)(2,1)S(1)} %shard_map.91.o_vmem), custom_call_target="tpu_custom_call" | custom-call | tf_op jit(solution)/shard_map/pallas_call | solution.py:869

commit v10 on v9

--- a/solution.py
+++ b/solution.py
@@ -335,7 +335,7 @@
           vp_ref, vl_ref, sl_ref, cnt_ref,
           q_raw, nk_raw, nv_raw, ck_raw, cv_raw, q_ref, sort_kv, sort_q, ext,
           pool, acc, peak, total, mask, part_acc, part_stat, scores_a, scores_b, top_a, top_b, most, sort_o,
-          send_sem, hop_recv, sib_recv, sl_sem, q_sem, part_sem, in_sem, table_sem, end_sem, ready):
+          send_sem, hop_recv, sib_recv, sl_sem, ends_sem, in_sem, ready):
     z = lax.axis_index("ctx")
     s = lax.axis_index("sub")
     heads = pool.shape[1]
@@ -346,7 +346,7 @@
     stay = heads - GUESTS
     loads = [pltpu.make_async_copy(src, dst, in_sem.at[i]) for i, (src, dst) in enumerate(
         [(ck_hbm, ck_raw), (cv_hbm, cv_raw), (nk_hbm, nk_raw), (nv_hbm, nv_raw), (q_hbm, q_raw)])]
-    tables = [pltpu.make_async_copy(src, dst, table_sem.at[i]) for i, (src, dst) in enumerate(
+    tables = [pltpu.make_async_copy(src, dst, in_sem.at[2 + i]) for i, (src, dst) in enumerate(
         [(vp_hbm, vp_ref), (vl_hbm, vl_ref), (sl_hbm, sl_ref), (cnt_hbm, cnt_ref)])]
     loads[0].start()
     loads[1].start()
@@ -433,19 +433,19 @@
         block = pool.at[last, end, s, kv]
         return pltpu.make_async_remote_copy(
             src_ref=block, dst_ref=block,
-            send_sem=send_sem.at[0], recv_sem=end_sem.at[0] if kv else hop_recv.at[last - 1, end],
+            send_sem=send_sem.at[0], recv_sem=ends_sem.at[1, 0] if kv else hop_recv.at[last - 1, end],
             device_id={"ctx": z - 1}, device_id_type=MESH)
 
     def end_across():
         block = pool.at[last, end, s, 1]
         return pltpu.make_async_remote_copy(
-            src_ref=block, dst_ref=block, send_sem=end_sem.at[2], recv_sem=end_sem.at[1],
+            src_ref=block, dst_ref=block, send_sem=ends_sem.at[0, 0], recv_sem=ends_sem.at[1, 1],
             device_id={"ctx": z - 1, "sub": 1 - s}, device_id_type=MESH)
 
     def end_sib(part):
         block = pool.at[last, end, part, 0]
         return pltpu.make_async_remote_copy(
-            src_ref=block, dst_ref=block, send_sem=end_sem.at[3], recv_sem=sib_recv.at[last - 1, end],
+            src_ref=block, dst_ref=block, send_sem=ends_sem.at[0, 1], recv_sem=sib_recv.at[last - 1, end],
             device_id=sib_id, device_id_type=MESH)
 
     def slash_hop(count):
@@ -464,19 +464,19 @@
     def guest_q(g):
         return pltpu.make_async_remote_copy(
             src_ref=q_ref.at[stay + g, pl.ds(0, head_dim)], dst_ref=q_ref.at[heads + g, pl.ds(0, head_dim)],
-            send_sem=q_sem.at[0, g], recv_sem=q_sem.at[1, g],
+            send_sem=ends_sem.at[0, g], recv_sem=ends_sem.at[1, g],
             device_id={"ctx": z - 1}, device_id_type=MESH)
 
     def guest_mask():
         return pltpu.make_async_remote_copy(
             src_ref=mask.at[0], dst_ref=mask.at[1],
-            send_sem=q_sem.at[0, GUESTS], recv_sem=q_sem.at[1, GUESTS],
+            send_sem=ends_sem.at[0, GUESTS], recv_sem=ends_sem.at[1, GUESTS],
             device_id={"ctx": z - 1}, device_id_type=MESH)
 
     def guest_part(g):
         return [pltpu.make_async_remote_copy(
             src_ref=ref.at[g], dst_ref=ref.at[g],
-            send_sem=part_sem.at[0, g, i], recv_sem=part_sem.at[1, g, i],
+            send_sem=ends_sem.at[0, 2 * g + i], recv_sem=ends_sem.at[1, 2 * g + i],
             device_id={"ctx": z + 1}, device_id_type=MESH)
             for i, ref in enumerate((part_acc, part_stat))]
 
@@ -791,7 +791,7 @@
         ahead(unit, scores_b, top_b)
         end_hop(1).wait_recv()
         block = pool.at[last, end, 1 - s, 1]
-        pltpu.make_async_copy(block, block, end_sem.at[1]).wait()
+        pltpu.make_async_copy(block, block, ends_sem.at[1, 1]).wait()
         behind(unit, scores_b, top_b)
 
     @pl.when(z == last)
@@ -861,7 +861,7 @@
             wide_vmem(2 * BLK, rows), wide_vmem(2 * BLK, rows), wide_vmem(1, rows), wide_vmem(1, rows),
             wide_vmem(rows // BLK, EARLY * BLK, head_dim), vmem(EARLY * BLK, EARLY * BLK),
             dma((3,)), dma((n - 1, heads)), dma((n - 1, heads)), dma((4,)),
-            dma((2, GUESTS + 1)), dma((2, GUESTS, 2)), dma((5,)), dma((4,)), dma((4,)), pltpu.SemaphoreType.REGULAR,
+            dma((2, 2 * GUESTS)), dma((6,)), pltpu.SemaphoreType.REGULAR,
         ],
         compiler_params=pltpu.CompilerParams(
             collective_id=0, has_side_effects=True, vmem_limit_bytes=60 * 2**20),

time: 25.6 us -> 25.4 us (level)
  no operation moved by 1% of the time
where the time goes in v10:
time: 25.4 us; the launch traced here: 25.3 us
  Pallas kernels  25.3 us (100%)
    pallas_call x1, Pallas kernels, chain_call(): pl.pallas_call(functools.partial(chain, n), out_shape=pltpu.VMEM((heads *...  24.5 us
    pallas_call x1, Pallas kernels, chain_call(): pl.pallas_call(store, out_shape=jax.ShapeDtypeStruct(out.shape, out.dtype...  0.82 us

profile of v10, /device:TPU:0, one launch (start us, length us, event | category | flops | bytes accessed | tf_op | source)
XLA Modules:
  0.0 25.3 jit_solution(14002708471206467650)
XLA Ops:
  0.0 24.5 %shard_map.91.o_vmem = bf16[2048,128]{1,0:T(8,128)(2,1)S(1)} custom-call(bf16[2048,128]{1,0:T(8,128)(2,1)} %bitcast.8, bf16[512,128]{1,0:T(8,128)(2,1)} %bitcast.9, bf16[512,128]{1,0:T(8,128)(2,1)} %bitcast.10, bf16[16,512,128]{2,1,0:T(8,128)(2,1)} %bitcast.6, bf16[16,512,128]{2,1,0:T(8,128)(2,1)} %bitcast.7, s32[2]{0:T(128)} %vp_hbm.1, s32[1,6]{1,0:T(1,128)} %vl_hbm.1, ...), custom_call_target="tpu_custom_call" | custom-call | tf_op jit(solution)/shard_map/pallas_call | solution.py:848
  24.5 0.8 %shard_map.92 = bf16[2048,128]{1,0:T(8,128)(2,1)} custom-call(bf16[2048,128]{1,0:T(8,128)(2,1)S(1)} %shard_map.91.o_vmem), custom_call_target="tpu_custom_call" | custom-call | tf_op jit(solution)/shard_map/pallas_call | solution.py:869

commit v11 on v10

--- a/solution.py
+++ b/solution.py
@@ -292,7 +292,7 @@
         (NONE, NONE, 0), ((1, 3), NONE, 0), (NONE, (2, 1), 0), (NONE, NONE, 0), (NONE, (3, 1), 0), ((2, 0), NONE, 0),
         ((2, 1), NONE, 0), (NONE, (0, 2), 0), (NONE, NONE, 0), (NONE, (1, 2), 0), ((2, 2), NONE, 0),
         ((2, 3), NONE, 0), (NONE, (2, 2), 0), (NONE, NONE, 0), (NONE, (3, 2), 0), ((3, 0), NONE, 0),
-        ((3, 1), NONE, 0), (NONE, (0, 3), 0), (NONE, NONE, 0), (NONE, (1, 3), 0), ((3, 2), NONE, 16)]
+        ((3, 1), NONE, 0), (NONE, (0, 3), 0), (NONE, NONE, 0), (NONE, (1, 3), 0), ((3, 2), NONE, 0)]
     one = [((0, 0), (0, 1), 0), ((2, 0), (1, 1), 0), ((0, 3), (2, 1), 0), (NONE, (0, 0), 0), ((2, 1), (0, 2), 0),
         ((0, 1), (3, 0), 4), (NONE, (3, 1), 0), (NONE, (1, 2), 0), ((2, 2), (1, 0), 0), ((0, 2), NONE, 8),
         ((2, 3), NONE, 0), (NONE, (2, 2), 0), (NONE, (2, 0), 0), (NONE, NONE, 0), ((3, 0), (3, 2), 0),
@@ -633,33 +633,32 @@
             [(acc[h, :, lanes] * (1.0 / total[h, :, lanes])).astype(jnp.bfloat16) for h in those], 1)
         return lax.dot_general(sort_o[...], done, (((0,), (1,)), ((), ())), preferred_element_type=jnp.float32)
 
-    def drain():
+    def early_output():
+        for part in range(rows // BLK):
+            most[part] = ordered(part, range(EARLY))
+
+    def drain(index):
         def sent(kind, sources, count):
             blocks = pool.at[pl.ds(0, sources), pl.ds(0, count), s]
             pltpu.make_async_copy(blocks, blocks, send_sem.at[kind]).wait()
 
-        for index in range(n):
-            right = heads if index < last - 1 else stay if index < last else 0
-
-            @pl.when(z == index)
-            def _():
-                if right:
-                    sent(1, index + 1, right)
-                    slash_hop(right).wait_send()
-                if index > 0:
-                    sent(0, n - index, heads)
-                    slash_sib(heads if index < last else stay, s).wait_send()
-                if index > 0:
-                    sent(2, n - 1, heads if index < last else stay)
-                else:
-                    copied = q_ref.at[pl.ds(0, heads), pl.ds(0, ((n - 1) * heads - 1) * (2 * BLK * head_dim // rows) // heads)]
-                    pltpu.make_async_copy(copied, copied, send_sem.at[2]).wait()
-                if index == 1:
-                    end_across().wait_send()
-                if index == last:
-                    guest_mask().wait_send()
-                    for g in range(GUESTS):
-                        guest_q(g).wait_send()
+        right = heads if index < last - 1 else stay if index < last else 0
+        if right:
+            sent(1, index + 1, right)
+            slash_hop(right).wait_send()
+        if index > 0:
+            sent(0, n - index, heads)
+            slash_sib(heads if index < last else stay, s).wait_send()
+            sent(2, n - 1, heads if index < last else stay)
+        else:
+            copied = q_ref.at[pl.ds(0, heads), pl.ds(0, ((n - 1) * heads - 1) * (2 * BLK * head_dim // rows) // heads)]
+            pltpu.make_async_copy(copied, copied, send_sem.at[2]).wait()
+        if index == 1:
+            end_across().wait_send()
+        if index == last:
+            guest_mask().wait_send()
+            for g in range(GUESTS):
+                guest_q(g).wait_send()
 
     words = [[by_role([sum(step[field] << (BITS * i) for i, step in enumerate(role[start:start + PACK]))
                        for role in roles]) for start in range(0, steps, PACK)] for field in range(5)]
@@ -752,8 +751,7 @@
 
             @pl.when(flags // 16 == 1)
             def _():
-                for part in range(rows // BLK):
-                    most[part] = ordered(part, range(EARLY))
+                early_output()
 
         return unit
 
@@ -776,7 +774,10 @@
     idle = (jnp.int32(IDLE[0]), jnp.int32(GUEST), jnp.int32(0))
     lax.fori_loop(0, by_role([-(-length // PACK) for length in lengths]), some_steps, idle)
 
-    drain()
+    for index in range(1, n):
+        @pl.when(z == index)
+        def _():
+            drain(index)
 
     @pl.when(z == 0)
     def _():
@@ -786,6 +787,8 @@
         unit = (end - 1, last, end - 1)
         ahead(unit, scores_a, top_a)
         behind(unit, scores_a, top_a)
+        early_output()
+        drain(0)
         end_sib(1 - s).wait_recv()
         unit = (end, last, end)
         ahead(unit, scores_b, top_b)

time: 25.4 us -> 25.2 us (level)
  no operation moved by 1% of the time
where the time goes in v11:
time: 25.2 us; the launch traced here: 25.1 us
  Pallas kernels  25.1 us (100%)
    pallas_call x1, Pallas kernels, chain_call(): pl.pallas_call(functools.partial(chain, n), out_shape=pltpu.VMEM((heads *...  24.3 us
    pallas_call x1, Pallas kernels, chain_call(): pl.pallas_call(store, out_shape=jax.ShapeDtypeStruct(out.shape, out.dtype...  0.82 us

profile of v11, /device:TPU:0, one launch (start us, length us, event | category | flops | bytes accessed | tf_op | source)
XLA Modules:
  0.0 25.1 jit_solution(7745655270116342281)
XLA Ops:
  0.0 24.3 %shard_map.91.o_vmem = bf16[2048,128]{1,0:T(8,128)(2,1)S(1)} custom-call(bf16[2048,128]{1,0:T(8,128)(2,1)} %bitcast.8, bf16[512,128]{1,0:T(8,128)(2,1)} %bitcast.9, bf16[512,128]{1,0:T(8,128)(2,1)} %bitcast.10, bf16[16,512,128]{2,1,0:T(8,128)(2,1)} %bitcast.6, bf16[16,512,128]{2,1,0:T(8,128)(2,1)} %bitcast.7, s32[2]{0:T(128)} %vp_hbm.1, s32[1,6]{1,0:T(1,128)} %vl_hbm.1, ...), custom_call_target="tpu_custom_call" | custom-call | tf_op jit(solution)/shard_map/pallas_call | solution.py:851
  24.3 0.8 %shard_map.92 = bf16[2048,128]{1,0:T(8,128)(2,1)} custom-call(bf16[2048,128]{1,0:T(8,128)(2,1)S(1)} %shard_map.91.o_vmem), custom_call_target="tpu_custom_call" | custom-call | tf_op jit(solution)/shard_map/pallas_call | solution.py:872

commit v12 on v11

--- a/solution.py
+++ b/solution.py
@@ -783,11 +783,11 @@
     def _():
         end_hop(0).wait_recv()
         end_sib(s).start()
+        early_output()
         sib(last, end - 1, 1 - s).wait_recv()
         unit = (end - 1, last, end - 1)
         ahead(unit, scores_a, top_a)
         behind(unit, scores_a, top_a)
-        early_output()
         drain(0)
         end_sib(1 - s).wait_recv()
         unit = (end, last, end)

time: 25.2 us -> 25.1 us (level)
  no operation moved by 1% of the time
where the time goes in v12:
time: 25.1 us; the launch traced here: 25 us
  Pallas kernels  25 us (100%)
    pallas_call x1, Pallas kernels, chain_call(): pl.pallas_call(functools.partial(chain, n), out_shape=pltpu.VMEM((heads *...  24.2 us
    pallas_call x1, Pallas kernels, chain_call(): pl.pallas_call(store, out_shape=jax.ShapeDtypeStruct(out.shape, out.dtype...  0.82 us

profile of v12, /device:TPU:0, one launch (start us, length us, event | category | flops | bytes accessed | tf_op | source)
XLA Modules:
  0.0 25.0 jit_solution(11176078727229859920)
XLA Ops:
  0.0 24.2 %shard_map.91.o_vmem = bf16[2048,128]{1,0:T(8,128)(2,1)S(1)} custom-call(bf16[2048,128]{1,0:T(8,128)(2,1)} %bitcast.8, bf16[512,128]{1,0:T(8,128)(2,1)} %bitcast.9, bf16[512,128]{1,0:T(8,128)(2,1)} %bitcast.10, bf16[16,512,128]{2,1,0:T(8,128)(2,1)} %bitcast.6, bf16[16,512,128]{2,1,0:T(8,128)(2,1)} %bitcast.7, s32[2]{0:T(128)} %vp_hbm.1, s32[1,6]{1,0:T(1,128)} %vl_hbm.1, ...), custom_call_target="tpu_custom_call" | custom-call | tf_op jit(solution)/shard_map/pallas_call | solution.py:851
  24.2 0.8 %shard_map.92 = bf16[2048,128]{1,0:T(8,128)(2,1)} custom-call(bf16[2048,128]{1,0:T(8,128)(2,1)S(1)} %shard_map.91.o_vmem), custom_call_target="tpu_custom_call" | custom-call | tf_op jit(solution)/shard_map/pallas_call | solution.py:872

commit v13 on v12

--- a/solution.py
+++ b/solution.py
@@ -577,13 +577,13 @@
 
     key_id = lax.broadcasted_iota(jnp.int32, (BLK, rows), 0)
     row_id = lax.broadcasted_iota(jnp.int32, (BLK, rows), 1) // groups
-    later = jnp.where(key_id > row_id, -1e30, 0.0).astype(jnp.bfloat16)
+    later = jnp.where(key_id > row_id, -3e38, 0.0).astype(jnp.bfloat16)
     slots = acc.shape[0]
     for slot in range(slots):
         q_ref[slot, head_dim:] = later if slot < heads else jnp.zeros_like(later)
         acc[slot] = jnp.zeros_like(acc[slot])
         total[slot] = jnp.zeros_like(total[slot])
-        peak[slot] = jnp.full_like(peak[slot], -1e30)
+        peak[slot] = jnp.full_like(peak[slot], jnp.finfo(jnp.float32).min)
     q_ref[slots - 1, 0:head_dim] = jnp.zeros_like(later)
     one_at = lax.broadcasted_iota(jnp.int32, (BLK, BLK), 0) == lax.broadcasted_iota(jnp.int32, (BLK, BLK), 1)
     ext[0] = jnp.zeros((BLK, BLK), jnp.bfloat16)

time: 25.1 us -> 25.1 us (level)
  no operation moved by 1% of the time
where the time goes in v13:
time: 25.1 us; the launch traced here: 25 us
  Pallas kernels  25 us (100%)
    pallas_call x1, Pallas kernels, chain_call(): pl.pallas_call(functools.partial(chain, n), out_shape=pltpu.VMEM((heads *...  24.2 us
    pallas_call x1, Pallas kernels, chain_call(): pl.pallas_call(store, out_shape=jax.ShapeDtypeStruct(out.shape, out.dtype...  0.82 us

profile of v13, /device:TPU:0, one launch (start us, length us, event | category | flops | bytes accessed | tf_op | source)
XLA Modules:
  0.0 25.0 jit_solution(16364341524117321292)
XLA Ops:
  0.0 24.2 %shard_map.91.o_vmem = bf16[2048,128]{1,0:T(8,128)(2,1)S(1)} custom-call(bf16[2048,128]{1,0:T(8,128)(2,1)} %bitcast.8, bf16[512,128]{1,0:T(8,128)(2,1)} %bitcast.9, bf16[512,128]{1,0:T(8,128)(2,1)} %bitcast.10, bf16[16,512,128]{2,1,0:T(8,128)(2,1)} %bitcast.6, bf16[16,512,128]{2,1,0:T(8,128)(2,1)} %bitcast.7, s32[2]{0:T(128)} %vp_hbm.1, s32[1,6]{1,0:T(1,128)} %vl_hbm.1, ...), custom_call_target="tpu_custom_call" | custom-call | tf_op jit(solution)/shard_map/pallas_call | solution.py:851
  24.2 0.8 %shard_map.92 = bf16[2048,128]{1,0:T(8,128)(2,1)} custom-call(bf16[2048,128]{1,0:T(8,128)(2,1)S(1)} %shard_map.91.o_vmem), custom_call_target="tpu_custom_call" | custom-call | tf_op jit(solution)/shard_map/pallas_call | solution.py:872

commit v14 on v13

--- a/solution.py
+++ b/solution.py
@@ -348,7 +348,10 @@
         [(ck_hbm, ck_raw), (cv_hbm, cv_raw), (nk_hbm, nk_raw), (nv_hbm, nv_raw), (q_hbm, q_raw)])]
     tables = [pltpu.make_async_copy(src, dst, in_sem.at[2 + i]) for i, (src, dst) in enumerate(
         [(vp_hbm, vp_ref), (vl_hbm, vl_ref), (sl_hbm, sl_ref), (cnt_hbm, cnt_ref)])]
-    loads[0].start()
+    half = ck_raw.shape[0] // 2
+    for i in range(2):
+        lines = pl.ds(i * half, half)
+        pltpu.make_async_copy(ck_hbm.at[lines], ck_raw.at[lines], in_sem.at[0]).start()
     loads[1].start()
     for table in tables:
         table.start()

time: 25.1 us -> 25.1 us (level)
  no operation moved by 1% of the time
where the time goes in v14:
time: 25.1 us; the launch traced here: 25 us
  Pallas kernels  25 us (100%)
    pallas_call x1, Pallas kernels, chain_call(): pl.pallas_call(functools.partial(chain, n), out_shape=pltpu.VMEM((heads *...  24.1 us
    pallas_call x1, Pallas kernels, chain_call(): pl.pallas_call(store, out_shape=jax.ShapeDtypeStruct(out.shape, out.dtype...  0.82 us

profile of v14, /device:TPU:0, one launch (start us, length us, event | category | flops | bytes accessed | tf_op | source)
XLA Modules:
  0.0 25.0 jit_solution(7472874909902429943)
XLA Ops:
  0.0 24.1 %shard_map.91.o_vmem = bf16[2048,128]{1,0:T(8,128)(2,1)S(1)} custom-call(bf16[2048,128]{1,0:T(8,128)(2,1)} %bitcast.8, bf16[512,128]{1,0:T(8,128)(2,1)} %bitcast.9, bf16[512,128]{1,0:T(8,128)(2,1)} %bitcast.10, bf16[16,512,128]{2,1,0:T(8,128)(2,1)} %bitcast.6, bf16[16,512,128]{2,1,0:T(8,128)(2,1)} %bitcast.7, s32[2]{0:T(128)} %vp_hbm.1, s32[1,6]{1,0:T(1,128)} %vl_hbm.1, ...), custom_call_target="tpu_custom_call" | custom-call | tf_op jit(solution)/shard_map/pallas_call | solution.py:854
  24.2 0.8 %shard_map.92 = bf16[2048,128]{1,0:T(8,128)(2,1)} custom-call(bf16[2048,128]{1,0:T(8,128)(2,1)S(1)} %shard_map.91.o_vmem), custom_call_target="tpu_custom_call" | custom-call | tf_op jit(solution)/shard_map/pallas_call | solution.py:875
